TPU v7x, 32 devices: a whole 2x2x4 slice. The times are simulated.
32 devices in a mesh: dp: 4 (over y, x), seq: 8 (over z, core).
Axes of the slice: x: 2, y: 2, z: 4, core: 2. Of those that a mesh axis runs over, the one named last changes fastest.
Arguments:
- tokens: bfloat16 [4, 1024, 2048], P('dp', 'seq'), may hold values from -6 to 6
- qkv_weight: bfloat16 [2048, 3072], P(('dp', 'seq')), may hold values from -0.125 to 0.125
- out_weight: bfloat16 [2048, 2048], P(('dp', 'seq')), may hold values from -1 to 1
- gate_weight: bfloat16 [8192, 2048], P(('dp', 'seq')), may hold values from -0.125 to 0.125
- up_weight: bfloat16 [8192, 2048], P(('dp', 'seq')), may hold values from -0.125 to 0.125
- down_weight: bfloat16 [8192, 2048], P(('dp', 'seq')), may hold values from -0.0625 to 0.0625
- attn_gain: bfloat16 [2048], P(('dp', 'seq')), may hold values from 0.5 to 1.5
- mlp_gain: bfloat16 [2048], P(('dp', 'seq')), may hold values from 0.5 to 1.5
- cotangent: bfloat16 [4, 1024, 2048], P('dp', 'seq'), may hold values from -6 to 6
Outputs:
- block_out: bfloat16 [4, 1024, 2048], P('dp', 'seq')
- grad_tokens: float32 [4, 1024, 2048], P('dp', 'seq')
- grad_qkv: float32 [2048, 3072], P(('dp', 'seq'))
- grad_out: float32 [2048, 2048], P(('dp', 'seq'))
- grad_gate: float32 [8192, 2048], P(('dp', 'seq'))
- grad_up: float32 [8192, 2048], P(('dp', 'seq'))
- grad_down: float32 [8192, 2048], P(('dp', 'seq'))
- grad_attn_gain: float32 [2048], P(('dp', 'seq'))
- grad_mlp_gain: float32 [2048], P(('dp', 'seq'))
All inputs are finite; a program needn't handle non-finite values.
Results may differ from a plain program's by a relative error of at most 0.017.
Values may be sent and summed in bfloat16 or wider, within the bound.
A program may use at most 192 MiB of HBM per device.

v0:
```python
import jax
import jax.numpy as jnp
from jax import lax
from jax.sharding import PartitionSpec as P

HEADS = 32
KV_HEADS = 8
HEAD_DIM = 64


epsilon = 1e-05
rope_base = 500000.0
masked_value = -1e30
contract_rows = (((0,), (0,)), ((), ()))
contract_cols = (((1,), (1,)), ((), ()))


def norm_factor(values):
    return lax.rsqrt(jnp.mean(values * values, axis=-1, keepdims=True) + epsilon)


def norm_grad(values, factor, gain, gradient):
    weighted = gradient * gain
    inner_mean = jnp.mean(weighted * values, axis=-1, keepdims=True)
    return factor * weighted - values * (factor * factor * factor) * inner_mean


def rope_tables(positions, head_width):
    half_width = head_width // 2
    frequency = rope_base ** (-2.0 * jnp.arange(half_width, dtype=jnp.float32) / head_width)
    angles = positions.astype(jnp.float32)[:, None] * frequency[None, :]
    return (jnp.cos(angles)[:, None, :], jnp.sin(angles)[:, None, :])


def rotate(values, cosine_table, sine_table):
    half_width = values.shape[-1] // 2
    first_half = values[..., :half_width]
    second_half = values[..., half_width:]
    return jnp.concatenate(
        [
            first_half * cosine_table - second_half * sine_table,
            second_half * cosine_table + first_half * sine_table,
        ],
        axis=-1,
    )


def gated_grad(gate, upward, grad_inner):
    sigmoid_gate = jax.nn.sigmoid(gate)
    grad_gate = grad_inner * upward * sigmoid_gate * (1.0 + gate * (1.0 - sigmoid_gate))
    grad_upward = grad_inner * (gate * sigmoid_gate)
    return (grad_gate.astype(jnp.bfloat16), grad_upward.astype(jnp.bfloat16))


def block_scores(query_block, key_heads, lower, upper, score_scale):
    scores = (
        jnp.einsum(
            "qhd,kd->hqk", query_block, key_heads[:upper], preferred_element_type=jnp.float32
        )
        * score_scale
    )
    rows_at = lower + jnp.arange(query_block.shape[0], dtype=jnp.int32)
    cols_at = jnp.arange(upper, dtype=jnp.int32)
    allowed = (cols_at[None, :] <= rows_at[:, None])[None]
    return jnp.where(allowed, scores, masked_value)


def feed_split(normed_two, gate_weight, up_weight, down_weight, grad_low):
    gate_part, up_part, down_part = (
        lax.all_gather(gate_weight, "dp", axis=0, tiled=True),
        lax.all_gather(up_weight, "dp", axis=0, tiled=True),
        lax.all_gather(down_weight, "dp", axis=0, tiled=True),
    )
    normed_all = lax.all_gather(normed_two, "seq", axis=0, tiled=True)
    gate = lax.dot_general(normed_all, gate_part, contract_cols, preferred_element_type=jnp.float32)
    upward = lax.dot_general(normed_all, up_part, contract_cols, preferred_element_type=jnp.float32)
    inner = (jax.nn.silu(gate) * upward).astype(jnp.bfloat16)
    result = lax.psum_scatter(
        jnp.dot(inner, down_part, preferred_element_type=jnp.float32).astype(jnp.bfloat16),
        "seq",
        scatter_dimension=0,
        tiled=True,
    ).astype(jnp.float32)
    grad_all = lax.all_gather(grad_low, "seq", axis=0, tiled=True)
    grad_inner = lax.dot_general(
        grad_all, down_part, contract_cols, preferred_element_type=jnp.float32
    )
    grad_gate, grad_upward = gated_grad(gate, upward, grad_inner)
    grad_normed = lax.psum_scatter(
        (
            jnp.dot(grad_gate, gate_part, preferred_element_type=jnp.float32)
            + jnp.dot(grad_upward, up_part, preferred_element_type=jnp.float32)
        ).astype(jnp.bfloat16),
        "seq",
        scatter_dimension=0,
        tiled=True,
    ).astype(jnp.float32)
    owned = (
        lax.psum_scatter(
            lax.dot_general(
                grad_gate, normed_all, contract_rows, preferred_element_type=jnp.float32
            ).astype(jnp.bfloat16),
            "dp",
            scatter_dimension=0,
            tiled=True,
        ).astype(jnp.float32),
        lax.psum_scatter(
            lax.dot_general(
                grad_upward, normed_all, contract_rows, preferred_element_type=jnp.float32
            ).astype(jnp.bfloat16),
            "dp",
            scatter_dimension=0,
            tiled=True,
        ).astype(jnp.float32),
        lax.psum_scatter(
            lax.dot_general(
                inner, grad_all, contract_rows, preferred_element_type=jnp.float32
            ).astype(jnp.bfloat16),
            "dp",
            scatter_dimension=0,
            tiled=True,
        ).astype(jnp.float32),
    )
    return (result, grad_normed, owned)


def per_device(
    tokens,
    qkv_weight,
    out_weight,
    gate_weight,
    up_weight,
    down_weight,
    attn_gain,
    mlp_gain,
    cotangent,
):
    groups = lax.axis_size("seq")
    tok_rows = tokens.shape[1]
    model_width = tokens.shape[2]
    seq_len = tok_rows * groups
    local_heads = HEADS // groups
    local_width = local_heads * HEAD_DIM
    kv_width = KV_HEADS * HEAD_DIM
    kv_copies = groups // KV_HEADS
    score_scale = HEAD_DIM ** (-0.5)
    block_rows = min(512, seq_len)
    block_count = seq_len // block_rows
    qkv_full, out_full, gain_one, gain_two = (
        lax.all_gather(qkv_weight, ("dp", "seq"), axis=0, tiled=True),
        lax.all_gather(out_weight, ("dp", "seq"), axis=0, tiled=True),
        lax.all_gather(attn_gain, ("dp", "seq"), axis=0, tiled=True),
        lax.all_gather(mlp_gain, ("dp", "seq"), axis=0, tiled=True),
    )
    gain_one = gain_one.astype(jnp.float32)
    gain_two = gain_two.astype(jnp.float32)
    x_rows = tokens[0].astype(jnp.float32)
    factor_one = norm_factor(x_rows)
    normed = (x_rows * factor_one * gain_one).astype(jnp.bfloat16)
    mixed = jnp.dot(normed, qkv_full, preferred_element_type=jnp.float32)
    positions = lax.axis_index("seq") * tok_rows + jnp.arange(tok_rows, dtype=jnp.int32)
    cosine_table, sine_table = rope_tables(positions, HEAD_DIM)
    queries = rotate(
        mixed[:, :model_width].reshape(tok_rows, HEADS, HEAD_DIM), cosine_table, sine_table
    ).astype(jnp.bfloat16)
    keys = rotate(
        mixed[:, model_width : model_width + kv_width].reshape(tok_rows, KV_HEADS, HEAD_DIM),
        cosine_table,
        sine_table,
    ).astype(jnp.bfloat16)
    values = (
        mixed[:, model_width + kv_width :]
        .reshape(tok_rows, KV_HEADS, HEAD_DIM)
        .astype(jnp.bfloat16)
    )
    key_value = jnp.repeat(jnp.concatenate([keys, values], axis=-1), kv_copies, axis=1)
    query_send = queries.reshape(1, tok_rows, groups, local_width)
    query_heads, pair_heads = (
        lax.all_to_all(query_send, "seq", split_axis=2, concat_axis=1, tiled=True),
        lax.all_to_all(key_value[None], "seq", split_axis=2, concat_axis=1, tiled=True),
    )
    query_heads = query_heads.reshape(seq_len, local_heads, HEAD_DIM)
    key_heads = pair_heads[0, :, 0, :HEAD_DIM]
    value_heads = pair_heads[0, :, 0, HEAD_DIM:]
    outputs = []
    log_sums = []
    for block in range(block_count):
        lower = block * block_rows
        upper = lower + block_rows
        scores = block_scores(query_heads[lower:upper], key_heads, lower, upper, score_scale)
        highest = jnp.max(scores, axis=-1, keepdims=True)
        log_sum = highest + jnp.log(jnp.sum(jnp.exp(scores - highest), axis=-1, keepdims=True))
        probs = jnp.exp(scores - log_sum).astype(jnp.bfloat16)
        attended = jnp.einsum(
            "hqk,kd->qhd", probs, value_heads[:upper], preferred_element_type=jnp.float32
        )
        outputs.append(attended.astype(jnp.bfloat16))
        log_sums.append(log_sum)
    attended_all = jnp.concatenate(outputs, axis=0).reshape(1, seq_len, 1, local_width)
    attended_rows = lax.all_to_all(
        attended_all, "seq", split_axis=1, concat_axis=2, tiled=True
    ).reshape(tok_rows, model_width)
    hidden = x_rows + jnp.dot(attended_rows, out_full, preferred_element_type=jnp.float32)
    factor_two = norm_factor(hidden)
    normed_two = (hidden * factor_two * gain_two).astype(jnp.bfloat16)
    grad_low = cotangent[0]
    grad_output = grad_low.astype(jnp.float32)
    mlp_result, grad_normed, mlp_grads = feed_split(
        normed_two, gate_weight, up_weight, down_weight, grad_low
    )
    block_out = (hidden + mlp_result).astype(jnp.bfloat16)[None]
    gain_two_term = jnp.sum(grad_normed * hidden * factor_two, axis=0)
    grad_hidden = grad_output + norm_grad(hidden, factor_two, gain_two, grad_normed)
    grad_branch = grad_hidden.astype(jnp.bfloat16)
    out_term = lax.dot_general(
        attended_rows, grad_branch, contract_rows, preferred_element_type=jnp.float32
    )
    grad_attended = lax.dot_general(
        grad_branch, out_full, contract_cols, preferred_element_type=jnp.float32
    ).astype(jnp.bfloat16)
    grad_send = grad_attended.reshape(1, tok_rows, groups, local_width)
    grad_heads = lax.all_to_all(grad_send, "seq", split_axis=2, concat_axis=1, tiled=True).reshape(
        seq_len, local_heads, HEAD_DIM
    )
    grad_keys = jnp.zeros((seq_len, HEAD_DIM), jnp.float32)
    grad_values = jnp.zeros((seq_len, HEAD_DIM), jnp.float32)
    grad_queries = []
    for block in range(block_count):
        lower = block * block_rows
        upper = lower + block_rows
        query_block = query_heads[lower:upper]
        grad_block = grad_heads[lower:upper]
        scores = block_scores(query_block, key_heads, lower, upper, score_scale)
        probs = jnp.exp(scores - log_sums[block])
        probs_low = probs.astype(jnp.bfloat16)
        grad_probs = jnp.einsum(
            "qhd,kd->hqk", grad_block, value_heads[:upper], preferred_element_type=jnp.float32
        )
        row_delta = jnp.sum(probs * grad_probs, axis=-1, keepdims=True)
        grad_scores = (probs * (grad_probs - row_delta)).astype(jnp.bfloat16)
        grad_queries.append(
            jnp.einsum(
                "hqk,kd->qhd", grad_scores, key_heads[:upper], preferred_element_type=jnp.float32
            )
            * score_scale
        )
        grad_keys = grad_keys.at[:upper].add(
            jnp.einsum("hqk,qhd->kd", grad_scores, query_block, preferred_element_type=jnp.float32)
            * score_scale
        )
        grad_values = grad_values.at[:upper].add(
            jnp.einsum("hqk,qhd->kd", probs_low, grad_block, preferred_element_type=jnp.float32)
        )
    query_back = jnp.concatenate(grad_queries, axis=0).reshape(1, seq_len, 1, local_width)
    pair_back = jnp.concatenate([grad_keys, grad_values], axis=-1).reshape(
        1, seq_len, 1, 2 * HEAD_DIM
    )
    query_rows, pair_rows = (
        lax.all_to_all(
            query_back.astype(jnp.bfloat16), "seq", split_axis=1, concat_axis=2, tiled=True
        ).astype(query_back.dtype),
        lax.all_to_all(
            pair_back.astype(jnp.bfloat16), "seq", split_axis=1, concat_axis=2, tiled=True
        ).astype(pair_back.dtype),
    )
    query_rows = query_rows.reshape(tok_rows, HEADS, HEAD_DIM)
    pair_rows = jnp.sum(pair_rows.reshape(tok_rows, KV_HEADS, kv_copies, 2 * HEAD_DIM), axis=2)
    grad_q = rotate(query_rows, cosine_table, -sine_table).reshape(tok_rows, model_width)
    grad_k = rotate(pair_rows[..., :HEAD_DIM], cosine_table, -sine_table).reshape(
        tok_rows, kv_width
    )
    grad_v = pair_rows[..., HEAD_DIM:].reshape(tok_rows, kv_width)
    grad_mixed = jnp.concatenate([grad_q, grad_k, grad_v], axis=1).astype(jnp.bfloat16)
    qkv_term = lax.dot_general(
        normed, grad_mixed, contract_rows, preferred_element_type=jnp.float32
    )
    grad_normed_one = lax.dot_general(
        grad_mixed, qkv_full, contract_cols, preferred_element_type=jnp.float32
    )
    gain_one_term = jnp.sum(grad_normed_one * x_rows * factor_one, axis=0)
    grad_input = grad_hidden + norm_grad(x_rows, factor_one, gain_one, grad_normed_one)
    attn_owned = (
        lax.psum_scatter(qkv_term, ("dp", "seq"), scatter_dimension=0, tiled=True),
        lax.psum_scatter(out_term, ("dp", "seq"), scatter_dimension=0, tiled=True),
        lax.psum_scatter(gain_one_term, ("dp", "seq"), scatter_dimension=0, tiled=True),
        lax.psum_scatter(gain_two_term, ("dp", "seq"), scatter_dimension=0, tiled=True),
    )
    return (
        block_out,
        grad_input[None],
        attn_owned[0],
        attn_owned[1],
        mlp_grads[0],
        mlp_grads[1],
        mlp_grads[2],
        attn_owned[2],
        attn_owned[3],
    )


def solution(mesh):
    in_specs = (
        P("dp", "seq", None),
        P(("dp", "seq"), None),
        P(("dp", "seq"), None),
        P(("dp", "seq"), None),
        P(("dp", "seq"), None),
        P(("dp", "seq"), None),
        P(("dp", "seq")),
        P(("dp", "seq")),
        P("dp", "seq", None),
    )
    out_specs = (
        P("dp", "seq", None),
        P("dp", "seq", None),
        P(("dp", "seq"), None),
        P(("dp", "seq"), None),
        P(("dp", "seq"), None),
        P(("dp", "seq"), None),
        P(("dp", "seq"), None),
        P(("dp", "seq")),
        P(("dp", "seq")),
    )
    return jax.shard_map(
        per_device, mesh=mesh, in_specs=in_specs, out_specs=out_specs, check_vma=False
    )
```

profile of v0, /device:TPU:0, one launch (start us, length us, event | category | flops | bytes accessed | tf_op | source)
XLA Modules:
  0.0 1199.9 jit_solution(6816701573668174001)
XLA Ops:
  10.4 43.2 %all-reduce.7 = (bf16[2048]{0:T(1024)(128)(2,1)S(1)}, bf16[2048]{0:T(1024)(128)(2,1)S(1)}) all-reduce(bf16[2048]{0:T(1024)(128)(2,1)S(1)} %dynamic-update-slice.10, bf16[2048]{0:T(1024)(128)(2,1)S(1)} %dynamic-update-slice.11), channel_id=1, replica_groups=mesh['dp'=4,'seq'=8] {'dp','seq'}, use_global_device_ids=true, to_apply=%add.2 | all-reduce | flops 4096 | bytes 16384
  56.2 53.6 %all-gather.9.cloned.1.call-done = bf16[2048,3072]{1,0:T(8,128)(2,1)} async-done(((bf16[64,3072]{1,0:T(8,128)(2,1)}), bf16[2048,3072]{1,0:T(8,128)(2,1)}) %all-gather.9.cloned.1.call-update) | async-done | bytes 12582928 | tf_op jit(solution)/shard_map/all_gather | solution.py:150
  109.9 6.7 fusion.56
  117.6 3.4 all-to-all-start
  122.5 12.6 %all-to-all-done = bf16[1,128,8,128]{1,3,0,2:T(8,128)(2,1)S(1)} async-done(((bf16[1,128,8,128]{1,3,0,2:T(8,128)(2,1)}), bf16[1,128,8,128]{1,3,0,2:T(8,128)(2,1)S(1)}, u32[]{:S(2)}, u32[]{:S(2)}) %all-to-all-start) | async-done | bytes 262176 | tf_op jit(solution)/shard_map/all_to_all | solution.py:180
  135.1 3.5 all-to-all-start.1
  140.9 23.8 %all-to-all-done.1 = bf16[1,128,8,256]{1,3,0,2:T(8,128)(2,1)S(1)} async-done(((bf16[1,128,8,256]{1,3,0,2:T(8,128)(2,1)}), bf16[1,128,8,256]{1,3,0,2:T(8,128)(2,1)S(1)}, u32[]{:S(2)}, u32[]{:S(2)}) %all-to-all-start.1) | async-done | bytes 524320 | tf_op jit(solution)/shard_map/all_to_all | solution.py:179
  176.6 3.8 reduce.10
  181.3 3.5 all-to-all-start.2
  184.9 22.9 %all-to-all-done.2 = bf16[8,2,16384]{2,1,0:T(2,128)(2,1)S(1)} async-done(((bf16[8,2,16384]{2,1,0:T(2,128)(2,1)}), bf16[8,2,16384]{2,1,0:T(2,128)(2,1)S(1)}, u32[]{:S(2)}, u32[]{:S(2)}) %all-to-all-start.2) | async-done | bytes 524320 | tf_op jit(solution)/shard_map/all_to_all | solution.py:200
  209.1 4.7 multiply_reduce_fusion
  216.9 44.1 %all-gather.15.cloned.1.call-done = bf16[1024,2048]{1,0:T(8,128)(2,1)} async-done(((bf16[256,2048]{1,0:T(8,128)(2,1)}), bf16[1024,2048]{1,0:T(8,128)(2,1)}) %all-gather.15.cloned.1.call-update) | async-done | bytes 4194320 | tf_op jit(solution)/shard_map/all_gather | solution.py:70
  261.0 48.9 %all-gather.13.cloned.1.call-done = bf16[1024,2048]{1,0:T(8,128)(2,1)} async-done(((bf16[128,2048]{1,0:T(8,128)(2,1)}), bf16[1024,2048]{1,0:T(8,128)(2,1)}) %all-gather.13.cloned.1.call-update) | async-done | bytes 4194320 | tf_op jit(solution)/shard_map/all_gather | solution.py:74
  309.9 10.0 fusion.71
  319.9 43.1 %all-gather.17.cloned.1.call-done = bf16[1024,2048]{1,0:T(8,128)(2,1)} async-done(((bf16[256,2048]{1,0:T(8,128)(2,1)}), bf16[1024,2048]{1,0:T(8,128)(2,1)}) %all-gather.17.cloned.1.call-update) | async-done | bytes 4194320 | tf_op jit(solution)/shard_map/all_gather | solution.py:71
  363.0 10.0 fusion.72
  373.0 44.3 %all-gather.19.cloned.1.call-done = bf16[1024,2048]{1,0:T(8,128)(2,1)} async-done(((bf16[256,2048]{1,0:T(8,128)(2,1)}), bf16[1024,2048]{1,0:T(8,128)(2,1)}) %all-gather.19.cloned.1.call-update) | async-done | bytes 4194320 | tf_op jit(solution)/shard_map/all_gather | solution.py:72
  417.3 48.5 %all-gather.21.cloned.1.call-done = bf16[1,1024,2048]{2,1,0:T(8,128)(2,1)} async-done(((bf16[1,128,2048]{2,1,0:T(8,128)(2,1)}), bf16[1,1024,2048]{2,1,0:T(8,128)(2,1)}) %all-gather.21.cloned.1.call-update) | async-done | bytes 4194320 | tf_op jit(solution)/shard_map/all_gather | solution.py:84
  465.8 13.3 %multiply_convert_fusion = (bf16[1024,1024]{1,0:T(8,128)(2,1)S(1)}, bf16[1024,1024]{1,0:T(8,128)(2,1)S(1)}, bf16[1024,1024]{1,0:T(8,128)(2,1)}) fusion(f32[1024,1024]{1,0:T(8,128)} %fusion.71, f32[1024,1024]{1,0:T(8,128)} %fusion.72, bf16[1024,2048]{1,0:T(8,128)(2,1)} %all-gather.19.cloned.1.call-done, bf16[1,1024,2048]{2,1,0:T(8,128)(2,1)} %all-gather.21.cloned.1.call-done), kind=kOutput, calls=%fused_computation.21 | convolution fusion | flops 4310695936 | bytes 23068672 | tf_op jit(solution)/shard_map/dot_general | solution.py:85
  479.2 4.9 fusion.73
  484.2 6.2 add_convert_fusion
  490.4 9.4 convolution_convert_fusion.2
  499.8 9.5 convolution_convert_fusion.1
  509.5 9.4 convolution_convert_fusion
  519.0 9.5 fusion.13
  528.6 10.7 reduce-scatter.10.cloned.1.call-done
  540.6 49.3 %reduce-scatter.8.cloned.1.call-done = bf16[128,2048]{1,0:T(8,128)(2,1)} async-done(((bf16[1024,2048]{1,0:T(8,128)(2,1)}), bf16[128,2048]{1,0:T(8,128)(2,1)}) %reduce-scatter.8.cloned.1.call-update) | async-done | bytes 524304 | tf_op jit(solution)/shard_map/reduce_scatter | solution.py:78
  592.4 10.0 fusion.52
  602.4 6.5 convolution_convert_fusion.3
  609.2 17.9 %all_to_all.81 = bf16[1,128,8,256]{3,1,0,2:T(8,128)(2,1)S(1)} all-to-all(bf16[1,128,8,256]{3,1,0,2:T(8,128)(2,1)S(1)} %copy.107), channel_id=1, replica_groups=mesh['dp'=4,'seq'=8] {'seq'}, dimensions={2} | all-to-all | bytes 1048576 | tf_op jit(solution)/shard_map/all_to_all | solution.py:222
  628.5 4.3 fusion.5
  635.3 2.8 fusion
  648.2 2.9 reduce.11
  652.8 3.4 all-to-all-start.5
  656.8 3.0 fusion.22
  660.7 3.8 reduce.12
  665.9 4.6 all-to-all-start.4
  671.4 14.4 %all-to-all-done.4 = bf16[8,2,16384]{2,1,0:T(2,128)(2,1)S(1)} async-done(((bf16[8,2,16384]{2,1,0:T(2,128)(2,1)}), bf16[8,2,16384]{2,1,0:T(2,128)(2,1)S(1)}, u32[]{:S(2)}, u32[]{:S(2)}) %all-to-all-start.4) | async-done | bytes 524320 | tf_op jit(solution)/shard_map/all_to_all | solution.py:259
  687.2 11.0 fusion.50
  698.3 2.8 convert_element_type.208
  701.1 2.8 convert_element_type.210
  703.8 51.1 %reduce-scatter.20.cloned.1.call-done = bf16[256,2048]{1,0:T(8,128)(2,1)} async-done(((bf16[1024,2048]{1,0:T(8,128)(2,1)}), bf16[256,2048]{1,0:T(8,128)(2,1)}) %reduce-scatter.20.cloned.1.call-update) | async-done | bytes 1048592 | tf_op jit(solution)/shard_map/reduce_scatter | solution.py:115
  754.9 2.8 convert_element_type.212
  757.7 10.0 fusion.48
  767.7 41.3 %all-reduce.6 = (f32[2048]{0:T(1024)S(1)}, f32[2048]{0:T(1024)S(1)}) all-reduce(f32[2048]{0:T(1024)S(1)} %get-tuple-element.75, f32[2048]{0:T(1024)S(1)} %get-tuple-element.73), channel_id=10, replica_groups=mesh['dp'=4,'seq'=8] {'dp','seq'}, use_global_device_ids=true, to_apply=%region_18.19.clone | all-reduce | flops 4096 | bytes 32768
  810.2 2.7 fusion.45
  812.9 132.6 %reduce-scatter.14.cloned.1.call-done = f32[64,2048]{1,0:T(8,128)} async-done(((f32[2048,2048]{1,0:T(8,128)}), f32[64,2048]{1,0:T(8,128)}) %reduce-scatter.14.cloned.1.call-update) | async-done | bytes 524304 | tf_op jit(solution)/shard_map/reduce_scatter | solution.py:284
  945.5 247.7 %reduce-scatter.12.cloned.1.call-done = f32[64,3072]{1,0:T(8,128)} async-done(((f32[2048,3072]{1,0:T(8,128)}), f32[64,3072]{1,0:T(8,128)}) %reduce-scatter.12.cloned.1.call-update) | async-done | bytes 786448 | tf_op jit(solution)/shard_map/reduce_scatter | solution.py:283
  (185 shorter events, 53.6 us)
Async XLA Ops:
  7.2 102.7 %all-gather.9.cloned.1.call-start = ((), (), s32[]{:S(2)}) async-start(), calls=%async_computation.13 | async-start | bytes 12976128 | tf_op jit(solution)/shard_map/all_gather | solution.py:150
  7.9 201.1 %all-gather.11.cloned.1.call-start = ((), (), s32[]{:S(2)}) async-start(), calls=%async_computation.14 | async-start | bytes 8650752 | tf_op jit(solution)/shard_map/all_gather | solution.py:151
  53.6 56.3 %copy-start.19 = (f32[2048]{0:T(1024)}, f32[2048]{0:T(1024)S(1)}, u32[]{:S(2)}) copy-start(f32[2048]{0:T(1024)S(1)} %convert_element_type.172) | copy-start | bytes 24580
  55.5 54.4 %copy-start.24 = (f32[128]{0:T(128)}, f32[128]{0:T(128)S(1)}, u32[]{:S(2)}) copy-start(f32[128]{0:T(128)S(1)} %get-tuple-element.102) | copy-start | bytes 1540
  56.2 65.3 %copy-start.21 = (f32[128,32]{0,1:T(8,128)}, f32[128,32]{0,1:T(8,128)S(1)}, u32[]{:S(2)}) copy-start(f32[128,32]{0,1:T(8,128)S(1)} %get-tuple-element.100) | copy-start | bytes 49156
  117.6 17.5 %all-to-all-start = ((bf16[1,128,8,128]{1,3,0,2:T(8,128)(2,1)}), bf16[1,128,8,128]{1,3,0,2:T(8,128)(2,1)S(1)}, u32[]{:S(2)}, u32[]{:S(2)}) async-start(bf16[1,128,8,128]{1,3,0,2:T(8,128)(2,1)} %maximum_bitcast_fusion), calls=%async_computation | async-start | bytes 524288 | tf_op jit(solution)/shard_map/all_to_all | solution.py:180
  135.1 4.2 copy-start.18
  135.1 29.6 %all-to-all-start.1 = ((bf16[1,128,8,256]{1,3,0,2:T(8,128)(2,1)}), bf16[1,128,8,256]{1,3,0,2:T(8,128)(2,1)S(1)}, u32[]{:S(2)}, u32[]{:S(2)}) async-start(bf16[1,128,8,256]{1,3,0,2:T(8,128)(2,1)} %bitcast.14), calls=%async_computation.1 | async-start | bytes 1048576 | tf_op jit(solution)/shard_map/all_to_all | solution.py:179
  138.6 122.4 %all-gather.15.cloned.1.call-start = ((), (), s32[]{:S(2)}) async-start(), calls=%async_computation.16 | async-start | bytes 5242880 | tf_op jit(solution)/shard_map/all_gather | solution.py:70
  140.9 31.5 %copy-start.10 = (bf16[1,1024,1,128]{1,3,2,0:T(8,128)(2,1)}, bf16[1,1024,1,128]{1,3,2,0:T(8,128)(2,1)S(1)}, u32[]{:S(2)}) copy-start(bf16[1,1024,1,128]{1,3,2,0:T(8,128)(2,1)S(1)} %copy_bitcast_fusion) | copy-start | bytes 786436
  165.0 2.2 copy-start.8
  165.4 1.9 copy-start.14
  166.3 4.8 copy-start.1
  168.8 3.9 copy-start
  176.0 33.0 %copy-start.4 = (bf16[1,128,2048]{2,1,0:T(8,128)(2,1)S(1)}, bf16[1,128,2048]{2,1,0:T(8,128)(2,1)}, u32[]{:S(2)}) copy-start(bf16[1,128,2048]{2,1,0:T(8,128)(2,1)} %param.21) | copy-start | bytes 1572868
  181.3 26.4 %all-to-all-start.2 = ((bf16[8,2,16384]{2,1,0:T(2,128)(2,1)}), bf16[8,2,16384]{2,1,0:T(2,128)(2,1)S(1)}, u32[]{:S(2)}, u32[]{:S(2)}) async-start(bf16[8,2,16384]{2,1,0:T(2,128)(2,1)} %reshape.437), calls=%async_computation.2 | async-start | bytes 1048576 | tf_op jit(solution)/shard_map/all_to_all | solution.py:200
  184.8 125.1 %all-gather.13.cloned.1.call-start = ((), (), s32[]{:S(2)}) async-start(), calls=%async_computation.15 | async-start | bytes 4718592 | tf_op jit(solution)/shard_map/all_gather | solution.py:74
  208.6 5.2 copy-start.7
  214.8 148.2 %all-gather.17.cloned.1.call-start = ((), (), s32[]{:S(2)}) async-start(), calls=%async_computation.17 | async-start | bytes 5242880 | tf_op jit(solution)/shard_map/all_gather | solution.py:71
  215.4 202.0 %all-gather.19.cloned.1.call-start = ((), (), s32[]{:S(2)}) async-start(), calls=%async_computation.18 | async-start | bytes 5242880 | tf_op jit(solution)/shard_map/all_gather | solution.py:72
  216.0 249.9 %all-gather.21.cloned.1.call-start = ((), (), s32[]{:S(2)}) async-start(), calls=%async_computation.26 | async-start | bytes 4718592 | tf_op jit(solution)/shard_map/all_gather | solution.py:84
  216.7 322.5 %reduce-scatter.10.cloned.1.call-start = ((), (), s32[]{:S(2)}) async-start(), calls=%async_computation.20 | async-start | bytes 4718592 | tf_op jit(solution)/shard_map/reduce_scatter | solution.py:89
  465.8 13.3 %copy-start.27 = (bf16[1024,2048]{1,0:T(8,128)(2,1)S(1)}, bf16[1024,2048]{1,0:T(8,128)(2,1)}, u32[]{:S(2)}) copy-start(bf16[1024,2048]{1,0:T(8,128)(2,1)} %all-gather.15.cloned.1.call-done) | copy-start | bytes 12582916
  479.2 5.0 copy-start.30
  479.2 5.0 copy-start.29
  479.2 5.0 copy-start.28
  490.3 99.6 %reduce-scatter.8.cloned.1.call-start = ((), (), s32[]{:S(2)}) async-start(), calls=%async_computation.19 | async-start | bytes 4718592 | tf_op jit(solution)/shard_map/reduce_scatter | solution.py:78
  499.8 198.5 %reduce-scatter.16.cloned.1.call-start = ((), (), s32[]{:S(2)}) async-start(), calls=%async_computation.23 | async-start | bytes 5242880 | tf_op jit(solution)/shard_map/reduce_scatter | solution.py:99
  509.3 191.7 %reduce-scatter.18.cloned.1.call-start = ((), (), s32[]{:S(2)}) async-start(), calls=%async_computation.24 | async-start | bytes 5242880 | tf_op jit(solution)/shard_map/reduce_scatter | solution.py:107
  519.0 235.9 %reduce-scatter.20.cloned.1.call-start = ((), (), s32[]{:S(2)}) async-start(), calls=%async_computation.25 | async-start | bytes 5242880 | tf_op jit(solution)/shard_map/reduce_scatter | solution.py:115
  528.5 416.9 %reduce-scatter.14.cloned.1.call-start = ((), (), s32[]{:S(2)}) async-start(), calls=%async_computation.22 | async-start | bytes 17301504 | tf_op jit(solution)/shard_map/reduce_scatter | solution.py:284
  592.4 10.0 copy-start.5
  627.5 5.3 copy-start.16
  628.5 4.3 copy-start.2
  628.5 6.4 slice-start
  632.8 2.5 slice-start.1
  632.8 2.5 copy-start.11
  632.8 2.5 copy-start.13
  638.1 2.6 copy-start.15
  640.8 2.6 copy-start.3
  643.4 12.8 %copy-start.12 = (bf16[1,1024,1,128]{1,3,2,0:T(8,128)(2,1)S(1)}, bf16[1,1024,1,128]{1,3,2,0:T(8,128)(2,1)}, u32[]{:S(2)}) copy-start(bf16[1,1024,1,128]{1,3,2,0:T(8,128)(2,1)} %copy-done.10) | copy-start | bytes 786436
  652.8 13.1 %all-to-all-start.5 = ((bf16[8,2,8192]{2,1,0:T(2,128)(2,1)}), bf16[8,2,8192]{2,1,0:T(2,128)(2,1)S(1)}, u32[]{:S(2)}, u32[]{:S(2)}) async-start(bf16[8,2,8192]{2,1,0:T(2,128)(2,1)} %reshape.439), calls=%async_computation.7 | async-start | bytes 524288 | tf_op jit(solution)/shard_map/all_to_all | solution.py:262
  659.8 11.5 copy-start.22
  659.9 11.5 copy-start.23
  665.9 19.9 %all-to-all-start.4 = ((bf16[8,2,16384]{2,1,0:T(2,128)(2,1)}), bf16[8,2,16384]{2,1,0:T(2,128)(2,1)S(1)}, u32[]{:S(2)}, u32[]{:S(2)}) async-start(bf16[8,2,16384]{2,1,0:T(2,128)(2,1)} %reshape.441), calls=%async_computation.6 | async-start | bytes 1048576 | tf_op jit(solution)/shard_map/all_to_all | solution.py:259
  670.5 522.7 %reduce-scatter.12.cloned.1.call-start = ((), (), s32[]{:S(2)}) async-start(), calls=%async_computation.21 | async-start | bytes 25952256 | tf_op jit(solution)/shard_map/reduce_scatter | solution.py:283
  757.7 52.5 %copy-start.6 = (f32[128,2048]{1,0:T(8,128)S(1)}, f32[128,2048]{1,0:T(8,128)}, u32[]{:S(2)}) copy-start(f32[128,2048]{1,0:T(8,128)} %copy-done.5) | copy-start | bytes 3145732
  757.7 52.5 %copy-start.26 = (f32[128]{0:T(128)S(1)}, f32[128]{0:T(128)}, u32[]{:S(2)}) copy-start(f32[128]{0:T(128)} %get-tuple-element.101) | copy-start | bytes 1540
  (4 other events, 4.2 us)
Sparse Core Ops, SparseCore 0:
  11.0 98.8 all-gather.8
  112.8 96.1 all-gather.10
  210.9 50.0 all-gather.14
  263.0 46.8 all-gather.12
  311.6 51.3 all-gather.16
  364.7 52.5 all-gather.18
  418.9 46.8 all-gather.20
  490.5 48.7 reduce-scatter.9
  541.5 48.3 reduce-scatter.7
  592.7 51.0 reduce-scatter.15
  646.8 52.5 reduce-scatter.17
  702.3 52.5 reduce-scatter.19
  757.8 187.6 reduce-scatter.13
  952.3 240.8 reduce-scatter.11
where the time goes:
time: 1210 us; the launch traced here: 1200 us
  waiting for transfers between devices  852 us (70%)
  matrix products  153 us (13%)
  blocking collectives  103 us (9%)
  other arithmetic  39.6 us (3%)
  starting transfers between devices  19.3 us (2%)
  local copies, waits for them, and re-layouts  17.6 us (1%)
  between operations  15 us (1%)
    reduce_scatter x1, waiting for transfers between devices, per_device(): lax.psum_scatter(qkv_term, ('dp', 'seq'), scatter_dimension=0, tiled=True)  248 us
    reduce_scatter x1, waiting for transfers between devices, per_device(): lax.psum_scatter(out_term, ('dp', 'seq'), scatter_dimension=0, tiled=True)  133 us
    unnamed x2, blocking collectives  84.6 us
    all_gather x1, waiting for transfers between devices, per_device(): lax.all_gather(qkv_weight, ('dp', 'seq'), axis=0, tiled=True)  53.6 us
    reduce_scatter x1, waiting for transfers between devices, feed_split(): lax.psum_scatter(lax.dot_general(inner, grad_all, contract_rows, preferre...  51.1 us
    reduce_scatter x1, waiting for transfers between devices, feed_split(): lax.psum_scatter(jnp.dot(inner, down_part, preferred_element_type=jnp.flo...  49.3 us
    all_gather x1, waiting for transfers between devices, feed_split(): normed_all = lax.all_gather(normed_two, 'seq', axis=0, tiled=True)  48.9 us
    all_gather x1, waiting for transfers between devices, feed_split(): grad_all = lax.all_gather(grad_low, 'seq', axis=0, tiled=True)  48.5 us
  transfers between devices with their start and end apart: 19, of which 17 were waited for; matrix products, arithmetic and copies ran while one was open for 15% of the time, Pallas kernels for 0%

commit v1 on v0

v1 whole, which is shorter than its diff:
```python
import functools

import jax
import jax.numpy as jnp
from jax import lax
from jax.experimental import pallas as pl
from jax.experimental.pallas import tpu as pltpu
from jax.sharding import PartitionSpec as P

HEADS = 32
KV_HEADS = 8
HEAD_DIM = 64

MESH = pl.DeviceIdType.MESH
ANY = pl.BlockSpec(memory_space=pl.ANY)
VM = pl.BlockSpec(memory_space=pltpu.VMEM)
SUB = 2

epsilon = 1e-05
rope_base = 500000.0
masked_value = -1e30
contract_rows = (((0,), (0,)), ((), ()))
contract_cols = (((1,), (1,)), ((), ()))


class Place:
    def __init__(self, dps, groups):
        self.dps, self.groups, self.chips, self.hops = dps, groups, groups // 2, dps // 2
        self.d, self.s = lax.axis_index("dp"), lax.axis_index("seq")
        self.chip, self.core = self.s // 2, self.s % 2
        self.partner = 2 * self.chip + 1 - self.core
        row, side = self.d // 2, self.d % 2
        self.turn = side * (dps - 1 - row) + (1 - side) * row

    def ring(self, distance):
        at = (self.turn + distance + self.dps) % self.dps
        side = at // self.hops
        return (1 - side) * 2 * at + side * (2 * (self.dps - 1 - at) + 1)


def remote(src, dst, send, recv, **target):
    return pltpu.make_async_remote_copy(
        src_ref=src, dst_ref=dst, send_sem=send, recv_sem=recv, device_id=target, device_id_type=MESH
    )


def greet_near(place):
    barrier = pltpu.get_barrier_semaphore()

    def signal(**target):
        pl.semaphore_signal(barrier, inc=1, device_id=target, device_id_type=MESH)

    signal(seq=place.partner)
    signal(dp=place.ring(1))
    signal(dp=place.ring(-1))

    @pl.when(place.chip > 0)
    def _():
        signal(seq=place.s - 2)

    @pl.when(place.chip < place.chips - 1)
    def _():
        signal(seq=place.s + 2)

    ends = (place.chips - place.chip) // place.chips + (place.chip + 1) // place.chips
    pl.semaphore_wait(barrier, 5 - ends)


def greet_all(place):
    barrier = pltpu.get_barrier_semaphore()
    count = place.dps * place.groups
    me = place.d * place.groups + place.s

    def signal(i, _):
        other = (me + i) % count
        pl.semaphore_signal(
            barrier,
            inc=1,
            device_id={"dp": other // place.groups, "seq": other % place.groups},
            device_id_type=MESH,
        )
        return 0

    lax.fori_loop(1, count, signal, 0)
    pl.semaphore_wait(barrier, count - 1)


DMA = pltpu.SemaphoreType.DMA


class LineGather:
    def __init__(self, x, dps, groups):
        rows, width = x.shape
        shape = (SUB, rows // SUB, width)
        self.inputs, self.in_specs = [x.reshape(shape)], [VM]
        self.outs, self.out_specs = [jax.ShapeDtypeStruct((groups,) + shape, x.dtype)], [ANY]
        self.scratch = [DMA] + [DMA((groups // 2, SUB))] * 6
        self.result = lambda out: out.reshape(groups * rows, width)

    def bind(self, place, x_ref, out_ref, own_sem, us, ur, ds, dr, ps, pr):
        s, chip, chips = place.s, place.chip, place.chips

        def copy(src, group, half, sends, recvs, at, target):
            return remote(
                src, out_ref.at[group, half], sends.at[at, half], recvs.at[at, half], seq=target
            )

        def up(src, group, hop, half):
            return copy(src, group, half, us, ur, hop, s + 2)

        def down(src, group, hop, half):
            return copy(src, group, half, ds, dr, hop, s - 2)

        def pair(src, group, half):
            return copy(src, group, half, ps, pr, group // 2, place.partner)

        own = pltpu.make_async_copy(x_ref, out_ref.at[s], own_sem)

        def start():
            own.start()
            for half in range(SUB):

                @pl.when(chip < chips - 1)
                def _():
                    up(x_ref.at[half], s, 0, half).start()

                @pl.when(chip > 0)
                def _():
                    down(x_ref.at[half], s, 0, half).start()

            for half in range(SUB):
                pair(x_ref.at[half], s, half).start()

        def step(hop, half):
            below, above = s - 2 * hop, s + 2 * hop

            @pl.when(chip - hop >= 0)
            def _():
                block = out_ref.at[below, half]
                up(block, below, hop - 1, half).wait_recv()

                @pl.when(chip < chips - 1)
                def _():
                    up(block, below, hop, half).start()

                pair(block, below, half).start()

            @pl.when(chip + hop < chips)
            def _():
                block = out_ref.at[above, half]
                down(block, above, hop - 1, half).wait_recv()

                @pl.when(chip > 0)
                def _():
                    down(block, above, hop, half).start()

                pair(block, above, half).start()

        def finish():
            own.wait()

            def each(i, _):
                k, half = i // SUB, i % SUB
                mine, other = 2 * k + place.core, 2 * k + 1 - place.core
                block = out_ref.at[mine, half]
                pair(block, other, half).wait_recv()
                pair(block, mine, half).wait_send()

                @pl.when(jnp.logical_and(chip - k >= 0, chip < chips - 1))
                def _():
                    up(block, mine, k, half).wait_send()

                @pl.when(jnp.logical_and(chip + k < chips, chip > 0))
                def _():
                    down(block, mine, k, half).wait_send()

                return 0

            lax.fori_loop(0, chips * SUB, each, 0)

        ticks = {
            (hop - 1) * SUB + half: functools.partial(step, hop, half)
            for hop in range(1, chips)
            for half in range(SUB)
        }
        return start, ticks, finish


class LineScatter:
    def __init__(self, partial, dps, groups):
        total, width = partial.shape
        rows, chips = total // groups, groups // 2
        shape = (SUB, rows // SUB, width)
        self.inputs, self.in_specs = [partial.reshape((groups,) + shape)], [VM]
        self.outs, self.out_specs = [jax.ShapeDtypeStruct(shape, jnp.float32)], [VM]
        self.scratch = [pltpu.VMEM((chips,) + shape, jnp.bfloat16)] * 5 + [DMA((chips, SUB))] * 6
        self.result = lambda out: out.reshape(rows, width)

    def bind(
        self, place, p_ref, out_ref, pairbuf, upbuf, downbuf, usend, dsend, us, ur, ds, dr, ps, pr
    ):
        s, chip, chips, core = place.s, place.chip, place.chips, place.core

        def copy(src, buffer, at, half, sends, recvs, target):
            return remote(
                src, buffer.at[at, half], sends.at[at, half], recvs.at[at, half], seq=target
            )

        def pair(at, half):
            src = p_ref.at[2 * at + 1 - core, half]
            return copy(src, pairbuf, at, half, ps, pr, place.partner)

        def up(at, half):
            return copy(usend.at[at, half], upbuf, at, half, us, ur, s + 2)

        def down(at, half):
            return copy(dsend.at[at, half], downbuf, at, half, ds, dr, s - 2)

        def wide(ref, *at):
            return ref[at].astype(jnp.float32)

        def local(at, half):
            return wide(p_ref, 2 * at + core, half) + wide(pairbuf, at, half)

        def start():
            def issue(i, _):
                low, half = i // SUB, i % SUB
                high = chips - 1 - low

                @pl.when(high > chip)
                def _():
                    pair(high, half).start()

                @pl.when(low < chip)
                def _():
                    pair(low, half).start()

                return 0

            lax.fori_loop(0, (chips - 1) * SUB, issue, 0)
            for half in range(SUB):
                pair(chip, half).start()

        def step(i):
            low, half = i // SUB, i % SUB
            high = chips - 1 - low

            @pl.when(high > chip)
            def _():
                pair(high, half).wait_recv()

                @pl.when(chip > 0)
                def _():
                    up(high, half).wait_recv()
                    total = local(high, half) + wide(upbuf, high, half)
                    usend[high, half] = total.astype(jnp.bfloat16)

                @pl.when(chip == 0)
                def _():
                    usend[high, half] = local(high, half).astype(jnp.bfloat16)

                up(high, half).start()

            @pl.when(low < chip)
            def _():
                pair(low, half).wait_recv()

                @pl.when(chip < chips - 1)
                def _():
                    down(low, half).wait_recv()
                    total = local(low, half) + wide(downbuf, low, half)
                    dsend[low, half] = total.astype(jnp.bfloat16)

                @pl.when(chip == chips - 1)
                def _():
                    dsend[low, half] = local(low, half).astype(jnp.bfloat16)

                down(low, half).start()

        def finish():
            for half in range(SUB):
                pair(chip, half).wait_recv()
                out_ref[half] = local(chip, half)

                @pl.when(chip > 0)
                def _():
                    up(chip, half).wait_recv()
                    out_ref[half] += wide(upbuf, chip, half)

                @pl.when(chip < chips - 1)
                def _():
                    down(chip, half).wait_recv()
                    out_ref[half] += wide(downbuf, chip, half)

            def each(i, _):
                at, half = i // SUB, i % SUB
                pair(at, half).wait_send()

                @pl.when(at > chip)
                def _():
                    up(at, half).wait_send()

                @pl.when(at < chip)
                def _():
                    down(at, half).wait_send()

                return 0

            lax.fori_loop(0, chips * SUB, each, 0)

        return start, {i: functools.partial(step, i) for i in range((chips - 1) * SUB)}, finish


def ring_sems(hops):
    return [DMA((hops, 2))] * 4


def ring_gather(place, own, out, rs, rr, ls, lr):
    hops = place.hops

    def right(src, chunk, hop, half):
        return remote(
            src, out(chunk, half), rs.at[hop - 1, half], rr.at[hop - 1, half], dp=place.ring(1)
        )

    def left(src, chunk, hop, half):
        return remote(
            src, out(chunk, half), ls.at[hop - 1, half], lr.at[hop - 1, half], dp=place.ring(-1)
        )

    def start():
        for half in range(2):
            right(own(half), place.d, 1, half).start()
            left(own(1 - half), place.d, 1, 1 - half).start()

    def forward(hop):
        before, after = place.ring(-hop), place.ring(hop)
        full = hop < hops - 1
        right(out(before, 0), before, hop, 0).wait_recv()
        right(out(before, 0), before, hop + 1, 0).start()
        left(out(after, 1), after, hop, 1).wait_recv()
        left(out(after, 1), after, hop + 1, 1).start()
        right(out(before, 1), before, hop, 1).wait_recv()
        left(out(after, 0), after, hop, 0).wait_recv()
        if full:
            right(out(before, 1), before, hop + 1, 1).start()
            left(out(after, 0), after, hop + 1, 0).start()

    def finish():
        right(out(place.d, 0), place.ring(-hops), hops, 0).wait_recv()
        left(out(place.d, 1), place.ring(hops), hops, 1).wait_recv()
        for hop in range(1, hops + 1):
            for half in range(2):
                if hop < hops or half == 0:
                    right(out(place.d, half), place.d, hop, half).wait_send()
                if hop < hops or half == 1:
                    left(out(place.d, half), place.d, hop, half).wait_send()

    return start, forward, finish


def ring_scatter(place, part, put, rbuf, lbuf, rout, lout, rs, rr, ls, lr):
    hops = place.hops

    def wide(ref):
        return ref[...].astype(jnp.float32)

    def right(src, hop, half):
        return remote(
            src,
            rbuf.at[hop - 1, half],
            rs.at[hop - 1, half],
            rr.at[hop - 1, half],
            dp=place.ring(1),
        )

    def left(src, hop, half):
        return remote(
            src,
            lbuf.at[hop - 1, half],
            ls.at[hop - 1, half],
            lr.at[hop - 1, half],
            dp=place.ring(-1),
        )

    def start():
        right(part(place.ring(hops), 0), hops, 0).start()
        left(part(place.ring(-hops), 1), hops, 1).start()
        right(part(place.ring(hops - 1), 1), hops - 1, 1).start()
        left(part(place.ring(1 - hops), 0), hops - 1, 0).start()

    def forward(hop):
        for first in range(2 if hop < hops - 1 else 1):
            half = first
            right(rbuf.at[hop, half], hop + 1, half).wait_recv()
            total = wide(part(place.ring(hop), half)) + wide(rbuf.at[hop, half])
            rout[hop - 1, half] = total.astype(jnp.bfloat16)
            right(rout.at[hop - 1, half], hop, half).start()
            half = 1 - first
            left(lbuf.at[hop, half], hop + 1, half).wait_recv()
            total = wide(part(place.ring(-hop), half)) + wide(lbuf.at[hop, half])
            lout[hop - 1, half] = total.astype(jnp.bfloat16)
            left(lout.at[hop - 1, half], hop, half).start()

    def finish():
        for half in range(2):
            right(rbuf.at[0, half], 1, half).wait_recv()
            left(lbuf.at[0, half], 1, half).wait_recv()
            put(
                half,
                wide(part(place.d, half)) + wide(rbuf.at[0, half]) + wide(lbuf.at[0, half]),
            )
        for hop in range(1, hops + 1):
            for half in range(2):
                if hop < hops or half == 0:
                    right(rbuf.at[0, half], hop, half).wait_send()
                if hop < hops or half == 1:
                    left(lbuf.at[0, half], hop, half).wait_send()

    return start, forward, finish


class RingGather:
    def __init__(self, x, dps, groups):
        rows, width = x.shape
        shape = (2, rows // 2, width)
        self.inputs, self.in_specs = [x.reshape(shape)], [VM]
        self.outs, self.out_specs = [jax.ShapeDtypeStruct((dps,) + shape, x.dtype)], [ANY]
        self.scratch = [DMA] + ring_sems(dps // 2)
        self.result = lambda out: out.reshape(dps * rows, width)

    def bind(self, place, x_ref, out_ref, own_sem, *sems):
        own = pltpu.make_async_copy(x_ref, out_ref.at[place.d], own_sem)
        ring = ring_gather(
            place, lambda half: x_ref.at[half], lambda chunk, half: out_ref.at[chunk, half], *sems
        )

        def start():
            ring[0]()
            own.start()

        def finish():
            own.wait()
            ring[2]()

        ticks = {2 * hop - 1: functools.partial(ring[1], hop) for hop in range(1, place.hops)}
        return start, ticks, finish


class RingScatter:
    def __init__(self, partial, dps, groups):
        total, width = partial.shape
        rows, hops = total // dps, dps // 2
        shape = (2, rows // 2, width)
        self.inputs, self.in_specs = [partial.reshape((dps,) + shape)], [VM]
        self.outs, self.out_specs = [jax.ShapeDtypeStruct(shape, jnp.float32)], [VM]
        self.scratch = (
            [pltpu.VMEM((hops,) + shape, jnp.bfloat16)] * 2
            + [pltpu.VMEM((hops - 1,) + shape, jnp.bfloat16)] * 2
            + ring_sems(hops)
        )
        self.result = lambda out: out.reshape(rows, width)

    def bind(self, place, p_ref, out_ref, *scratch):
        def put(half, value):
            out_ref[half] = value

        ring = ring_scatter(place, lambda chunk, half: p_ref.at[chunk, half], put, *scratch)
        ticks = {
            2 * (place.hops - hop) - 1: functools.partial(ring[1], hop)
            for hop in range(1, place.hops)
        }
        return ring[0], ticks, ring[2]


class Columns:
    def __init__(self, blocks, dps, groups):
        _, rows, width = blocks.shape
        self.inputs, self.in_specs = [blocks], [VM]
        self.outs = [jax.ShapeDtypeStruct((dps, groups, rows, width), blocks.dtype)]
        self.out_specs = [ANY]
        self.scratch = [
            pltpu.VMEM((groups, rows, width), blocks.dtype),
            DMA((2,)),
            DMA((groups,)),
            DMA((groups,)),
        ] + ring_sems(dps // 2)
        self.result = lambda out: out.reshape(dps * groups * rows, width)

    def bind(self, place, x_ref, out_ref, landing, own_sem, sends, recvs, *sems):
        s, groups = place.s, place.groups
        half_of = groups // 2
        here = pltpu.make_async_copy(x_ref.at[s], landing.at[s], own_sem.at[0])
        own = pltpu.make_async_copy(landing, out_ref.at[place.d], own_sem.at[1])

        def swap(i):
            to = (s + i) % groups
            return remote(x_ref.at[to], landing.at[s], sends.at[i], recvs.at[i], seq=to)

        ring = ring_gather(
            place,
            lambda half: landing.at[pl.ds(half * half_of, half_of)],
            lambda chunk, half: out_ref.at[chunk, pl.ds(half * half_of, half_of)],
            *sems,
        )

        def start():
            here.start()
            for i in range(1, groups):
                swap(i).start()

        def middle():
            here.wait()
            for i in range(1, groups):
                swap(i).wait_recv()
            ring[0]()
            own.start()

        def finish():
            for i in range(1, groups):
                swap(i).wait_send()
            own.wait()
            ring[2]()

        ticks = {1 + 2 * hop: functools.partial(ring[1], hop) for hop in range(1, place.hops)}
        ticks[1] = middle
        return start, ticks, finish


class ColumnsBack:
    def __init__(self, partial, rows, dps, groups):
        width, hops = partial.shape[1], dps // 2
        shape = (groups, rows, width)
        halves = (2, groups // 2, rows, width)
        self.inputs, self.in_specs = [partial.reshape((dps,) + halves)], [VM]
        self.outs, self.out_specs = [jax.ShapeDtypeStruct(shape, jnp.bfloat16)], [ANY]
        self.scratch = (
            [pltpu.VMEM(halves, jnp.bfloat16), DMA, DMA((groups,)), DMA((groups,))]
            + [pltpu.VMEM((hops,) + halves, jnp.bfloat16)] * 2
            + [pltpu.VMEM((hops - 1,) + halves, jnp.bfloat16)] * 2
            + ring_sems(hops)
        )
        self.result = lambda out: out

    def bind(self, place, p_ref, out_ref, total, own_sem, sends, recvs, *scratch):
        s, groups = place.s, place.groups
        half_of = groups // 2

        def put(half, value):
            total[half] = value.astype(jnp.bfloat16)

        ring = ring_scatter(place, lambda chunk, half: p_ref.at[chunk, half], put, *scratch)
        here = pltpu.make_async_copy(
            total.at[s // half_of, s % half_of], out_ref.at[s], own_sem
        )

        def swap(i):
            to = (s + i) % groups
            src = total.at[to // half_of, to % half_of]
            return remote(src, out_ref.at[s], sends.at[i], recvs.at[i], seq=to)

        def last():
            ring[2]()
            here.start()
            for i in range(1, groups):
                swap(i).start()

        def finish():
            here.wait()
            for i in range(1, groups):
                swap(i).wait_recv()
                swap(i).wait_send()

        ticks = {
            2 * (place.hops - hop) - 1: functools.partial(ring[1], hop)
            for hop in range(1, place.hops)
        }
        ticks[2 * place.hops - 1] = last
        return ring[0], ticks, finish


class Rows:
    def __init__(self, x, dps, groups):
        rows, width = x.shape
        shape = (2, rows // 2, width)
        self.inputs, self.in_specs = [x.reshape(shape)], [VM]
        self.outs, self.out_specs = [jax.ShapeDtypeStruct((dps,) + shape, x.dtype)], [ANY]
        self.scratch = [
            pltpu.VMEM((dps,) + shape, x.dtype),
            DMA((2,)),
            DMA((dps,)),
            DMA((dps,)),
        ] + ring_sems(dps // 2)
        self.result = lambda out: out.reshape(dps * rows, width)

    def bind(self, place, x_ref, out_ref, landing, own_sem, sends, recvs, *sems):
        s, dps = place.s, place.dps
        slot, base = s % dps, s // dps * dps
        first = pltpu.make_async_copy(x_ref, landing.at[place.d], own_sem.at[0])
        here = pltpu.make_async_copy(landing.at[slot], out_ref.at[slot], own_sem.at[1])
        ring = ring_gather(
            place, lambda half: x_ref.at[half], lambda chunk, half: landing.at[chunk, half], *sems
        )

        def swap(i):
            to = (slot + i) % dps
            return remote(landing.at[to], out_ref.at[slot], sends.at[i], recvs.at[i], seq=base + to)

        def start():
            ring[0]()
            first.start()

        def last():
            first.wait()
            ring[2]()
            here.start()
            for i in range(1, dps):
                swap(i).start()

        def finish():
            here.wait()
            for i in range(1, dps):
                swap(i).wait_recv()
                swap(i).wait_send()

        ticks = {2 * hop - 1: functools.partial(ring[1], hop) for hop in range(1, place.hops)}
        ticks[2 * place.hops] = last
        return start, ticks, finish


class RowsBack:
    def __init__(self, partial, rows, dps, groups):
        width, hops = partial.shape[1], dps // 2
        shape = (2, rows // 2, width)
        self.inputs, self.in_specs = [partial.reshape((dps,) + shape)], [VM]
        self.outs, self.out_specs = [jax.ShapeDtypeStruct(shape, jnp.float32)], [VM]
        self.scratch = (
            [pltpu.VMEM((dps,) + shape, jnp.bfloat16), DMA, DMA((dps,)), DMA((dps,))]
            + [pltpu.VMEM((hops,) + shape, jnp.bfloat16)] * 2
            + [pltpu.VMEM((hops - 1,) + shape, jnp.bfloat16)] * 2
            + ring_sems(hops)
        )
        self.result = lambda out: out.reshape(rows, width)

    def bind(self, place, p_ref, out_ref, landing, own_sem, sends, recvs, *scratch):
        s, dps = place.s, place.dps
        slot, base = s % dps, s // dps * dps
        here = pltpu.make_async_copy(p_ref.at[slot], landing.at[slot], own_sem)

        def swap(i):
            to = (slot + i) % dps
            return remote(p_ref.at[to], landing.at[slot], sends.at[i], recvs.at[i], seq=base + to)

        def put(half, value):
            out_ref[half] = value

        ring = ring_scatter(place, lambda chunk, half: landing.at[chunk, half], put, *scratch)

        def start():
            here.start()
            for i in range(1, dps):
                swap(i).start()

        def middle():
            here.wait()
            for i in range(1, dps):
                swap(i).wait_recv()
            ring[0]()

        def finish():
            for i in range(1, dps):
                swap(i).wait_send()
            ring[2]()

        ticks = {
            2 * (place.hops - hop) + 2: functools.partial(ring[1], hop)
            for hop in range(1, place.hops)
        }
        ticks[2] = middle
        return start, ticks, finish


class Spread:
    def __init__(self, tiles, total, dps, groups):
        count, shape = dps * groups, tiles.shape[-2:]
        self.total = total
        self.inputs, self.in_specs = [tiles], [VM]
        out = shape if total else (count,) + shape
        self.outs, self.out_specs = [jax.ShapeDtypeStruct(out, jnp.float32)], [VM]
        self.scratch = [pltpu.VMEM((count,) + shape, jnp.float32), DMA((count,)), DMA((count,))]
        self.result = lambda out: out

    def bind(self, place, x_ref, out_ref, landing, sends, recvs):
        count = place.dps * place.groups
        me = place.d * place.groups + place.s

        def copy(i):
            other = (me + i) % count
            return remote(
                x_ref.at[other] if self.total else x_ref,
                landing.at[me],
                sends.at[i],
                recvs.at[i],
                dp=other // place.groups,
                seq=other % place.groups,
            )

        def start():
            def each(i, _):
                copy(i).start()
                return 0

            lax.fori_loop(1, count, each, 0)

        def finish():
            def each(i, _):
                copy(i).wait_recv()
                copy(i).wait_send()
                return 0

            lax.fori_loop(1, count, each, 0)
            landing[me] = x_ref[me] if self.total else x_ref[...]
            out_ref[...] = jnp.sum(landing[...], axis=0) if self.total else landing[...]

        return start, {}, finish


def move(parts, dps, groups, number, greet=greet_near):
    def kernel(*refs):
        place = Place(dps, groups)
        at = [
            0,
            sum(len(part.inputs) for part in parts),
            sum(len(part.inputs) + len(part.outs) for part in parts),
        ]
        bound = []
        for part in parts:
            mine = []
            for kind, length in enumerate((len(part.inputs), len(part.outs), len(part.scratch))):
                mine += refs[at[kind] : at[kind] + length]
                at[kind] += length
            bound.append(part.bind(place, *mine))
        greet(place)
        for start, _, _ in bound:
            start()
        for tick in range(1 + max([0] + [max(list(ticks) + [0]) for _, ticks, _ in bound])):
            for _, ticks, _ in bound:
                if tick in ticks:
                    ticks[tick]()
        for _, _, finish in bound:
            finish()

    outs = pl.pallas_call(
        kernel,
        out_shape=[out for part in parts for out in part.outs],
        in_specs=[spec for part in parts for spec in part.in_specs],
        out_specs=[spec for part in parts for spec in part.out_specs],
        scratch_shapes=[one for part in parts for one in part.scratch],
        compiler_params=pltpu.CompilerParams(
            collective_id=number, has_side_effects=True, vmem_limit_bytes=56 << 20
        ),
        cost_estimate=pl.CostEstimate(flops=0, bytes_accessed=120_000_000, transcendentals=0),
        name=f"move_{number}",
    )(*[x for part in parts for x in part.inputs])
    results = []
    for part in parts:
        results.append(part.result(outs[len(results)]))
    return results


def norm_factor(values):
    return lax.rsqrt(jnp.mean(values * values, axis=-1, keepdims=True) + epsilon)


def norm_grad(values, factor, gain, gradient):
    weighted = gradient * gain
    inner_mean = jnp.mean(weighted * values, axis=-1, keepdims=True)
    return factor * weighted - values * (factor * factor * factor) * inner_mean


def rope_tables(positions, head_width):
    half_width = head_width // 2
    frequency = rope_base ** (-2.0 * jnp.arange(half_width, dtype=jnp.float32) / head_width)
    angles = positions.astype(jnp.float32)[:, None] * frequency[None, :]
    return (jnp.cos(angles)[:, None, :], jnp.sin(angles)[:, None, :])


def rotate(values, cosine_table, sine_table):
    half_width = values.shape[-1] // 2
    first_half = values[..., :half_width]
    second_half = values[..., half_width:]
    return jnp.concatenate(
        [
            first_half * cosine_table - second_half * sine_table,
            second_half * cosine_table + first_half * sine_table,
        ],
        axis=-1,
    )


def gated_grad(gate, upward, grad_inner):
    sigmoid_gate = jax.nn.sigmoid(gate)
    grad_gate = grad_inner * upward * sigmoid_gate * (1.0 + gate * (1.0 - sigmoid_gate))
    grad_upward = grad_inner * (gate * sigmoid_gate)
    return (grad_gate.astype(jnp.bfloat16), grad_upward.astype(jnp.bfloat16))


def block_scores(query_block, key_heads, lower, upper, score_scale):
    scores = (
        jnp.einsum(
            "qhd,kd->hqk", query_block, key_heads[:upper], preferred_element_type=jnp.float32
        )
        * score_scale
    )
    rows_at = lower + jnp.arange(query_block.shape[0], dtype=jnp.int32)
    cols_at = jnp.arange(upper, dtype=jnp.int32)
    allowed = (cols_at[None, :] <= rows_at[:, None])[None]
    return jnp.where(allowed, scores, masked_value)


def per_device(
    tokens,
    qkv_weight,
    out_weight,
    gate_weight,
    up_weight,
    down_weight,
    attn_gain,
    mlp_gain,
    cotangent,
):
    groups = lax.axis_size("seq")
    dps = lax.axis_size("dp")
    tok_rows = tokens.shape[1]
    model_width = tokens.shape[2]
    weight_rows = qkv_weight.shape[0]
    seq_len = tok_rows * groups
    local_heads = HEADS // groups
    local_width = local_heads * HEAD_DIM
    kv_copies = groups // KV_HEADS
    score_scale = HEAD_DIM ** (-0.5)
    block_rows = min(512, seq_len)
    block_count = seq_len // block_rows
    fold = groups // dps
    order = [(at % dps) * fold + at // dps for at in range(groups)]

    q_part = qkv_weight[:, :model_width].reshape(weight_rows, groups, local_width)
    k_part = qkv_weight[:, model_width : model_width + KV_HEADS * HEAD_DIM]
    v_part = qkv_weight[:, model_width + KV_HEADS * HEAD_DIM :]
    k_part = k_part.reshape(weight_rows, KV_HEADS, HEAD_DIM)
    v_part = v_part.reshape(weight_rows, KV_HEADS, HEAD_DIM)
    columns = jnp.stack(
        [
            jnp.concatenate(
                [q_part[:, g], k_part[:, g // kv_copies], v_part[:, g // kv_copies]], axis=1
            )
            for g in order
        ]
    )
    gain_width = attn_gain.shape[0]
    tile = jnp.zeros((8, 128), jnp.float32)
    tile = tile.at[0, :gain_width].set(attn_gain.astype(jnp.float32))
    tile = tile.at[1, :gain_width].set(mlp_gain.astype(jnp.float32))
    qkv_local, tokens_all, out_rows, gate_part, gains = move(
        [
            Columns(columns, dps, groups),
            LineGather(tokens[0], dps, groups),
            Rows(out_weight, dps, groups),
            RingGather(gate_weight, dps, groups),
            Spread(tile, False, dps, groups),
        ],
        dps,
        groups,
        1,
        greet_all,
    )
    gain_one = gains[:, 0, :gain_width].reshape(model_width)
    gain_two = gains[:, 1, :gain_width].reshape(model_width)

    x_rows = tokens[0].astype(jnp.float32)
    factor_one = norm_factor(x_rows)
    all_rows = tokens_all.astype(jnp.float32)
    normed_all = (all_rows * norm_factor(all_rows) * gain_one).astype(jnp.bfloat16)
    grad_low = cotangent[0]
    grad_low, _ = lax.optimization_barrier((grad_low, gains))
    grad_all = lax.all_gather(grad_low, "seq", axis=0, tiled=True)

    mixed = jnp.dot(normed_all, qkv_local, preferred_element_type=jnp.float32)
    cosine_table, sine_table = rope_tables(jnp.arange(seq_len, dtype=jnp.int32), HEAD_DIM)
    query_heads = rotate(
        mixed[:, :local_width].reshape(seq_len, local_heads, HEAD_DIM), cosine_table, sine_table
    ).astype(jnp.bfloat16)
    key_heads = rotate(
        mixed[:, None, local_width : local_width + HEAD_DIM], cosine_table, sine_table
    ).astype(jnp.bfloat16)[:, 0]
    value_heads = mixed[:, local_width + HEAD_DIM :].astype(jnp.bfloat16)
    outputs = []
    log_sums = []
    for block in range(block_count):
        lower = block * block_rows
        upper = lower + block_rows
        scores = block_scores(query_heads[lower:upper], key_heads, lower, upper, score_scale)
        highest = jnp.max(scores, axis=-1, keepdims=True)
        log_sum = highest + jnp.log(jnp.sum(jnp.exp(scores - highest), axis=-1, keepdims=True))
        probs = jnp.exp(scores - log_sum).astype(jnp.bfloat16)
        attended = jnp.einsum(
            "hqk,kd->qhd", probs, value_heads[:upper], preferred_element_type=jnp.float32
        )
        outputs.append(attended.astype(jnp.bfloat16))
        log_sums.append(log_sum)
    attended = jnp.concatenate(outputs, axis=0).reshape(seq_len, local_width)
    partial = jnp.dot(attended, out_rows, preferred_element_type=jnp.float32)
    summed, up_part = move(
        [
            LineScatter(partial.astype(jnp.bfloat16), dps, groups),
            RingGather(up_weight, dps, groups),
        ],
        dps,
        groups,
        2,
    )
    hidden = x_rows + summed
    factor_two = norm_factor(hidden)
    normed_two = (hidden * factor_two * gain_two).astype(jnp.bfloat16)
    hn_all, down_part = move(
        [LineGather(normed_two, dps, groups), RingGather(down_weight, dps, groups)],
        dps,
        groups,
        3,
    )

    gate = lax.dot_general(hn_all, gate_part, contract_cols, preferred_element_type=jnp.float32)
    upward = lax.dot_general(hn_all, up_part, contract_cols, preferred_element_type=jnp.float32)
    grad_inner = lax.dot_general(
        grad_all, down_part, contract_cols, preferred_element_type=jnp.float32
    )
    inner = (jax.nn.silu(gate) * upward).astype(jnp.bfloat16)
    grad_gate, grad_upward = gated_grad(gate, upward, grad_inner)
    mlp_result = lax.psum_scatter(
        jnp.dot(inner, down_part, preferred_element_type=jnp.float32).astype(jnp.bfloat16),
        "seq",
        scatter_dimension=0,
        tiled=True,
    ).astype(jnp.float32)
    down_term, gate_term, up_term = [
        lax.dot_general(left, right, contract_rows, preferred_element_type=jnp.float32).astype(
            jnp.bfloat16
        )
        for left, right in ((inner, grad_all), (grad_gate, hn_all), (grad_upward, hn_all))
    ]
    partial = jnp.dot(grad_gate, gate_part, preferred_element_type=jnp.float32) + jnp.dot(
        grad_upward, up_part, preferred_element_type=jnp.float32
    )
    grad_normed, down_owned = move(
        [
            LineScatter(partial.astype(jnp.bfloat16), dps, groups),
            RingScatter(down_term, dps, groups),
        ],
        dps,
        groups,
        4,
    )

    block_out = (hidden + mlp_result).astype(jnp.bfloat16)[None]
    gain_two_term = jnp.sum(grad_normed * hidden * factor_two, axis=0)
    grad_hidden = grad_low.astype(jnp.float32) + norm_grad(
        hidden, factor_two, gain_two, grad_normed
    )
    grad_branch, gate_owned = move(
        [
            LineGather(grad_hidden.astype(jnp.bfloat16), dps, groups),
            RingScatter(gate_term, dps, groups),
        ],
        dps,
        groups,
        5,
    )
    out_term = lax.dot_general(
        attended, grad_branch, contract_rows, preferred_element_type=jnp.float32
    ).astype(jnp.bfloat16)
    grad_heads = (
        lax.dot_general(grad_branch, out_rows, contract_cols, preferred_element_type=jnp.float32)
        .astype(jnp.bfloat16)
        .reshape(seq_len, local_heads, HEAD_DIM)
    )
    grad_keys = jnp.zeros((seq_len, HEAD_DIM), jnp.float32)
    grad_values = jnp.zeros((seq_len, HEAD_DIM), jnp.float32)
    grad_queries = []
    for block in range(block_count):
        lower = block * block_rows
        upper = lower + block_rows
        query_block = query_heads[lower:upper]
        grad_block = grad_heads[lower:upper]
        scores = block_scores(query_block, key_heads, lower, upper, score_scale)
        probs = jnp.exp(scores - log_sums[block])
        probs_low = probs.astype(jnp.bfloat16)
        grad_probs = jnp.einsum(
            "qhd,kd->hqk", grad_block, value_heads[:upper], preferred_element_type=jnp.float32
        )
        row_delta = jnp.sum(probs * grad_probs, axis=-1, keepdims=True)
        grad_scores = (probs * (grad_probs - row_delta)).astype(jnp.bfloat16)
        grad_queries.append(
            jnp.einsum(
                "hqk,kd->qhd", grad_scores, key_heads[:upper], preferred_element_type=jnp.float32
            )
            * score_scale
        )
        grad_keys = grad_keys.at[:upper].add(
            jnp.einsum("hqk,qhd->kd", grad_scores, query_block, preferred_element_type=jnp.float32)
            * score_scale
        )
        grad_values = grad_values.at[:upper].add(
            jnp.einsum("hqk,qhd->kd", probs_low, grad_block, preferred_element_type=jnp.float32)
        )
    grad_q = rotate(jnp.concatenate(grad_queries, axis=0), cosine_table, -sine_table)
    grad_k = rotate(grad_keys[:, None], cosine_table, -sine_table)[:, 0]
    grad_mixed = jnp.concatenate(
        [grad_q.reshape(seq_len, local_width), grad_k, grad_values], axis=1
    ).astype(jnp.bfloat16)
    qkv_term = lax.dot_general(
        normed_all, grad_mixed, contract_rows, preferred_element_type=jnp.float32
    )
    partial = lax.dot_general(
        grad_mixed, qkv_local, contract_cols, preferred_element_type=jnp.float32
    )
    qkv_owned, grad_normed_one, out_owned, up_owned = move(
        [
            ColumnsBack(qkv_term.astype(jnp.bfloat16), weight_rows, dps, groups),
            LineScatter(partial.astype(jnp.bfloat16), dps, groups),
            RowsBack(out_term, weight_rows, dps, groups),
            RingScatter(up_term, dps, groups),
        ],
        dps,
        groups,
        6,
        greet_all,
    )
    qkv_owned = qkv_owned.astype(jnp.float32)
    place = [order.index(g) for g in range(groups)]
    qkv_owned = jnp.concatenate(
        [qkv_owned[place[g], :, :local_width] for g in range(groups)]
        + [
            sum(
                qkv_owned[place[head * kv_copies + i], :, at : at + HEAD_DIM]
                for i in range(kv_copies)
            )
            for at in (local_width, local_width + HEAD_DIM)
            for head in range(KV_HEADS)
        ],
        axis=1,
    )
    gain_one_term = jnp.sum(grad_normed_one * x_rows * factor_one, axis=0)
    grad_input = grad_hidden + norm_grad(x_rows, factor_one, gain_one, grad_normed_one)
    terms = jnp.stack([gain_one_term, gain_two_term]).reshape(2, dps * groups, gain_width)
    terms = jnp.pad(terms.transpose(1, 0, 2), ((0, 0), (0, 6), (0, 128 - gain_width)))
    (gain_grads,) = move([Spread(terms, True, dps, groups)], dps, groups, 7, greet_all)
    return (
        block_out,
        grad_input[None],
        qkv_owned,
        out_owned,
        gate_owned,
        up_owned,
        down_owned,
        gain_grads[0, :gain_width],
        gain_grads[1, :gain_width],
    )


def solution(mesh):
    rows = P(("dp", "seq"), None)
    tokens = P("dp", "seq", None)
    gains = P(("dp", "seq"))
    return jax.shard_map(
        per_device,
        mesh=mesh,
        in_specs=(tokens, rows, rows, rows, rows, rows, gains, gains, tokens),
        out_specs=(tokens, tokens, rows, rows, rows, rows, rows, gains, gains),
        check_vma=False,
    )
```

time: 1210 us -> 554 us (0.46)
  waiting for transfers between devices: 852 us -> 0.04 us
  Pallas kernels: 0 us -> 370 us
  blocking collectives: 103 us -> 0 us
  matrix products: 153 us -> 106 us
  starting transfers between devices: 19.3 us -> 0.25 us
    reduce_scatter x7 -> x1, waiting for transfers between devices: 491 us -> 0.01 us  [per_device(): lax.psum_scatter(jnp.dot(inner, down_part, preferred_element_type=jnp.flo...]
    pallas_call x0 -> x7, Pallas kernels: none -> 370 us  [move(): pl.pallas_call(kernel, out_shape=[out for part in parts for out in part.o...]
    all_gather x7 -> x1, waiting for transfers between devices: 283 us -> 0.01 us  [per_device(): grad_all = lax.all_gather(grad_low, 'seq', axis=0, tiled=True)]
    unnamed x2 -> x0, blocking collectives: 84.6 us -> none
    all_to_all x5 -> x0, waiting for transfers between devices: 74.1 us -> none  [the longest x1 23.8 us: per_device(): lax.all_to_all(query_send, 'seq', split_axis=2, concat_axis=1, tiled=True)]
    dot_general x15, matrix products: 131 us -> 86.6 us  [the longest x3 22.2 us: per_device(): lax.dot_general(left, right, contract_rows, preferred_element_type=jnp.fl...]
    all_to_all x5 -> x0, starting transfers between devices: 18.4 us -> none  [the longest x1 4.62 us: per_device(): lax.all_to_all(query_back.astype(jnp.bfloat16), 'seq', split_axis=1, conc...]
    all_to_all x1 -> x0, blocking collectives: 17.9 us -> none  [per_device(): lax.all_to_all(grad_send, 'seq', split_axis=2, concat_axis=1, tiled=True)]
  transfers between devices with their start and end apart: 19 -> 2, of which waited for: 17 -> 0; matrix products, arithmetic and copies ran while one was open for 15% -> 15% of each run, Pallas kernels for 0% -> 30%
where the time goes in v1:
time: 554 us; the launch traced here: 550 us
  Pallas kernels  370 us (67%)
  matrix products  106 us (19%)
  other arithmetic  37.4 us (7%)
  local copies, waits for them, and re-layouts  20.5 us (4%)
  between operations  15.4 us (3%)
    pallas_call x7, Pallas kernels, move(): pl.pallas_call(kernel, out_shape=[out for part in parts for out in part.o...  370 us
    dot_general x3, matrix products, per_device(): lax.dot_general(left, right, contract_rows, preferred_element_type=jnp.fl...  22.2 us
    dot_general x1, matrix products, per_device(): lax.dot_general(grad_all, down_part, contract_cols, preferred_element_typ...  14 us
  transfers between devices with their start and end apart: 2, of which 0 were waited for; matrix products, arithmetic and copies ran while one was open for 15% of the time, Pallas kernels for 30%

profile of v1, /device:TPU:0, one launch (start us, length us, event | category | flops | bytes accessed | tf_op | source)
XLA Modules:
  0.0 549.9 jit_solution(17737101571693652724)
XLA Ops:
  13.5 69.4 %move_1.1 = (bf16[4,8,64,384]{3,2,1,0:T(8,128)(2,1)}, bf16[8,2,64,2048]{3,2,1,0:T(8,128)(2,1)}, bf16[4,2,32,2048]{3,2,1,0:T(8,128)(2,1)}, bf16[4,2,128,2048]{3,2,1,0:T(8,128)(2,1)}, f32[32,8,128]{2,1,0:T(8,128)}) custom-call(bf16[8,64,384]{2,1,0:T(8,128)(2,1)} %copy-done.23, bf16[2,64,2048]{2,1,0:T(8,128)(2,1)} %bitcast.356, bf16[2,32,2048]{2,1,0:T(8,128)(2,1)} %bitcast.397, ...), custom_call_target="tpu_custom_call" | custom-call | bytes 120000000 | tf_op jit(solution)/shard_map/move_1/pallas_call | solution.py:753
  84.4 3.1 multiply_reduce_fusion
  87.6 3.7 multiply_convert_fusion
  91.3 1.9 fusion.90
  97.6 1.5 fusion.6
  99.2 2.1 exponential_reduce_fusion
  101.3 1.3 fusion.20
  102.6 2.4 fusion.15
  105.1 3.2 convolution_convert_fusion.1
  108.3 58.2 %move_2.1 = (f32[2,64,2048]{2,1,0:T(8,128)}, bf16[4,2,128,2048]{3,2,1,0:T(8,128)(2,1)}) custom-call(bf16[8,2,64,2048]{3,2,1,0:T(8,128)(2,1)} %bitcast.355, bf16[2,128,2048]{2,1,0:T(8,128)(2,1)} %bitcast.380), custom_call_target="tpu_custom_call" | custom-call | bytes 120000000 | tf_op jit(solution)/shard_map/move_2/pallas_call | solution.py:753
  166.5 1.6 multiply_reduce_fusion.3
  168.1 2.2 multiply_convert_fusion.4.refs_0_
  170.3 46.5 %move_3.1 = (bf16[8,2,64,2048]{3,2,1,0:T(8,128)(2,1)}, bf16[4,2,128,2048]{3,2,1,0:T(8,128)(2,1)}) custom-call(bf16[2,64,2048]{2,1,0:T(8,128)(2,1)} %multiply_convert_fusion.4.refs_0_, bf16[2,128,2048]{2,1,0:T(8,128)(2,1)} %bitcast.381), custom_call_target="tpu_custom_call" | custom-call | bytes 120000000 | tf_op jit(solution)/shard_map/move_3/pallas_call | solution.py:753
  216.8 8.5 %fusion.92 = f32[1024,1024]{1,0:T(8,128)} fusion(bf16[1024,2048]{1,0:T(8,128)(2,1)} %bitcast.401, bf16[1024,2048]{1,0:T(8,128)(2,1)S(1)} %bitcast.405), kind=kOutput, calls=%fused_computation.231 | convolution fusion | flops 4294967296 | bytes 12582912 | tf_op jit(solution)/shard_map/dot_general | solution.py:933
  225.3 6.1 %fusion.91 = f32[1024,1024]{1,0:T(8,128)} fusion(bf16[1024,2048]{1,0:T(8,128)(2,1)S(1)} %bitcast.403, bf16[1024,2048]{1,0:T(8,128)(2,1)S(1)} %bitcast.399), kind=kOutput, calls=%fused_computation.230 | convolution fusion | flops 4294967296 | bytes 12582912 | tf_op jit(solution)/shard_map/dot_general | solution.py:932
  231.4 14.0 %multiply_convert_fusion.1 = (bf16[1024,1024]{1,0:T(8,128)(2,1)}, bf16[1024,1024]{1,0:T(8,128)(2,1)}, bf16[1024,1024]{1,0:T(8,128)(2,1)S(1)}) fusion(f32[1024,1024]{1,0:T(8,128)} %fusion.91, f32[1024,1024]{1,0:T(8,128)} %fusion.92, bf16[1024,2048]{1,0:T(8,128)(2,1)} %all-gather.2.cloned.1.call-done, bf16[1024,2048]{1,0:T(8,128)(2,1)} %bitcast.407), kind=kOutput, calls=%fused_computation.22 | convolution fusion | flops 4310695936 | bytes 23068672 | tf_op jit(solution)/shard_map/dot_general | solution.py:934
  245.5 1.3 copy-done.50
  246.8 6.2 %convolution_convert_fusion.5 = bf16[1024,2048]{1,0:T(8,128)(2,1)} fusion(bf16[1024,1024]{1,0:T(8,128)(2,1)S(1)} %get-tuple-element.143, bf16[1024,2048]{1,0:T(8,128)(2,1)S(1)} %bitcast.408), kind=kOutput, calls=%fused_computation.34 | convolution fusion | flops 4297064448 | bytes 10485760 | tf_op jit(solution)/shard_map/dot_general | solution.py:940
  253.7 5.3 fusion.4
  259.0 4.5 fusion.93
  263.6 6.3 %convolution_convert_fusion.4 = bf16[1024,2048]{1,0:T(8,128)(2,1)} fusion(bf16[1024,1024]{1,0:T(8,128)(2,1)S(1)} %copy-done.51, bf16[1024,2048]{1,0:T(8,128)(2,1)S(1)} %copy-done.38), kind=kOutput, calls=%fused_computation.33 | convolution fusion | flops 4297064448 | bytes 10485760 | tf_op jit(solution)/shard_map/dot_general | solution.py:946
  269.9 6.1 %add_convert_fusion = bf16[1024,2048]{1,0:T(8,128)(2,1)} fusion(f32[1024,2048]{1,0:T(8,128)S(1)} %fusion.93, bf16[1024,1024]{1,0:T(8,128)(2,1)S(1)} %copy-done.49, bf16[1024,2048]{1,0:T(8,128)(2,1)S(1)} %bitcast.406), kind=kOutput, calls=%fused_computation.9 | convolution fusion | flops 4299161600 | bytes 18874368 | tf_op jit(solution)/shard_map/dot_general | solution.py:951
  276.0 60.4 %move_4.1 = (f32[2,64,2048]{2,1,0:T(8,128)}, f32[2,128,2048]{2,1,0:T(8,128)}) custom-call(bf16[8,2,64,2048]{3,2,1,0:T(8,128)(2,1)} %bitcast.366, bf16[4,2,128,2048]{3,2,1,0:T(8,128)(2,1)} %bitcast.365), custom_call_target="tpu_custom_call" | custom-call | bytes 120000000 | tf_op jit(solution)/shard_map/move_4/pallas_call | solution.py:753
  336.4 1.5 multiply_reduce_fusion.1
  339.3 9.5 %convolution_convert_fusion.2 = bf16[1024,2048]{1,0:T(8,128)(2,1)} fusion(bf16[1024,1024]{1,0:T(8,128)(2,1)} %get-tuple-element.141, bf16[1024,2048]{1,0:T(8,128)(2,1)} %bitcast.402), kind=kOutput, calls=%fused_computation.31 | convolution fusion | flops 4297064448 | bytes 10485760 | tf_op jit(solution)/shard_map/dot_general | solution.py:946
  348.8 6.3 %convolution_convert_fusion.3 = bf16[1024,2048]{1,0:T(8,128)(2,1)} fusion(bf16[1024,1024]{1,0:T(8,128)(2,1)S(1)} %copy-done.48, bf16[1024,2048]{1,0:T(8,128)(2,1)S(1)} %bitcast.404), kind=kOutput, calls=%fused_computation.32 | convolution fusion | flops 4297064448 | bytes 10485760 | tf_op jit(solution)/shard_map/dot_general | solution.py:946
  355.1 3.1 fusion.83
  358.2 46.0 %move_5.1 = (bf16[8,2,64,2048]{3,2,1,0:T(8,128)(2,1)}, f32[2,128,2048]{2,1,0:T(8,128)}) custom-call(bf16[2,64,2048]{2,1,0:T(8,128)(2,1)} %bitcast.374, bf16[4,2,128,2048]{3,2,1,0:T(8,128)(2,1)} %bitcast.361), custom_call_target="tpu_custom_call" | custom-call | bytes 120000000 | tf_op jit(solution)/shard_map/move_5/pallas_call | solution.py:753
  404.2 3.6 convolution_convert_fusion.8
  407.9 2.3 convolution_convert_fusion.7
  411.4 2.5 fusion.7
  414.0 1.3 fusion.9
  416.6 3.8 fusion
  420.4 2.4 fusion.21
  422.8 2.8 fusion.2
  426.5 1.4 fusion.19
  428.7 4.4 convolution_convert_fusion
  433.1 3.6 convolution_convert_fusion.6
  436.7 72.2 %move_6.1 = (bf16[8,64,384]{2,1,0:T(8,128)(2,1)}, f32[2,64,2048]{2,1,0:T(8,128)}, f32[2,32,2048]{2,1,0:T(8,128)}, f32[2,128,2048]{2,1,0:T(8,128)}) custom-call(bf16[4,2,4,64,384]{4,3,2,1,0:T(8,128)(2,1)} %bitcast.377, bf16[8,2,64,2048]{3,2,1,0:T(8,128)(2,1)} %bitcast.364, bf16[4,2,32,2048]{3,2,1,0:T(8,128)(2,1)} %bitcast.388, bf16[4,2,128,2048]{3,2,1,0:T(8,128)(2,1)} %bitcast.363), custom_call_target="tpu_custom_call" | custom-call | bytes 120000000 | tf_op jit(solution)/shard_map/move_6/pallas_call | solution.py:753
  511.8 1.5 fusion.25
  514.2 17.6 %move_7.1 = f32[8,128]{1,0:T(8,128)} custom-call(f32[32,8,128]{2,1,0:T(8,128)} %pad.25.refs_0_), custom_call_target="tpu_custom_call" | custom-call | bytes 120000000 | tf_op jit(solution)/shard_map/move_7/pallas_call | solution.py:753
  531.8 1.3 slice_bitcast_fusion.31
  533.1 1.4 fusion.30
  534.5 2.3 concatenate.102
  536.8 2.0 copy.127
  538.8 1.3 copy.128
  540.2 1.3 copy.129
  541.5 1.3 copy.130
  (190 shorter events, 22.0 us)
Async XLA Ops:
  7.2 224.3 %all-gather.2.cloned.1.call-start = ((), (), s32[]{:S(2)}) async-start(), calls=%async_computation.2 | async-start | bytes 4718592 | tf_op jit(solution)/shard_map/all_gather | solution.py:886
  83.0 272.1 %reduce-scatter.2.cloned.1.call-start = ((), (), s32[]{:S(2)}) async-start(), calls=%async_computation.1 | async-start | bytes 4718592 | tf_op jit(solution)/shard_map/reduce_scatter | solution.py:939
  83.2 11.6 %copy-start.33 = (f32[32]{0:T(128)}, f32[32]{0:T(128)S(1)}, u32[]{:S(2)}) copy-start(f32[32]{0:T(128)S(1)} %multiply_power_fusion) | copy-start | bytes 388
  83.3 11.5 %copy-start.28 = (f32[1024]{0:T(1024)}, f32[1024]{0:T(1024)S(1)}, u32[]{:S(2)}) copy-start(f32[1024]{0:T(1024)S(1)} %iota_convert_fusion) | copy-start | bytes 12292
  87.6 3.7 copy-start.45
  93.2 9.3 %copy-start.31 = (bf16[1024,384]{0,1:T(8,128)(2,1)}, bf16[1024,384]{0,1:T(8,128)(2,1)S(1)}, u32[]{:S(2)}) copy-start(bf16[1024,384]{0,1:T(8,128)(2,1)S(1)} %get-tuple-element.213) | copy-start | bytes 2359300
  94.7 2.9 copy-start.9
  94.7 2.9 copy-start.11
  95.3 2.3 copy-start.18
  95.4 2.3 copy-start.20
  96.2 5.0 copy-start.1
  97.2 4.1 copy-start.26
  99.2 3.4 copy-start
  101.2 3.7 copy-start.24
  102.6 2.5 copy-start.16
  105.0 61.4 %copy-start.7 = (bf16[1024,4,64]{0,2,1:T(8,128)(2,1)}, bf16[1024,4,64]{0,2,1:T(8,128)(2,1)S(1)}, u32[]{:S(2)}) copy-start(bf16[1024,4,64]{0,2,1:T(8,128)(2,1)S(1)} %pad_maximum_fusion.2) | copy-start | bytes 1572868
  108.3 58.2 %copy-start.3 = (bf16[1,128,2048]{2,1,0:T(8,128)(2,1)S(1)}, bf16[1,128,2048]{2,1,0:T(8,128)(2,1)}, u32[]{:S(2)}) copy-start(bf16[1,128,2048]{2,1,0:T(8,128)(2,1)} %param.25) | copy-start | bytes 1572868
  166.5 50.3 %copy-start.41 = (bf16[4,2,128,2048]{3,2,1,0:T(8,128)(2,1)S(1)}, bf16[4,2,128,2048]{3,2,1,0:T(8,128)(2,1)}, u32[]{:S(2)}) copy-start(bf16[4,2,128,2048]{3,2,1,0:T(8,128)(2,1)} %get-tuple-element.122) | copy-start | bytes 12582916
  216.8 8.6 %copy-start.36 = (bf16[4,2,128,2048]{3,2,1,0:T(8,128)(2,1)S(1)}, bf16[4,2,128,2048]{3,2,1,0:T(8,128)(2,1)}, u32[]{:S(2)}) copy-start(bf16[4,2,128,2048]{3,2,1,0:T(8,128)(2,1)} %get-tuple-element.121) | copy-start | bytes 12582916
  216.8 8.5 %copy-start.39 = (bf16[8,2,64,2048]{3,2,1,0:T(8,128)(2,1)S(1)}, bf16[8,2,64,2048]{3,2,1,0:T(8,128)(2,1)}, u32[]{:S(2)}) copy-start(bf16[8,2,64,2048]{3,2,1,0:T(8,128)(2,1)} %get-tuple-element.120) | copy-start | bytes 12582916
  231.4 15.4 %copy-start.43 = (bf16[4,2,128,2048]{3,2,1,0:T(8,128)(2,1)S(1)}, bf16[4,2,128,2048]{3,2,1,0:T(8,128)(2,1)}, u32[]{:S(2)}) copy-start(bf16[4,2,128,2048]{3,2,1,0:T(8,128)(2,1)} %get-tuple-element.123) | copy-start | bytes 12582916
  253.2 5.8 %copy-start.35 = (f32[128]{0:T(128)}, f32[128]{0:T(128)S(1)}, u32[]{:S(2)}) copy-start(f32[128]{0:T(128)S(1)} %rsqrt.44) | copy-start | bytes 1540
  253.7 5.3 copy-start.37
  253.7 5.3 copy-start.47
  259.0 4.5 copy-start.38
  259.0 4.5 copy-start.51
  263.5 6.3 %copy-start.42 = (bf16[4,2,128,2048]{3,2,1,0:T(8,128)(2,1)S(1)}, bf16[4,2,128,2048]{3,2,1,0:T(8,128)(2,1)}, u32[]{:S(2)}) copy-start(bf16[4,2,128,2048]{3,2,1,0:T(8,128)(2,1)} %get-tuple-element.122) | copy-start | bytes 12582916
  263.6 6.3 %copy-start.49 = (bf16[1024,1024]{1,0:T(8,128)(2,1)S(1)}, bf16[1024,1024]{1,0:T(8,128)(2,1)}, u32[]{:S(2)}) copy-start(bf16[1024,1024]{1,0:T(8,128)(2,1)} %get-tuple-element.141) | copy-start | bytes 6291460
  276.0 60.4 %copy-start.4 = (f32[2,64,2048]{2,1,0:T(8,128)S(1)}, f32[2,64,2048]{2,1,0:T(8,128)}, u32[]{:S(2)}) copy-start(f32[2,64,2048]{2,1,0:T(8,128)} %get-tuple-element.119) | copy-start | bytes 3145732
  339.2 9.5 %copy-start.40 = (bf16[8,2,64,2048]{3,2,1,0:T(8,128)(2,1)S(1)}, bf16[8,2,64,2048]{3,2,1,0:T(8,128)(2,1)}, u32[]{:S(2)}) copy-start(bf16[8,2,64,2048]{3,2,1,0:T(8,128)(2,1)} %get-tuple-element.120) | copy-start | bytes 12582916
  339.3 9.5 %copy-start.48 = (bf16[1024,1024]{1,0:T(8,128)(2,1)S(1)}, bf16[1024,1024]{1,0:T(8,128)(2,1)}, u32[]{:S(2)}) copy-start(bf16[1024,1024]{1,0:T(8,128)(2,1)} %get-tuple-element.142) | copy-start | bytes 6291460
  355.1 49.1 %copy-start.17 = (bf16[4,2,32,2048]{3,2,1,0:T(8,128)(2,1)S(1)}, bf16[4,2,32,2048]{3,2,1,0:T(8,128)(2,1)}, u32[]{:S(2)}) copy-start(bf16[4,2,32,2048]{3,2,1,0:T(8,128)(2,1)} %get-tuple-element.118) | copy-start | bytes 3145732
  404.2 3.7 copy-start.8
  404.2 3.7 copy-start.44
  407.9 2.3 copy-start.2
  407.9 2.3 copy-start.27
  411.4 5.1 slice-start
  414.0 2.1 copy-start.19
  414.0 2.1 copy-start.21
  414.0 2.6 slice-start.1
  426.4 2.0 copy-start.22
  426.5 2.2 copy-start.46
  428.7 4.4 copy-start.6
  508.9 4.6 copy-start.30
  508.9 24.2 %copy-start.5 = (f32[2,64,2048]{2,1,0:T(8,128)S(1)}, f32[2,64,2048]{2,1,0:T(8,128)}, u32[]{:S(2)}) copy-start(f32[2,64,2048]{2,1,0:T(8,128)} %get-tuple-element.127) | copy-start | bytes 3145732
  534.5 4.4 copy-start.14
  536.8 3.4 copy-start.15
  538.8 2.6 copy-start.13
  (8 other events, 9.5 us)
Sparse Core Ops, SparseCore 0:
  83.1 48.6 all-gather.1
  253.1 63.0 reduce-scatter.1

commit v2 on v1

--- a/solution.py
+++ b/solution.py
@@ -88,6 +88,92 @@
 DMA = pltpu.SemaphoreType.DMA
 
 
+def line_gather(place, x_ref, out_ref, own_sem, us, ur, ds, dr, ps, pr):
+    s, chip, chips = place.s, place.chip, place.chips
+
+    def copy(src, group, half, sends, recvs, at, target):
+        return remote(
+            src, out_ref.at[group, half], sends.at[at, half], recvs.at[at, half], seq=target
+        )
+
+    def up(src, group, hop, half):
+        return copy(src, group, half, us, ur, hop, s + 2)
+
+    def down(src, group, hop, half):
+        return copy(src, group, half, ds, dr, hop, s - 2)
+
+    def pair(src, group, half):
+        return copy(src, group, half, ps, pr, group // 2, place.partner)
+
+    own = pltpu.make_async_copy(x_ref, out_ref.at[s], own_sem)
+
+    def start():
+        own.start()
+        for half in range(SUB):
+
+            @pl.when(chip < chips - 1)
+            def _():
+                up(x_ref.at[half], s, 0, half).start()
+
+            @pl.when(chip > 0)
+            def _():
+                down(x_ref.at[half], s, 0, half).start()
+
+        for half in range(SUB):
+            pair(x_ref.at[half], s, half).start()
+
+    def step(hop, half):
+        below, above = s - 2 * hop, s + 2 * hop
+
+        @pl.when(chip - hop >= 0)
+        def _():
+            block = out_ref.at[below, half]
+            up(block, below, hop - 1, half).wait_recv()
+
+            @pl.when(chip < chips - 1)
+            def _():
+                up(block, below, hop, half).start()
+
+            pair(block, below, half).start()
+
+        @pl.when(chip + hop < chips)
+        def _():
+            block = out_ref.at[above, half]
+            down(block, above, hop - 1, half).wait_recv()
+
+            @pl.when(chip > 0)
+            def _():
+                down(block, above, hop, half).start()
+
+            pair(block, above, half).start()
+
+    def arrived(at):
+        for half in range(SUB):
+            group = 2 * at + 1 - place.core
+            pair(out_ref.at[group, half], group, half).wait_recv()
+
+    def sent():
+        def each(i, _):
+            k, half = i // SUB, i % SUB
+            mine = 2 * k + place.core
+            block = out_ref.at[mine, half]
+            pair(block, mine, half).wait_send()
+
+            @pl.when(jnp.logical_and(chip - k >= 0, chip < chips - 1))
+            def _():
+                up(block, mine, k, half).wait_send()
+
+            @pl.when(jnp.logical_and(chip + k < chips, chip > 0))
+            def _():
+                down(block, mine, k, half).wait_send()
+
+            return 0
+
+        lax.fori_loop(0, chips * SUB, each, 0)
+
+    return own, start, step, arrived, sent
+
+
 class LineGather:
     def __init__(self, x, dps, groups):
         rows, width = x.shape
@@ -97,218 +183,161 @@
         self.scratch = [DMA] + [DMA((groups // 2, SUB))] * 6
         self.result = lambda out: out.reshape(groups * rows, width)
 
-    def bind(self, place, x_ref, out_ref, own_sem, us, ur, ds, dr, ps, pr):
-        s, chip, chips = place.s, place.chip, place.chips
-
-        def copy(src, group, half, sends, recvs, at, target):
-            return remote(
-                src, out_ref.at[group, half], sends.at[at, half], recvs.at[at, half], seq=target
-            )
-
-        def up(src, group, hop, half):
-            return copy(src, group, half, us, ur, hop, s + 2)
-
-        def down(src, group, hop, half):
-            return copy(src, group, half, ds, dr, hop, s - 2)
-
-        def pair(src, group, half):
-            return copy(src, group, half, ps, pr, group // 2, place.partner)
-
-        own = pltpu.make_async_copy(x_ref, out_ref.at[s], own_sem)
-
-        def start():
-            own.start()
-            for half in range(SUB):
-
-                @pl.when(chip < chips - 1)
-                def _():
-                    up(x_ref.at[half], s, 0, half).start()
-
-                @pl.when(chip > 0)
-                def _():
-                    down(x_ref.at[half], s, 0, half).start()
-
-            for half in range(SUB):
-                pair(x_ref.at[half], s, half).start()
-
-        def step(hop, half):
-            below, above = s - 2 * hop, s + 2 * hop
-
-            @pl.when(chip - hop >= 0)
-            def _():
-                block = out_ref.at[below, half]
-                up(block, below, hop - 1, half).wait_recv()
-
-                @pl.when(chip < chips - 1)
-                def _():
-                    up(block, below, hop, half).start()
-
-                pair(block, below, half).start()
-
-            @pl.when(chip + hop < chips)
-            def _():
-                block = out_ref.at[above, half]
-                down(block, above, hop - 1, half).wait_recv()
-
-                @pl.when(chip > 0)
-                def _():
-                    down(block, above, hop, half).start()
-
-                pair(block, above, half).start()
+    def bind(self, place, *refs):
+        own, start, step, arrived, sent = line_gather(place, *refs)
 
         def finish():
             own.wait()
 
-            def each(i, _):
-                k, half = i // SUB, i % SUB
-                mine, other = 2 * k + place.core, 2 * k + 1 - place.core
-                block = out_ref.at[mine, half]
-                pair(block, other, half).wait_recv()
-                pair(block, mine, half).wait_send()
-
-                @pl.when(jnp.logical_and(chip - k >= 0, chip < chips - 1))
-                def _():
-                    up(block, mine, k, half).wait_send()
-
-                @pl.when(jnp.logical_and(chip + k < chips, chip > 0))
-                def _():
-                    down(block, mine, k, half).wait_send()
-
+            def each(at, _):
+                arrived(at)
                 return 0
 
-            lax.fori_loop(0, chips * SUB, each, 0)
+            lax.fori_loop(0, place.chips, each, 0)
+            sent()
 
         ticks = {
             (hop - 1) * SUB + half: functools.partial(step, hop, half)
-            for hop in range(1, chips)
+            for hop in range(1, place.chips)
             for half in range(SUB)
         }
         return start, ticks, finish
 
 
+def line_scatter(place, p_ref, out_ref, pairbuf, upbuf, downbuf, us, ur, ds, dr, ps, pr):
+    s, chip, chips, core = place.s, place.chip, place.chips, place.core
+
+    def copy(src, buffer, at, half, sends, recvs, target):
+        return remote(src, buffer.at[at, half], sends.at[at, half], recvs.at[at, half], seq=target)
+
+    def pair(at, half):
+        src = p_ref.at[2 * at + 1 - core, half]
+        return copy(src, pairbuf, at, half, ps, pr, place.partner)
+
+    def up(at, half):
+        return copy(upbuf.at[at, half], upbuf, at, half, us, ur, s + 2)
+
+    def down(at, half):
+        return copy(downbuf.at[at, half], downbuf, at, half, ds, dr, s - 2)
+
+    def wide(ref, *at):
+        return ref[at].astype(jnp.float32)
+
+    def local(at, half):
+        return wide(p_ref, 2 * at + core, half) + wide(pairbuf, at, half)
+
+    def send(at):
+        for half in range(SUB):
+            pair(at, half).start()
+
+    def step(low, half):
+        high = chips - 1 - low
+
+        @pl.when(high > chip)
+        def _():
+            pair(high, half).wait_recv()
+
+            @pl.when(chip > 0)
+            def _():
+                up(high, half).wait_recv()
+                total = local(high, half) + wide(upbuf, high, half)
+                upbuf[high, half] = total.astype(jnp.bfloat16)
+
+            @pl.when(chip == 0)
+            def _():
+                upbuf[high, half] = local(high, half).astype(jnp.bfloat16)
+
+            up(high, half).start()
+
+        @pl.when(low < chip)
+        def _():
+            pair(low, half).wait_recv()
+
+            @pl.when(chip < chips - 1)
+            def _():
+                down(low, half).wait_recv()
+                total = local(low, half) + wide(downbuf, low, half)
+                downbuf[low, half] = total.astype(jnp.bfloat16)
+
+            @pl.when(chip == chips - 1)
+            def _():
+                downbuf[low, half] = local(low, half).astype(jnp.bfloat16)
+
+            down(low, half).start()
+
+    def finish():
+        for half in range(SUB):
+            pair(chip, half).wait_recv()
+            out_ref[half] = local(chip, half)
+
+            @pl.when(chip > 0)
+            def _():
+                up(chip, half).wait_recv()
+                out_ref[half] += wide(upbuf, chip, half)
+
+            @pl.when(chip < chips - 1)
+            def _():
+                down(chip, half).wait_recv()
+                out_ref[half] += wide(downbuf, chip, half)
+
+        def each(i, _):
+            at, half = i // SUB, i % SUB
+            pair(at, half).wait_send()
+
+            @pl.when(at > chip)
+            def _():
+                up(at, half).wait_send()
+
+            @pl.when(at < chip)
+            def _():
+                down(at, half).wait_send()
+
+            return 0
+
+        lax.fori_loop(0, chips * SUB, each, 0)
+
+    return send, step, finish
+
+
+def line_scatter_scratch(chips, shape):
+    return [pltpu.VMEM((chips,) + shape, jnp.bfloat16)] * 3 + [DMA((chips, SUB))] * 6
+
+
 class LineScatter:
     def __init__(self, partial, dps, groups):
         total, width = partial.shape
-        rows, chips = total // groups, groups // 2
+        rows = total // groups
         shape = (SUB, rows // SUB, width)
         self.inputs, self.in_specs = [partial.reshape((groups,) + shape)], [VM]
         self.outs, self.out_specs = [jax.ShapeDtypeStruct(shape, jnp.float32)], [VM]
-        self.scratch = [pltpu.VMEM((chips,) + shape, jnp.bfloat16)] * 5 + [DMA((chips, SUB))] * 6
+        self.scratch = line_scatter_scratch(groups // 2, shape)
         self.result = lambda out: out.reshape(rows, width)
 
-    def bind(
-        self, place, p_ref, out_ref, pairbuf, upbuf, downbuf, usend, dsend, us, ur, ds, dr, ps, pr
-    ):
-        s, chip, chips, core = place.s, place.chip, place.chips, place.core
-
-        def copy(src, buffer, at, half, sends, recvs, target):
-            return remote(
-                src, buffer.at[at, half], sends.at[at, half], recvs.at[at, half], seq=target
-            )
-
-        def pair(at, half):
-            src = p_ref.at[2 * at + 1 - core, half]
-            return copy(src, pairbuf, at, half, ps, pr, place.partner)
-
-        def up(at, half):
-            return copy(usend.at[at, half], upbuf, at, half, us, ur, s + 2)
-
-        def down(at, half):
-            return copy(dsend.at[at, half], downbuf, at, half, ds, dr, s - 2)
-
-        def wide(ref, *at):
-            return ref[at].astype(jnp.float32)
-
-        def local(at, half):
-            return wide(p_ref, 2 * at + core, half) + wide(pairbuf, at, half)
+    def bind(self, place, *refs):
+        send, step, finish = line_scatter(place, *refs)
+        chip, chips = place.chip, place.chips
 
         def start():
-            def issue(i, _):
-                low, half = i // SUB, i % SUB
+            def issue(low, _):
                 high = chips - 1 - low
 
                 @pl.when(high > chip)
                 def _():
-                    pair(high, half).start()
+                    send(high)
 
                 @pl.when(low < chip)
                 def _():
-                    pair(low, half).start()
+                    send(low)
 
                 return 0
 
-            lax.fori_loop(0, (chips - 1) * SUB, issue, 0)
-            for half in range(SUB):
-                pair(chip, half).start()
-
-        def step(i):
-            low, half = i // SUB, i % SUB
-            high = chips - 1 - low
-
-            @pl.when(high > chip)
-            def _():
-                pair(high, half).wait_recv()
-
-                @pl.when(chip > 0)
-                def _():
-                    up(high, half).wait_recv()
-                    total = local(high, half) + wide(upbuf, high, half)
-                    usend[high, half] = total.astype(jnp.bfloat16)
-
-                @pl.when(chip == 0)
-                def _():
-                    usend[high, half] = local(high, half).astype(jnp.bfloat16)
-
-                up(high, half).start()
-
-            @pl.when(low < chip)
-            def _():
-                pair(low, half).wait_recv()
-
-                @pl.when(chip < chips - 1)
-                def _():
-                    down(low, half).wait_recv()
-                    total = local(low, half) + wide(downbuf, low, half)
-                    dsend[low, half] = total.astype(jnp.bfloat16)
-
-                @pl.when(chip == chips - 1)
-                def _():
-                    dsend[low, half] = local(low, half).astype(jnp.bfloat16)
-
-                down(low, half).start()
-
-        def finish():
-            for half in range(SUB):
-                pair(chip, half).wait_recv()
-                out_ref[half] = local(chip, half)
-
-                @pl.when(chip > 0)
-                def _():
-                    up(chip, half).wait_recv()
-                    out_ref[half] += wide(upbuf, chip, half)
-
-                @pl.when(chip < chips - 1)
-                def _():
-                    down(chip, half).wait_recv()
-                    out_ref[half] += wide(downbuf, chip, half)
-
-            def each(i, _):
-                at, half = i // SUB, i % SUB
-                pair(at, half).wait_send()
-
-                @pl.when(at > chip)
-                def _():
-                    up(at, half).wait_send()
-
-                @pl.when(at < chip)
-                def _():
-                    down(at, half).wait_send()
-
-                return 0
-
-            lax.fori_loop(0, chips * SUB, each, 0)
-
-        return start, {i: functools.partial(step, i) for i in range((chips - 1) * SUB)}, finish
+            lax.fori_loop(0, chips - 1, issue, 0)
+            send(chip)
+
+        ticks = {
+            i: functools.partial(step, i // SUB, i % SUB) for i in range((chips - 1) * SUB)
+        }
+        return start, ticks, finish
 
 
 def ring_sems(hops):
@@ -383,11 +412,17 @@
             dp=place.ring(-1),
         )
 
-    def start():
+    def start_far():
         right(part(place.ring(hops), 0), hops, 0).start()
         left(part(place.ring(-hops), 1), hops, 1).start()
+
+    def start_next():
         right(part(place.ring(hops - 1), 1), hops - 1, 1).start()
         left(part(place.ring(1 - hops), 0), hops - 1, 0).start()
+
+    def start():
+        start_far()
+        start_next()
 
     def forward(hop):
         for first in range(2 if hop < hops - 1 else 1):
@@ -417,7 +452,7 @@
                 if hop < hops or half == 1:
                     left(lbuf.at[0, half], hop, half).wait_send()
 
-    return start, forward, finish
+    return start, forward, finish, start_far, start_next
 
 
 class RingGather:
@@ -723,6 +758,358 @@
             out_ref[...] = jnp.sum(landing[...], axis=0) if self.total else landing[...]
 
         return start, {}, finish
+
+
+TILE = 256
+
+
+class FeedForward:
+    def __init__(self, normed, down, gate, up, grad_all, dps, groups):
+        rows, width = normed.shape
+        shape, chips = (SUB, rows // SUB, width), groups // 2
+        held = gate.shape[0]
+        ring = (2, down.shape[0] // 2, width)
+        pair = 2 * rows
+        self.inputs = [
+            normed.reshape(shape),
+            down.reshape(ring),
+            gate,
+            up,
+            grad_all.reshape(chips, pair, width),
+        ]
+        self.in_specs = [VM, VM, ANY, ANY, ANY]
+        act = jax.ShapeDtypeStruct((chips, pair, held), jnp.bfloat16)
+        self.outs = [
+            jax.ShapeDtypeStruct((groups,) + shape, jnp.bfloat16),
+            jax.ShapeDtypeStruct((dps,) + ring, jnp.bfloat16),
+            act,
+            act,
+            act,
+        ]
+        self.out_specs = [VM] * 5
+        self.scratch = [
+            pltpu.VMEM((held, width), jnp.bfloat16),
+            pltpu.VMEM((held, width), jnp.bfloat16),
+            pltpu.VMEM((chips, pair, width), jnp.bfloat16),
+            pltpu.VMEM((chips, pair, held), jnp.float32),
+            pltpu.VMEM((chips, pair, held), jnp.float32),
+            DMA((4,)),
+            DMA,
+        ]
+        self.scratch += [DMA((chips, SUB))] * 6 + ring_sems(dps // 2)
+        self.result = lambda hn, full, *acts: (
+            hn.reshape(groups * rows, width),
+            full.reshape(held, width),
+            *[one.reshape(groups * rows, held) for one in acts],
+        )
+
+    def bind(self, place, x_ref, shard, gate_at, up_at, grad_at, *refs):
+        hn, full, inner, dgate, dup, gate_w, up_w, grads, slope, silu = refs[:10]
+        loads, own_line = refs[10:12]
+        line_sems, ring_refs = refs[12:18], refs[18:]
+        chip, chips = place.chip, place.chips
+        pair, held = inner.shape[1:]
+        width = gate_w.shape[1]
+        own, start_line, step, arrived, sent = line_gather(place, x_ref, hn, own_line, *line_sems)
+        ring = ring_gather(
+            place,
+            lambda half: shard.at[half],
+            lambda chunk, half: full.at[chunk, half],
+            *ring_refs,
+        )
+        copies = [
+            pltpu.make_async_copy(gate_at, gate_w, loads.at[0]),
+            pltpu.make_async_copy(up_at, up_w, loads.at[1]),
+            pltpu.make_async_copy(grad_at, grads, loads.at[2]),
+            pltpu.make_async_copy(shard, full.at[place.d], loads.at[3]),
+        ]
+        wide = 512 if held % 512 == 0 else held
+
+        def start():
+            start_line()
+            ring[0]()
+            for one in copies:
+                one.start()
+
+        def forward(at):
+            rows = hn[pl.ds(2 * at, 2)].reshape(pair, width)
+            for first in range(0, held, wide):
+                span = slice(first, first + wide)
+                gate = lax.dot_general(
+                    rows, gate_w[span, :], contract_cols, preferred_element_type=jnp.float32
+                )
+                upward = lax.dot_general(
+                    rows, up_w[span, :], contract_cols, preferred_element_type=jnp.float32
+                )
+                sigmoid = jax.nn.sigmoid(gate)
+                passed = gate * sigmoid
+                inner[at, :, span] = (passed * upward).astype(jnp.bfloat16)
+                silu[at, :, span] = passed
+                slope[at, :, span] = upward * sigmoid * (1.0 + gate * (1.0 - sigmoid))
+
+        def when_there(at, there):
+            @pl.when(there)
+            def _():
+                arrived(at)
+                forward(at)
+
+        def tick(hop, half):
+            step(hop, half)
+            if hop == 1 and half == 0:
+                own.wait()
+                copies[0].wait()
+                copies[1].wait()
+                arrived(chip)
+                forward(chip)
+            if hop > 1 and half == 0:
+                when_there(chip - hop + 1, chip - hop + 1 >= 0)
+            if hop > 1 and half == SUB - 1:
+                when_there(chip + hop - 1, chip + hop - 1 < chips)
+
+        def finish():
+            last = chips - 1
+            when_there(chip - last, chip - last >= 0)
+            when_there(chip + last, chip + last < chips)
+            copies[2].wait()
+            copies[3].wait()
+            ring[2]()
+
+            def back(at, _):
+                rows = grads[at]
+                for first in range(0, held, wide):
+                    span = slice(first, first + wide)
+                    chunk = full.shape[1] * full.shape[2]
+                    part = full[first // chunk : (first + wide) // chunk].reshape(wide, width)
+                    grad = lax.dot_general(
+                        rows, part, contract_cols, preferred_element_type=jnp.float32
+                    )
+                    dgate[at, :, span] = (grad * slope[at, :, span]).astype(jnp.bfloat16)
+                    dup[at, :, span] = (grad * silu[at, :, span]).astype(jnp.bfloat16)
+                return 0
+
+            lax.fori_loop(0, chips, back, 0)
+            sent()
+
+        ticks = {
+            (hop - 1) * SUB + half: functools.partial(tick, hop, half)
+            for hop in range(1, chips)
+            for half in range(SUB)
+        }
+
+        def with_ring(tick, hop):
+            ticks[tick]()
+            ring[1](hop)
+
+        merged = dict(ticks)
+        for hop in range(1, place.hops):
+            merged[2 * hop - 1] = functools.partial(with_ring, 2 * hop - 1, hop)
+        return start, merged, finish
+
+
+class FeedBack:
+    def __init__(self, inner, dgate, dup, gate, up, down, normed, grads, dps, groups):
+        length, held = inner.shape
+        width, chips = normed.shape[1], groups // 2
+        rows = length // groups
+        shape = (SUB, rows // SUB, width)
+        owned = (2, held // dps // 2, width)
+        hops = dps // 2
+        tile = (2, SUB, rows // SUB, width)
+        self.inputs = [inner, dgate, dup, gate, up, down, normed, grads]
+        self.in_specs = [ANY] * 8
+        self.outs = [
+            jax.ShapeDtypeStruct(shape, jnp.float32),
+            jax.ShapeDtypeStruct(owned, jnp.float32),
+            jax.ShapeDtypeStruct((held // TILE,) + tile, jnp.bfloat16),
+            jax.ShapeDtypeStruct((held // TILE,) + tile, jnp.bfloat16),
+            jax.ShapeDtypeStruct((chips,) + tile, jnp.bfloat16),
+        ]
+        self.out_specs = [VM, VM, ANY, ANY, ANY]
+        act = pltpu.VMEM((length, held), jnp.bfloat16)
+        weight = pltpu.VMEM((held, width), jnp.bfloat16)
+        tokens = pltpu.VMEM((length, width), jnp.bfloat16)
+        self.scratch = [act] * 3 + [weight] * 2 + [tokens] * 2
+        self.scratch += [
+            pltpu.VMEM((groups,) + shape, jnp.bfloat16),
+            pltpu.VMEM((dps,) + owned, jnp.bfloat16),
+            pltpu.VMEM((2,) + tile, jnp.bfloat16),
+            DMA((8,)),
+            DMA((2,)),
+        ]
+        self.scratch += line_scatter_scratch(chips, shape)
+        self.scratch += (
+            [pltpu.VMEM((hops,) + owned, jnp.bfloat16)] * 2
+            + [pltpu.VMEM((hops - 1,) + owned, jnp.bfloat16)] * 2
+            + ring_sems(hops)
+        )
+        self.result = lambda total, mine, gate_term, up_term, out: (
+            total.reshape(rows, width),
+            mine.reshape(held // dps, width),
+            gate_term.reshape(held, width),
+            up_term.reshape(held, width),
+            out.reshape(length, width),
+        )
+
+    def bind(self, place, *refs):
+        sources, refs = refs[:8], refs[8:]
+        total_ref, own_ref, gate_out, up_out, result_out = refs[:5]
+        inner, dgate, dup, gate, up, normed, grads = refs[5:12]
+        p_ref, term, stage, loads, stage_sem = refs[12:17]
+        line_refs, ring_refs = refs[17:26], refs[26:]
+        chip, chips, hops = place.chip, place.chips, place.hops
+        held, width = gate.shape
+        pair = inner.shape[0] // chips
+        chunk = held // place.dps
+        wide = 1024 if width % 1024 == 0 else width
+        send, step, finish_line = line_scatter(place, p_ref, total_ref, *line_refs)
+
+        def put(half, value):
+            own_ref[half] = value
+
+        ring = ring_scatter(place, lambda at, half: term.at[at, half], put, *ring_refs)
+        targets = [inner, dgate, dup, gate, up, gate, normed, grads]
+        copies = [
+            pltpu.make_async_copy(source, target, loads.at[i])
+            for i, (source, target) in enumerate(zip(sources, targets))
+        ]
+
+        def start():
+            for i in (0, 7, 1, 3, 2, 4, 6):
+                copies[i].start()
+
+        def rows_of(ref, at):
+            return ref[pl.ds(pl.multiple_of(at * pair, pair), pair), :]
+
+        def partial(at):
+            left, right = rows_of(dgate, at), rows_of(dup, at)
+            for first in range(0, width, wide):
+                span = slice(first, first + wide)
+                value = jnp.dot(left, gate[:, span], preferred_element_type=jnp.float32)
+                value += jnp.dot(right, up[:, span], preferred_element_type=jnp.float32)
+                p_ref[pl.ds(2 * at, 2), :, :, span] = value.astype(jnp.bfloat16).reshape(
+                    p_ref[pl.ds(2 * at, 2), :, :, span].shape
+                )
+            send(at)
+
+        def term_rows(ref, other, start, count, span):
+            return lax.dot_general(
+                ref[:, pl.ds(start, count)],
+                other[:, span],
+                contract_rows,
+                preferred_element_type=jnp.float32,
+            ).astype(jnp.bfloat16)
+
+        def down_tile(at):
+            if chunk % 128 == 0:
+                for first in range(0, width, wide):
+                    span = slice(first, first + wide)
+                    value = term_rows(inner, grads, pl.multiple_of(at * chunk, chunk), chunk, span)
+                    term[at, :, :, span] = value.reshape(2, chunk // 2, wide)
+
+        def down_all():
+            if chunk % 128 != 0:
+                for row in range(0, held, TILE):
+                    for first in range(0, width, wide):
+                        span = slice(first, first + wide)
+                        value = term_rows(inner, grads, row, TILE, span)
+                        term[row // chunk : (row + TILE) // chunk, :, :, span] = value.reshape(
+                            TILE // chunk, 2, chunk // 2, wide
+                        )
+
+        jobs = []
+
+        def first_job():
+            copies[0].wait()
+            copies[7].wait()
+            down_all()
+            down_tile(place.ring(hops))
+            ring[3]()
+
+        def next_job(hop):
+            down_tile(place.ring(hop))
+            down_tile(place.ring(-hop))
+            if hop == hops - 1:
+                ring[4]()
+
+        first_job_at = first_job
+        for hop in range(hops - 1, 0, -1):
+            jobs.append(functools.partial(next_job, hop))
+            jobs.append(functools.partial(ring[1], hop))
+        jobs.append(lambda: down_tile(place.d))
+
+        count = [0]
+        waits = []
+
+        def staged(value_of, target):
+            slot = count[0] % 2
+            if count[0] >= 2:
+                waits[count[0] - 2].wait()
+            value_of(stage.at[slot])
+            copy = pltpu.make_async_copy(stage.at[slot], target, stage_sem.at[slot])
+            copy.start()
+            waits.append(copy)
+            count[0] += 1
+
+        def weight_tile(ref, row, out):
+            def fill(slot):
+                for first in range(0, width, wide):
+                    span = slice(first, first + wide)
+                    value = term_rows(ref, normed, row, TILE, span)
+                    slot[:, :, :, span] = value.reshape(slot.shape[:3] + (wide,))
+
+            staged(fill, out.at[row // TILE])
+
+        def result_tile(at):
+            def fill(slot):
+                left = rows_of(inner, at)
+                for first in range(0, width, wide):
+                    span = slice(first, first + wide)
+                    value = jnp.dot(left, gate[:, span], preferred_element_type=jnp.float32)
+                    slot[:, :, :, span] = value.astype(jnp.bfloat16).reshape(
+                        slot.shape[:3] + (wide,)
+                    )
+
+            staged(fill, result_out.at[at])
+
+        def sequence():
+            first_job_at()
+            for i in (1, 3, 2, 4):
+                copies[i].wait()
+            for low in range(chips - 1):
+                high = chips - 1 - low
+
+                @pl.when(high > chip)
+                def _():
+                    partial(high)
+
+                @pl.when(low < chip)
+                def _():
+                    partial(low)
+
+                if jobs:
+                    jobs.pop(0)()
+                for half in range(SUB):
+                    step(low, half)
+            partial(chip)
+            for job in jobs:
+                job()
+            copies[5].start()
+            copies[6].wait()
+            for row in range(0, held, TILE):
+                weight_tile(dgate, row, gate_out)
+            for row in range(0, held, TILE):
+                weight_tile(dup, row, up_out)
+            copies[5].wait()
+            for at in range(chips):
+                result_tile(at)
+
+        def finish():
+            ring[2]()
+            finish_line()
+            for copy in waits[-2:]:
+                copy.wait()
+
+        return start, {0: sequence}, finish
 
 
 def move(parts, dps, groups, number, greet=greet_near):
@@ -757,14 +1144,15 @@
         out_specs=[spec for part in parts for spec in part.out_specs],
         scratch_shapes=[one for part in parts for one in part.scratch],
         compiler_params=pltpu.CompilerParams(
-            collective_id=number, has_side_effects=True, vmem_limit_bytes=56 << 20
+            collective_id=number, has_side_effects=True, vmem_limit_bytes=63 << 20
         ),
         cost_estimate=pl.CostEstimate(flops=0, bytes_accessed=120_000_000, transcendentals=0),
         name=f"move_{number}",
     )(*[x for part in parts for x in part.inputs])
-    results = []
+    results, at = [], 0
     for part in parts:
-        results.append(part.result(outs[len(results)]))
+        results.append(part.result(*outs[at : at + len(part.outs)]))
+        at += len(part.outs)
     return results
 
 
@@ -796,13 +1184,6 @@
         ],
         axis=-1,
     )
-
-
-def gated_grad(gate, upward, grad_inner):
-    sigmoid_gate = jax.nn.sigmoid(gate)
-    grad_gate = grad_inner * upward * sigmoid_gate * (1.0 + gate * (1.0 - sigmoid_gate))
-    grad_upward = grad_inner * (gate * sigmoid_gate)
-    return (grad_gate.astype(jnp.bfloat16), grad_upward.astype(jnp.bfloat16))
 
 
 def block_scores(query_block, key_heads, lower, upper, score_scale):
@@ -922,46 +1303,31 @@
     hidden = x_rows + summed
     factor_two = norm_factor(hidden)
     normed_two = (hidden * factor_two * gain_two).astype(jnp.bfloat16)
-    hn_all, down_part = move(
-        [LineGather(normed_two, dps, groups), RingGather(down_weight, dps, groups)],
+    ((hn_all, down_part, inner, grad_gate, grad_upward),) = move(
+        [FeedForward(normed_two, down_weight, gate_part, up_part, grad_all, dps, groups)],
         dps,
         groups,
         3,
     )
-
-    gate = lax.dot_general(hn_all, gate_part, contract_cols, preferred_element_type=jnp.float32)
-    upward = lax.dot_general(hn_all, up_part, contract_cols, preferred_element_type=jnp.float32)
-    grad_inner = lax.dot_general(
-        grad_all, down_part, contract_cols, preferred_element_type=jnp.float32
-    )
-    inner = (jax.nn.silu(gate) * upward).astype(jnp.bfloat16)
-    grad_gate, grad_upward = gated_grad(gate, upward, grad_inner)
-    mlp_result = lax.psum_scatter(
-        jnp.dot(inner, down_part, preferred_element_type=jnp.float32).astype(jnp.bfloat16),
-        "seq",
-        scatter_dimension=0,
-        tiled=True,
-    ).astype(jnp.float32)
-    down_term, gate_term, up_term = [
-        lax.dot_general(left, right, contract_rows, preferred_element_type=jnp.float32).astype(
-            jnp.bfloat16
-        )
-        for left, right in ((inner, grad_all), (grad_gate, hn_all), (grad_upward, hn_all))
-    ]
-    partial = jnp.dot(grad_gate, gate_part, preferred_element_type=jnp.float32) + jnp.dot(
-        grad_upward, up_part, preferred_element_type=jnp.float32
-    )
-    grad_normed, down_owned = move(
+    ((grad_normed, down_owned, gate_term, up_term, result),) = move(
         [
-            LineScatter(partial.astype(jnp.bfloat16), dps, groups),
-            RingScatter(down_term, dps, groups),
+            FeedBack(
+                inner,
+                grad_gate,
+                grad_upward,
+                gate_part,
+                up_part,
+                down_part,
+                hn_all,
+                grad_all,
+                dps,
+                groups,
+            )
         ],
         dps,
         groups,
         4,
     )
-
-    block_out = (hidden + mlp_result).astype(jnp.bfloat16)[None]
     gain_two_term = jnp.sum(grad_normed * hidden * factor_two, axis=0)
     grad_hidden = grad_low.astype(jnp.float32) + norm_grad(
         hidden, factor_two, gain_two, grad_normed
@@ -975,6 +1341,9 @@
         groups,
         5,
     )
+    result, grad_branch = lax.optimization_barrier((result, grad_branch))
+    mlp_result = lax.psum_scatter(result, "seq", scatter_dimension=0, tiled=True)
+    block_out = (hidden + mlp_result.astype(jnp.float32)).astype(jnp.bfloat16)[None]
     out_term = lax.dot_general(
         attended, grad_branch, contract_rows, preferred_element_type=jnp.float32
     ).astype(jnp.bfloat16)

time: 554 us -> 526 us (0.949)
  matrix products: 106 us -> 39.8 us
  Pallas kernels: 370 us -> 405 us
    dot_general x9 -> x0, matrix products: 67.6 us -> none  [the longest x3 22.2 us: per_device(): lax.dot_general(left, right, contract_rows, preferred_element_type=jnp.fl...]
    pallas_call x7, Pallas kernels: 370 us -> 405 us  [move(): pl.pallas_call(kernel, out_shape=[out for part in parts for out in part.o...]
  transfers between devices with their start and end apart: 2 -> 2, of which waited for: 0 -> 0; matrix products, arithmetic and copies ran while one was open for 15% -> 14% of each run, Pallas kernels for 30% -> 30%
where the time goes in v2:
time: 526 us; the launch traced here: 523 us
  Pallas kernels  405 us (77%)
  other arithmetic  40.1 us (8%)
  matrix products  39.8 us (8%)
  local copies, waits for them, and re-layouts  22 us (4%)
  between operations  15.3 us (3%)
    pallas_call x7, Pallas kernels, move(): pl.pallas_call(kernel, out_shape=[out for part in parts for out in part.o...  405 us
  transfers between devices with their start and end apart: 2, of which 0 were waited for; matrix products, arithmetic and copies ran while one was open for 14% of the time, Pallas kernels for 30%

profile of v2, /device:TPU:0, one launch (start us, length us, event | category | flops | bytes accessed | tf_op | source)
XLA Modules:
  0.0 522.6 jit_solution(10643816445147851308)
XLA Ops:
  7.2 0.9 fusion.85
  8.1 1.0 slice.327
  13.5 69.5 %move_1.1 = (bf16[4,8,64,384]{3,2,1,0:T(8,128)(2,1)}, bf16[8,2,64,2048]{3,2,1,0:T(8,128)(2,1)}, bf16[4,2,32,2048]{3,2,1,0:T(8,128)(2,1)}, bf16[4,2,128,2048]{3,2,1,0:T(8,128)(2,1)}, f32[32,8,128]{2,1,0:T(8,128)}) custom-call(bf16[8,64,384]{2,1,0:T(8,128)(2,1)} %copy-done.23, bf16[2,64,2048]{2,1,0:T(8,128)(2,1)} %bitcast.341, bf16[2,32,2048]{2,1,0:T(8,128)(2,1)} %bitcast.391, ...), custom_call_target="tpu_custom_call" | custom-call | bytes 120000000 | tf_op jit(solution)/shard_map/move_1/pallas_call | solution.py:1140
  83.2 1.1 slice_reduce_fusion.1
  84.3 3.1 multiply_reduce_fusion
  87.5 3.7 multiply_convert_fusion
  91.2 1.9 fusion.89
  95.4 1.2 fusion.65
  96.8 0.9 fusion.11
  97.7 0.9 exponential_reduce_fusion.1
  99.0 1.5 fusion.6
  100.6 2.0 exponential_reduce_fusion
  102.7 1.3 fusion.19
  104.0 2.4 fusion.14
  107.3 3.2 convolution_convert_fusion.1
  110.5 57.3 %move_2.1 = (f32[2,64,2048]{2,1,0:T(8,128)}, bf16[4,2,128,2048]{3,2,1,0:T(8,128)(2,1)}) custom-call(bf16[8,2,64,2048]{3,2,1,0:T(8,128)(2,1)} %bitcast.340, bf16[2,128,2048]{2,1,0:T(8,128)(2,1)} %bitcast.374), custom_call_target="tpu_custom_call" | custom-call | bytes 120000000 | tf_op jit(solution)/shard_map/move_2/pallas_call | solution.py:1140
  167.8 1.5 multiply_reduce_fusion.3
  169.9 2.2 multiply_convert_fusion.1.refs_0_
  172.1 5.2 fusion.4
  177.2 61.0 %move_3.1 = (bf16[8,2,64,2048]{3,2,1,0:T(8,128)(2,1)}, bf16[4,2,128,2048]{3,2,1,0:T(8,128)(2,1)}, bf16[4,256,1024]{2,1,0:T(8,128)(2,1)}, bf16[4,256,1024]{2,1,0:T(8,128)(2,1)}, bf16[4,256,1024]{2,1,0:T(8,128)(2,1)}) custom-call(bf16[2,64,2048]{2,1,0:T(8,128)(2,1)} %multiply_convert_fusion.1.refs_0_, bf16[2,128,2048]{2,1,0:T(8,128)(2,1)} %bitcast.375, ...), custom_call_target="tpu_custom_call" | custom-call | bytes 120000000 | tf_op jit(solution)/shard_map/move_3/pallas_call | solution.py:1140
  238.2 53.2 %move_4.1 = (f32[2,64,2048]{2,1,0:T(8,128)}, f32[2,128,2048]{2,1,0:T(8,128)}, bf16[4,2,2,64,2048]{4,3,2,1,0:T(8,128)(2,1)}, bf16[4,2,2,64,2048]{4,3,2,1,0:T(8,128)(2,1)}, bf16[4,2,2,64,2048]{4,3,2,1,0:T(8,128)(2,1)}) custom-call(bf16[1024,1024]{1,0:T(8,128)(2,1)} %bitcast.368, bf16[1024,1024]{1,0:T(8,128)(2,1)} %bitcast.369, bf16[1024,1024]{1,0:T(8,128)(2,1)} %bitcast.370, ...), custom_call_target="tpu_custom_call" | custom-call | bytes 120000000 | tf_op jit(solution)/shard_map/move_4/pallas_call | solution.py:1140
  291.5 1.8 multiply_reduce_fusion.1
  294.1 3.4 fusion.82
  299.1 66.8 %move_5.1 = (bf16[8,2,64,2048]{3,2,1,0:T(8,128)(2,1)}, f32[2,128,2048]{2,1,0:T(8,128)}) custom-call(bf16[2,64,2048]{2,1,0:T(8,128)(2,1)} %bitcast.362, bf16[4,2,128,2048]{3,2,1,0:T(8,128)(2,1)} %bitcast.351), custom_call_target="tpu_custom_call" | custom-call | bytes 120000000 | tf_op jit(solution)/shard_map/move_5/pallas_call | solution.py:1140
  365.9 3.8 convolution_convert_fusion.4
  370.3 3.9 fusion.7
  374.3 1.3 fusion.9
  377.1 3.8 fusion
  380.9 2.8 fusion.2
  383.7 1.4 fusion.18
  386.2 0.8 fusion.13
  387.3 1.2 convolution_bitcast_fusion.2
  388.5 2.4 fusion.20
  390.9 4.4 convolution_convert_fusion
  395.3 2.2 convolution_convert_fusion.3
  397.5 3.6 convolution_convert_fusion.2
  401.1 74.4 %move_6.1 = (bf16[8,64,384]{2,1,0:T(8,128)(2,1)}, f32[2,64,2048]{2,1,0:T(8,128)}, f32[2,32,2048]{2,1,0:T(8,128)}, f32[2,128,2048]{2,1,0:T(8,128)}) custom-call(bf16[4,2,4,64,384]{4,3,2,1,0:T(8,128)(2,1)} %bitcast.371, bf16[8,2,64,2048]{3,2,1,0:T(8,128)(2,1)} %bitcast.355, bf16[4,2,32,2048]{3,2,1,0:T(8,128)(2,1)} %bitcast.382, bf16[4,2,128,2048]{3,2,1,0:T(8,128)(2,1)} %bitcast.354), custom_call_target="tpu_custom_call" | custom-call | bytes 120000000 | tf_op jit(solution)/shard_map/move_6/pallas_call | solution.py:1140
  475.6 1.5 fusion.24
  478.5 22.8 %move_7.1 = f32[8,128]{1,0:T(8,128)} custom-call(f32[32,8,128]{2,1,0:T(8,128)} %pad.25.refs_0_), custom_call_target="tpu_custom_call" | custom-call | bytes 120000000 | tf_op jit(solution)/shard_map/move_7/pallas_call | solution.py:1140
  501.4 1.2 convert_element_type.174
  502.6 0.8 slice_bitcast_fusion.15
  504.1 2.1 concatenate.102
  506.2 1.3 slice_bitcast_fusion.31
  507.5 3.2 fusion.29
  510.7 0.8 copy.127
  511.5 1.3 copy.128
  512.8 1.3 copy.129
  514.1 1.3 copy.130
  (169 shorter events, 16.9 us)
Async XLA Ops:
  7.2 170.1 %all-gather.2.cloned.1.call-start = ((), (), s32[]{:S(2)}) async-start(), calls=%async_computation.1 | async-start | bytes 4718592 | tf_op jit(solution)/shard_map/all_gather | solution.py:1267
  12.8 0.7 copy-start.23
  83.0 424.5 %reduce-scatter.2.cloned.1.call-start = ((), (), s32[]{:S(2)}) async-start(), calls=%async_computation.2 | async-start | bytes 4718592 | tf_op jit(solution)/shard_map/reduce_scatter | solution.py:1345
  87.5 3.7 copy-start.24
  87.5 3.8 copy-start.44
  93.1 10.8 %copy-start.33 = (bf16[1024,384]{0,1:T(8,128)(2,1)}, bf16[1024,384]{0,1:T(8,128)(2,1)S(1)}, u32[]{:S(2)}) copy-start(bf16[1024,384]{0,1:T(8,128)(2,1)S(1)} %get-tuple-element.227) | copy-start | bytes 2359300
  94.7 2.1 copy-start.36
  94.7 3.0 copy-start.30
  95.4 3.6 copy-start.19
  96.7 2.3 copy-start.11
  96.8 2.3 copy-start.13
  97.7 5.0 copy-start.1
  98.6 4.1 copy-start.28
  99.0 5.0 copy-start.5
  100.6 3.4 copy-start
  102.7 3.7 copy-start.26
  104.0 3.3 copy-start.18
  106.5 0.8 copy-start.9
  110.5 57.3 %copy-start.4 = (bf16[1,128,2048]{2,1,0:T(8,128)(2,1)S(1)}, bf16[1,128,2048]{2,1,0:T(8,128)(2,1)}, u32[]{:S(2)}) copy-start(bf16[1,128,2048]{2,1,0:T(8,128)(2,1)} %param.25) | copy-start | bytes 1572868
  169.3 8.0 %copy-start.35 = (f32[2,64]{1,0:T(2,128)}, f32[2,64]{1,0:T(2,128)S(1)}, u32[]{:S(2)}) copy-start(f32[2,64]{1,0:T(2,128)S(1)} %add_rsqrt_fusion.1) | copy-start | bytes 1540
  169.3 7.9 %copy-start.42 = (f32[128]{0:T(128)}, f32[128]{0:T(128)S(1)}, u32[]{:S(2)}) copy-start(f32[128]{0:T(128)S(1)} %rsqrt.44) | copy-start | bytes 1540
  369.6 0.7 copy-start.29
  370.3 3.9 copy-start.2
  370.3 6.0 %slice-start = ((s8[8388608]{0:T(1024)(128)(4,1)}), s8[4194304]{0:T(1024)(128)(4,1)S(1)}, s32[]{:S(2)}) async-start(s8[8388608]{0:T(1024)(128)(4,1)} %bitcast.338), calls=%async_computation.3 | async-start | bytes 8388608
  374.2 1.4 copy-start.12
  374.2 1.4 copy-start.14
  374.2 2.8 slice-start.1
  374.3 2.8 copy-start.6
  374.3 2.8 copy-start.27
  383.7 1.4 copy-start.31
  383.7 1.4 copy-start.37
  383.7 2.0 copy-start.20
  385.1 1.9 copy-start.21
  388.5 2.4 copy-start.45
  390.9 4.4 copy-start.10
  390.9 4.4 copy-start.43
  395.3 2.3 copy-start.8
  401.1 74.5 %copy-start.25 = (f32[2048]{0:T(1024)S(1)}, f32[2048]{0:T(1024)}, u32[]{:S(2)}) copy-start(f32[2048]{0:T(1024)} %copy-done.24) | copy-start | bytes 24580
  401.1 74.5 %copy-start.38 = (f32[2,64]{1,0:T(2,128)S(1)}, f32[2,64]{1,0:T(2,128)}, u32[]{:S(2)}) copy-start(f32[2,64]{1,0:T(2,128)} %rsqrt.47) | copy-start | bytes 1540
  401.1 76.6 %copy-start.32 = (f32[1,32,64]{2,0,1:T(1,128)S(1)}, f32[1,32,64]{2,0,1:T(1,128)}, u32[]{:S(2)}) copy-start(f32[1,32,64]{2,0,1:T(1,128)} %stack.46) | copy-start | bytes 24580
  475.6 31.9 %copy-start.39 = (f32[128]{0:T(128)S(1)}, f32[128]{0:T(128)}, u32[]{:S(2)}) copy-start(f32[128]{0:T(128)} %get-tuple-element.225) | copy-start | bytes 1540
  475.6 31.9 %copy-start.41 = (f32[128]{0:T(128)S(1)}, f32[128]{0:T(128)}, u32[]{:S(2)}) copy-start(f32[128]{0:T(128)} %copy-done.40) | copy-start | bytes 1540
  501.3 6.1 %copy-start.3 = (f32[2,64,2048]{2,1,0:T(8,128)S(1)}, f32[2,64,2048]{2,1,0:T(8,128)}, u32[]{:S(2)}) copy-start(f32[2,64,2048]{2,1,0:T(8,128)} %get-tuple-element.127) | copy-start | bytes 3145732
  501.4 6.1 %copy-start.7 = (f32[2,64,2048]{2,1,0:T(8,128)S(1)}, f32[2,64,2048]{2,1,0:T(8,128)}, u32[]{:S(2)}) copy-start(f32[2,64,2048]{2,1,0:T(8,128)} %get-tuple-element.143) | copy-start | bytes 3145732
  503.4 7.3 %copy-start.22 = (f32[2,32,2048]{2,1,0:T(8,128)S(1)}, f32[2,32,2048]{2,1,0:T(8,128)}, u32[]{:S(2)}) copy-start(f32[2,32,2048]{2,1,0:T(8,128)} %get-tuple-element.145) | copy-start | bytes 1572868
  507.5 4.0 copy-start.16
  507.5 5.3 %copy-start.17 = (f32[2,128,2048]{2,1,0:T(8,128)S(1)}, f32[2,128,2048]{2,1,0:T(8,128)}, u32[]{:S(2)}) copy-start(f32[2,128,2048]{2,1,0:T(8,128)} %get-tuple-element.147) | copy-start | bytes 6291460
  511.5 2.6 copy-start.15
  (2 other events, 1.2 us)
Sparse Core Ops, SparseCore 0:
  83.1 46.6 all-gather.1
  369.8 51.2 reduce-scatter.1

commit v3 on v2

--- a/solution.py
+++ b/solution.py
@@ -230,10 +230,10 @@
         for half in range(SUB):
             pair(at, half).start()
 
-    def step(low, half):
-        high = chips - 1 - low
-
-        @pl.when(high > chip)
+    def step(wave, half):
+        high, low = chips - 1 - wave + chip, wave - (chips - 1 - chip)
+
+        @pl.when(chip <= wave)
         def _():
             pair(high, half).wait_recv()
 
@@ -249,7 +249,7 @@
 
             up(high, half).start()
 
-        @pl.when(low < chip)
+        @pl.when(low >= 0)
         def _():
             pair(low, half).wait_recv()
 
@@ -563,21 +563,25 @@
 
 
 class ColumnsBack:
-    def __init__(self, partial, rows, dps, groups):
+    def __init__(self, partial, order, heads_width, copies, rows, dps, groups):
         width, hops = partial.shape[1], dps // 2
         shape = (groups, rows, width)
         halves = (2, groups // 2, rows, width)
+        self.where = [order.index(g) for g in range(groups)]
+        self.heads_width, self.copies = heads_width, copies
+        joint = groups * heads_width + 2 * KV_HEADS * HEAD_DIM
         self.inputs, self.in_specs = [partial.reshape((dps,) + halves)], [VM]
-        self.outs, self.out_specs = [jax.ShapeDtypeStruct(shape, jnp.bfloat16)], [ANY]
+        self.outs, self.out_specs = [jax.ShapeDtypeStruct((rows, joint), jnp.float32)], [VM]
         self.scratch = (
-            [pltpu.VMEM(halves, jnp.bfloat16), DMA, DMA((groups,)), DMA((groups,))]
+            [pltpu.VMEM(shape, jnp.bfloat16), pltpu.VMEM(halves, jnp.bfloat16)]
+            + [DMA, DMA((groups,)), DMA((groups,))]
             + [pltpu.VMEM((hops,) + halves, jnp.bfloat16)] * 2
             + [pltpu.VMEM((hops - 1,) + halves, jnp.bfloat16)] * 2
             + ring_sems(hops)
         )
         self.result = lambda out: out
 
-    def bind(self, place, p_ref, out_ref, total, own_sem, sends, recvs, *scratch):
+    def bind(self, place, p_ref, joint_ref, out_ref, total, own_sem, sends, recvs, *scratch):
         s, groups = place.s, place.groups
         half_of = groups // 2
 
@@ -600,11 +604,34 @@
             for i in range(1, groups):
                 swap(i).start()
 
+        def keys_values(head):
+            first = self.where[head * self.copies]
+            span = slice(self.heads_width, self.heads_width + 2 * HEAD_DIM)
+            value = out_ref[first, :, span].astype(jnp.float32)
+            for i in range(1, self.copies):
+                value += out_ref[self.where[head * self.copies + i], :, span].astype(jnp.float32)
+            return value
+
         def finish():
             here.wait()
             for i in range(1, groups):
                 swap(i).wait_recv()
                 swap(i).wait_send()
+            heads = self.heads_width
+            for g in range(groups):
+                value = out_ref[self.where[g], :, :heads]
+                joint_ref[:, g * heads : (g + 1) * heads] = value.astype(jnp.float32)
+            for head in range(0, KV_HEADS, 2):
+                even, odd = keys_values(head), keys_values(head + 1)
+                lanes = lax.broadcasted_iota(jnp.int32, even.shape, 1)
+                at = groups * heads + head * HEAD_DIM
+                joint_ref[:, at : at + 2 * HEAD_DIM] = jnp.where(
+                    lanes < HEAD_DIM, even, pltpu.roll(odd, HEAD_DIM, 1)
+                )
+                at += KV_HEADS * HEAD_DIM
+                joint_ref[:, at : at + 2 * HEAD_DIM] = jnp.where(
+                    lanes < HEAD_DIM, pltpu.roll(even, HEAD_DIM, 1), odd
+                )
 
         ticks = {
             2 * (place.hops - hop) - 1: functools.partial(ring[1], hop)
@@ -928,7 +955,7 @@
         act = pltpu.VMEM((length, held), jnp.bfloat16)
         weight = pltpu.VMEM((held, width), jnp.bfloat16)
         tokens = pltpu.VMEM((length, width), jnp.bfloat16)
-        self.scratch = [act] * 3 + [weight] * 2 + [tokens] * 2
+        self.scratch = [act] * 3 + [weight] * 3 + [tokens] * 2
         self.scratch += [
             pltpu.VMEM((groups,) + shape, jnp.bfloat16),
             pltpu.VMEM((dps,) + owned, jnp.bfloat16),
@@ -953,9 +980,9 @@
     def bind(self, place, *refs):
         sources, refs = refs[:8], refs[8:]
         total_ref, own_ref, gate_out, up_out, result_out = refs[:5]
-        inner, dgate, dup, gate, up, normed, grads = refs[5:12]
-        p_ref, term, stage, loads, stage_sem = refs[12:17]
-        line_refs, ring_refs = refs[17:26], refs[26:]
+        inner, dgate, dup, gate, up, down, normed, grads = refs[5:13]
+        p_ref, term, stage, loads, stage_sem = refs[13:18]
+        line_refs, ring_refs = refs[18:27], refs[27:]
         chip, chips, hops = place.chip, place.chips, place.hops
         held, width = gate.shape
         pair = inner.shape[0] // chips
@@ -967,14 +994,14 @@
             own_ref[half] = value
 
         ring = ring_scatter(place, lambda at, half: term.at[at, half], put, *ring_refs)
-        targets = [inner, dgate, dup, gate, up, gate, normed, grads]
+        targets = [inner, dgate, dup, gate, up, down, normed, grads]
         copies = [
             pltpu.make_async_copy(source, target, loads.at[i])
             for i, (source, target) in enumerate(zip(sources, targets))
         ]
 
         def start():
-            for i in (0, 7, 1, 3, 2, 4, 6):
+            for i in (0, 7, 1, 3, 2, 4, 6, 5):
                 copies[i].start()
 
         def rows_of(ref, at):
@@ -1031,7 +1058,6 @@
             if hop == hops - 1:
                 ring[4]()
 
-        first_job_at = first_job
         for hop in range(hops - 1, 0, -1):
             jobs.append(functools.partial(next_job, hop))
             jobs.append(functools.partial(ring[1], hop))
@@ -1064,7 +1090,7 @@
                 left = rows_of(inner, at)
                 for first in range(0, width, wide):
                     span = slice(first, first + wide)
-                    value = jnp.dot(left, gate[:, span], preferred_element_type=jnp.float32)
+                    value = jnp.dot(left, down[:, span], preferred_element_type=jnp.float32)
                     slot[:, :, :, span] = value.astype(jnp.bfloat16).reshape(
                         slot.shape[:3] + (wide,)
                     )
@@ -1072,36 +1098,51 @@
             staged(fill, result_out.at[at])
 
         def sequence():
-            first_job_at()
+            first_job()
             for i in (1, 3, 2, 4):
                 copies[i].wait()
-            for low in range(chips - 1):
-                high = chips - 1 - low
-
-                @pl.when(high > chip)
-                def _():
-                    partial(high)
-
-                @pl.when(low < chip)
-                def _():
-                    partial(low)
-
-                if jobs:
+            tiles = [
+                functools.partial(weight_tile, ref, row, out)
+                for ref, out in ((dgate, gate_out), (dup, up_out))
+                for row in range(0, held, TILE)
+            ]
+            tiles += [functools.partial(result_tile, at) for at in range(chips)]
+            done = [0]
+
+            def fill(most):
+                for _ in range(most):
+                    if tiles:
+                        if done[0] == 0:
+                            copies[6].wait()
+                        if done[0] == 2 * (held // TILE):
+                            copies[5].wait()
+                        done[0] += 1
+                        tiles.pop(0)()
+
+            for wave in range(chips - 1):
+                high = chips - 1 - wave
+                ups = (high > chip).astype(jnp.int32)
+                downs = (wave < chip).astype(jnp.int32)
+
+                def each(i, _, high=high, wave=wave, ups=ups):
+                    partial(jnp.where(i < ups, high, wave))
+                    return 0
+
+                lax.fori_loop(0, ups + downs, each, 0)
+                fill(1)
+                step(wave, 0)
+                if wave == 0:
+                    step(wave, 1)
                     jobs.pop(0)()
-                for half in range(SUB):
-                    step(low, half)
+                else:
+                    fill(1)
+                    step(wave, 1)
+                    if jobs:
+                        jobs.pop(0)()
             partial(chip)
             for job in jobs:
                 job()
-            copies[5].start()
-            copies[6].wait()
-            for row in range(0, held, TILE):
-                weight_tile(dgate, row, gate_out)
-            for row in range(0, held, TILE):
-                weight_tile(dup, row, up_out)
-            copies[5].wait()
-            for at in range(chips):
-                result_tile(at)
+            fill(len(tiles))
 
         def finish():
             ring[2]()
@@ -1392,37 +1433,26 @@
     partial = lax.dot_general(
         grad_mixed, qkv_local, contract_cols, preferred_element_type=jnp.float32
     )
-    qkv_owned, grad_normed_one, out_owned, up_owned = move(
+    qkv_term = qkv_term.astype(jnp.bfloat16)
+    gain_one_term = (
+        jnp.sum(qkv_term.astype(jnp.float32) * qkv_local.astype(jnp.float32), axis=1) / gain_one
+    )
+    terms = jnp.stack([gain_one_term, gain_two_term]).reshape(2, dps * groups, gain_width)
+    terms = jnp.pad(terms.transpose(1, 0, 2), ((0, 0), (0, 6), (0, 128 - gain_width)))
+    qkv_owned, grad_normed_one, out_owned, up_owned, gain_grads = move(
         [
-            ColumnsBack(qkv_term.astype(jnp.bfloat16), weight_rows, dps, groups),
+            ColumnsBack(qkv_term, order, local_width, kv_copies, weight_rows, dps, groups),
             LineScatter(partial.astype(jnp.bfloat16), dps, groups),
             RowsBack(out_term, weight_rows, dps, groups),
             RingScatter(up_term, dps, groups),
+            Spread(terms, True, dps, groups),
         ],
         dps,
         groups,
         6,
         greet_all,
     )
-    qkv_owned = qkv_owned.astype(jnp.float32)
-    place = [order.index(g) for g in range(groups)]
-    qkv_owned = jnp.concatenate(
-        [qkv_owned[place[g], :, :local_width] for g in range(groups)]
-        + [
-            sum(
-                qkv_owned[place[head * kv_copies + i], :, at : at + HEAD_DIM]
-                for i in range(kv_copies)
-            )
-            for at in (local_width, local_width + HEAD_DIM)
-            for head in range(KV_HEADS)
-        ],
-        axis=1,
-    )
-    gain_one_term = jnp.sum(grad_normed_one * x_rows * factor_one, axis=0)
     grad_input = grad_hidden + norm_grad(x_rows, factor_one, gain_one, grad_normed_one)
-    terms = jnp.stack([gain_one_term, gain_two_term]).reshape(2, dps * groups, gain_width)
-    terms = jnp.pad(terms.transpose(1, 0, 2), ((0, 0), (0, 6), (0, 128 - gain_width)))
-    (gain_grads,) = move([Spread(terms, True, dps, groups)], dps, groups, 7, greet_all)
     return (
         block_out,
         grad_input[None],

time: 526 us -> 477 us (0.907)
  Pallas kernels: 405 us -> 355 us
    pallas_call x7 -> x6, Pallas kernels: 405 us -> 355 us  [move(): pl.pallas_call(kernel, out_shape=[out for part in parts for out in part.o...]
  transfers between devices with their start and end apart: 2 -> 2, of which waited for: 0 -> 0; matrix products, arithmetic and copies ran while one was open for 14% -> 16% of each run, Pallas kernels for 30% -> 26%
where the time goes in v3:
time: 477 us; the launch traced here: 471 us
  Pallas kernels  355 us (74%)
  matrix products  40.6 us (9%)
  other arithmetic  40.4 us (8%)
  local copies, waits for them, and re-layouts  19.7 us (4%)
  between operations  15.5 us (3%)
    pallas_call x6, Pallas kernels, move(): pl.pallas_call(kernel, out_shape=[out for part in parts for out in part.o...  355 us
  transfers between devices with their start and end apart: 2, of which 0 were waited for; matrix products, arithmetic and copies ran while one was open for 16% of the time, Pallas kernels for 26%

profile of v3, /device:TPU:0, one launch (start us, length us, event | category | flops | bytes accessed | tf_op | source)
XLA Modules:
  0.0 471.4 jit_solution(15654932994731630284)
XLA Ops:
  7.2 0.9 fusion.83
  8.1 1.0 slice.255
  13.5 69.5 %move_1.1 = (bf16[4,8,64,384]{3,2,1,0:T(8,128)(2,1)}, bf16[8,2,64,2048]{3,2,1,0:T(8,128)(2,1)}, bf16[4,2,32,2048]{3,2,1,0:T(8,128)(2,1)}, bf16[4,2,128,2048]{3,2,1,0:T(8,128)(2,1)}, f32[32,8,128]{2,1,0:T(8,128)}) custom-call(bf16[8,64,384]{2,1,0:T(8,128)(2,1)} %copy-done.23, bf16[2,64,2048]{2,1,0:T(8,128)(2,1)} %bitcast.297, bf16[2,32,2048]{2,1,0:T(8,128)(2,1)} %bitcast.347, ...), custom_call_target="tpu_custom_call" | custom-call | bytes 120000000 | tf_op jit(solution)/shard_map/move_1/pallas_call | solution.py:1181
  83.3 0.9 copy.51
  84.2 3.1 multiply_reduce_fusion
  88.1 3.6 multiply_convert_fusion
  91.7 1.9 fusion.87
  93.6 1.1 slice_reduce_fusion
  96.2 1.2 fusion.63
  97.6 0.9 fusion.11
  98.5 0.9 exponential_reduce_fusion.1
  99.9 1.5 fusion.6
  101.5 2.2 exponential_reduce_fusion
  103.7 1.3 fusion.19
  105.0 2.4 fusion.14
  108.2 3.4 convolution_convert_fusion.1
  111.6 51.8 %move_2.1 = (f32[2,64,2048]{2,1,0:T(8,128)}, bf16[4,2,128,2048]{3,2,1,0:T(8,128)(2,1)}) custom-call(bf16[8,2,64,2048]{3,2,1,0:T(8,128)(2,1)} %bitcast.296, bf16[2,128,2048]{2,1,0:T(8,128)(2,1)} %bitcast.330), custom_call_target="tpu_custom_call" | custom-call | bytes 120000000 | tf_op jit(solution)/shard_map/move_2/pallas_call | solution.py:1181
  163.4 1.5 multiply_reduce_fusion.4
  165.5 2.2 multiply_convert_fusion.1.refs_0_
  167.7 5.2 %fusion.4 = bf16[1024,2048]{1,0:T(8,128)(2,1)} fusion(f32[2048]{0:T(1024)} %copy-done.24, f32[1024]{0:T(1024)} %rsqrt.42, bf16[8,2,64,2048]{3,2,1,0:T(8,128)(2,1)} %get-tuple-element.124), kind=kLoop, calls=%fused_computation.7 | loop fusion | flops 8388608 | bytes 8400896 | tf_op jit(solution)/shard_map/convert_element_type | solution.py:1305
  173.0 65.2 %move_3.1 = (bf16[8,2,64,2048]{3,2,1,0:T(8,128)(2,1)}, bf16[4,2,128,2048]{3,2,1,0:T(8,128)(2,1)}, bf16[4,256,1024]{2,1,0:T(8,128)(2,1)}, bf16[4,256,1024]{2,1,0:T(8,128)(2,1)}, bf16[4,256,1024]{2,1,0:T(8,128)(2,1)}) custom-call(bf16[2,64,2048]{2,1,0:T(8,128)(2,1)} %multiply_convert_fusion.1.refs_0_, bf16[2,128,2048]{2,1,0:T(8,128)(2,1)} %bitcast.331, ...), custom_call_target="tpu_custom_call" | custom-call | bytes 120000000 | tf_op jit(solution)/shard_map/move_3/pallas_call | solution.py:1181
  238.2 49.0 %move_4.1 = (f32[2,64,2048]{2,1,0:T(8,128)}, f32[2,128,2048]{2,1,0:T(8,128)}, bf16[4,2,2,64,2048]{4,3,2,1,0:T(8,128)(2,1)}, bf16[4,2,2,64,2048]{4,3,2,1,0:T(8,128)(2,1)}, bf16[4,2,2,64,2048]{4,3,2,1,0:T(8,128)(2,1)}) custom-call(bf16[1024,1024]{1,0:T(8,128)(2,1)} %bitcast.324, bf16[1024,1024]{1,0:T(8,128)(2,1)} %bitcast.325, bf16[1024,1024]{1,0:T(8,128)(2,1)} %bitcast.326, ...), custom_call_target="tpu_custom_call" | custom-call | bytes 120000000 | tf_op jit(solution)/shard_map/move_4/pallas_call | solution.py:1181
  287.2 2.4 multiply_reduce_fusion.2
  289.7 3.9 fusion.80
  293.6 46.7 %move_5.1 = (bf16[8,2,64,2048]{3,2,1,0:T(8,128)(2,1)}, f32[2,128,2048]{2,1,0:T(8,128)}) custom-call(bf16[2,64,2048]{2,1,0:T(8,128)(2,1)} %bitcast.318, bf16[4,2,128,2048]{3,2,1,0:T(8,128)(2,1)} %bitcast.307), custom_call_target="tpu_custom_call" | custom-call | bytes 120000000 | tf_op jit(solution)/shard_map/move_5/pallas_call | solution.py:1181
  340.4 1.2 copy-done.17
  341.6 4.3 convolution_convert_fusion.4
  345.9 1.1 fusion.82
  347.0 3.9 fusion.7
  351.0 1.3 fusion.9
  353.6 3.8 fusion
  357.4 2.9 fusion.2
  360.3 1.4 fusion.18
  362.8 0.8 fusion.13
  363.9 1.2 convolution_bitcast_fusion.2
  365.1 2.4 fusion.20
  367.9 3.7 multiply_reduce_fusion.1
  372.4 4.3 convolution_convert_fusion
  376.8 2.2 convolution_convert_fusion.3
  379.0 72.7 %move_6.1 = (f32[64,3072]{1,0:T(8,128)}, f32[2,64,2048]{2,1,0:T(8,128)}, f32[2,32,2048]{2,1,0:T(8,128)}, f32[2,128,2048]{2,1,0:T(8,128)}, f32[8,128]{1,0:T(8,128)}) custom-call(bf16[4,2,4,64,384]{4,3,2,1,0:T(8,128)(2,1)} %bitcast.327, bf16[8,2,64,2048]{3,2,1,0:T(8,128)(2,1)} %bitcast.311, bf16[4,2,32,2048]{3,2,1,0:T(8,128)(2,1)} %bitcast.338, ...), custom_call_target="tpu_custom_call" | custom-call | bytes 120000000 | tf_op jit(solution)/shard_map/move_6/pallas_call | solution.py:1181
  451.8 1.5 fusion.22
  453.4 1.3 slice_bitcast_fusion.7
  454.7 3.7 fusion.27
  458.4 0.9 copy.130
  459.3 0.8 copy.131
  460.1 1.3 copy.132
  461.4 1.3 copy.133
  462.8 1.3 copy.134
  (167 shorter events, 12.9 us)
Async XLA Ops:
  7.2 165.8 %all-gather.2.cloned.1.call-start = ((), (), s32[]{:S(2)}) async-start(), calls=%async_computation.1 | async-start | bytes 4718592 | tf_op jit(solution)/shard_map/all_gather | solution.py:1308
  83.0 371.7 %reduce-scatter.2.cloned.1.call-start = ((), (), s32[]{:S(2)}) async-start(), calls=%async_computation.2 | async-start | bytes 4718592 | tf_op jit(solution)/shard_map/reduce_scatter | solution.py:1386
  88.0 3.7 copy-start.26
  88.1 3.7 copy-start.24
  88.1 3.7 copy-start.43
  93.6 11.3 %copy-start.34 = (bf16[1024,384]{0,1:T(8,128)(2,1)}, bf16[1024,384]{0,1:T(8,128)(2,1)S(1)}, u32[]{:S(2)}) copy-start(bf16[1024,384]{0,1:T(8,128)(2,1)S(1)} %get-tuple-element.201) | copy-start | bytes 2359300
  95.5 3.0 copy-start.38
  95.5 3.0 copy-start.32
  96.2 3.7 copy-start.19
  97.6 2.3 copy-start.9
  97.6 2.3 copy-start.11
  98.5 5.1 %copy-start.1 = (f32[512,512,4]{1,0,2:T(8,128)}, f32[512,512,4]{1,0,2:T(8,128)S(1)}, u32[]{:S(2)}) copy-start(f32[512,512,4]{1,0,2:T(8,128)S(1)} %get-tuple-element.206) | copy-start | bytes 12582916
  99.5 4.2 copy-start.30
  99.9 5.1 %copy-start.4 = (pred[512,1024]{0,1:T(8,128)(4,1)}, pred[512,1024]{0,1:T(8,128)(4,1)S(1)}, u32[]{:S(2)}) copy-start(pred[512,1024]{0,1:T(8,128)(4,1)S(1)} %iota_compare_fusion) | copy-start | bytes 1572868
  101.5 3.5 copy-start
  103.6 3.7 copy-start.28
  105.0 3.3 copy-start.16
  107.4 0.8 copy-start.7
  111.6 51.8 %copy-start.3 = (bf16[1,128,2048]{2,1,0:T(8,128)(2,1)S(1)}, bf16[1,128,2048]{2,1,0:T(8,128)(2,1)}, u32[]{:S(2)}) copy-start(bf16[1,128,2048]{2,1,0:T(8,128)(2,1)} %param.25) | copy-start | bytes 1572868
  164.9 8.1 %copy-start.37 = (f32[2,64]{1,0:T(2,128)}, f32[2,64]{1,0:T(2,128)S(1)}, u32[]{:S(2)}) copy-start(f32[2,64]{1,0:T(2,128)S(1)} %add_rsqrt_fusion.1) | copy-start | bytes 1540
  165.0 8.0 %copy-start.41 = (f32[128]{0:T(128)}, f32[128]{0:T(128)S(1)}, u32[]{:S(2)}) copy-start(f32[128]{0:T(128)S(1)} %rsqrt.40) | copy-start | bytes 1540
  340.3 1.2 copy-start.17
  341.6 4.3 copy-start.35
  341.6 5.4 %copy-start.31 = (f32[4,512]{1,0:T(4,128)S(1)}, f32[4,512]{1,0:T(4,128)}, u32[]{:S(2)}) copy-start(f32[4,512]{1,0:T(4,128)} %copy-done.30) | copy-start | bytes 24580
  347.0 3.9 copy-start.2
  347.0 6.0 %slice-start = ((s8[8388608]{0:T(1024)(128)(4,1)}), s8[4194304]{0:T(1024)(128)(4,1)S(1)}, s32[]{:S(2)}) async-start(s8[8388608]{0:T(1024)(128)(4,1)} %bitcast.294), calls=%async_computation.3 | async-start | bytes 8388608
  350.9 1.4 copy-start.10
  350.9 1.4 copy-start.12
  350.9 2.6 slice-start.1
  351.0 2.6 copy-start.5
  351.0 2.6 copy-start.29
  360.3 1.4 copy-start.33
  360.3 1.4 copy-start.39
  360.3 2.0 copy-start.20
  361.7 1.9 copy-start.21
  365.1 2.4 copy-start.6
  365.1 2.7 copy-start.44
  367.9 3.8 copy-start.27
  367.9 4.6 copy-start.45
  372.4 4.3 copy-start.8
  372.4 4.3 copy-start.42
  379.0 72.7 %copy-start.25 = (f32[2048]{0:T(1024)S(1)}, f32[2048]{0:T(1024)}, u32[]{:S(2)}) copy-start(f32[2048]{0:T(1024)} %copy-done.24) | copy-start | bytes 24580
  379.0 74.4 %copy-start.40 = (f32[128]{0:T(128)S(1)}, f32[128]{0:T(128)}, u32[]{:S(2)}) copy-start(f32[128]{0:T(128)} %get-tuple-element.161) | copy-start | bytes 1540
  451.7 6.7 %copy-start.18 = (f32[64,3072]{1,0:T(8,128)S(1)}, f32[64,3072]{1,0:T(8,128)}, u32[]{:S(2)}) copy-start(f32[64,3072]{1,0:T(8,128)} %get-tuple-element.248) | copy-start | bytes 2359300
  451.8 7.6 %copy-start.22 = (f32[2,32,2048]{2,1,0:T(8,128)S(1)}, f32[2,32,2048]{2,1,0:T(8,128)}, u32[]{:S(2)}) copy-start(f32[2,32,2048]{2,1,0:T(8,128)} %get-tuple-element.146) | copy-start | bytes 1572868
  454.7 5.4 %copy-start.14 = (f32[2,128,2048]{2,1,0:T(8,128)S(1)}, f32[2,128,2048]{2,1,0:T(8,128)}, u32[]{:S(2)}) copy-start(f32[2,128,2048]{2,1,0:T(8,128)} %get-tuple-element.147) | copy-start | bytes 6291460
  458.4 3.0 copy-start.15
  460.1 2.6 copy-start.13
  (2 other events, 1.4 us)
Sparse Core Ops, SparseCore 0:
  83.1 45.3 all-gather.1
  340.5 48.0 reduce-scatter.1

commit v4 on v3

--- a/solution.py
+++ b/solution.py
@@ -369,13 +369,20 @@
         right(out(before, 0), before, hop + 1, 0).start()
         left(out(after, 1), after, hop, 1).wait_recv()
         left(out(after, 1), after, hop + 1, 1).start()
-        right(out(before, 1), before, hop, 1).wait_recv()
-        left(out(after, 0), after, hop, 0).wait_recv()
         if full:
+            right(out(before, 1), before, hop, 1).wait_recv()
+            left(out(after, 0), after, hop, 0).wait_recv()
             right(out(before, 1), before, hop + 1, 1).start()
             left(out(after, 0), after, hop + 1, 0).start()
 
-    def finish():
+    def near():
+        before, after = place.ring(1 - hops), place.ring(hops - 1)
+        right(out(before, 1), before, hops - 1, 1).wait_recv()
+        left(out(after, 0), after, hops - 1, 0).wait_recv()
+
+    def finish(waited=False):
+        if not waited:
+            near()
         right(out(place.d, 0), place.ring(-hops), hops, 0).wait_recv()
         left(out(place.d, 1), place.ring(hops), hops, 1).wait_recv()
         for hop in range(1, hops + 1):
@@ -385,7 +392,7 @@
                 if hop < hops or half == 1:
                     left(out(place.d, half), place.d, hop, half).wait_send()
 
-    return start, forward, finish
+    return start, forward, finish, near
 
 
 def ring_scatter(place, part, put, rbuf, lbuf, rout, lout, rs, rr, ls, lr):
@@ -483,7 +490,8 @@
 
 
 class RingScatter:
-    def __init__(self, partial, dps, groups):
+    def __init__(self, partial, dps, groups, late=False):
+        self.late = late
         total, width = partial.shape
         rows, hops = total // dps, dps // 2
         shape = (2, rows // 2, width)
@@ -501,10 +509,14 @@
             out_ref[half] = value
 
         ring = ring_scatter(place, lambda chunk, half: p_ref.at[chunk, half], put, *scratch)
+        first = 1 if self.late else -1
         ticks = {
-            2 * (place.hops - hop) - 1: functools.partial(ring[1], hop)
+            2 * (place.hops - hop) + first: functools.partial(ring[1], hop)
             for hop in range(1, place.hops)
         }
+        if self.late:
+            ticks[1] = ring[0]
+            return lambda: None, ticks, ring[2]
         return ring[0], ticks, ring[2]
 
 
@@ -820,6 +832,7 @@
             pltpu.VMEM((chips, pair, width), jnp.bfloat16),
             pltpu.VMEM((chips, pair, held), jnp.float32),
             pltpu.VMEM((chips, pair, held), jnp.float32),
+            pltpu.VMEM((dps, chips, pair, held // dps), jnp.float32),
             DMA((4,)),
             DMA,
         ]
@@ -831,9 +844,9 @@
         )
 
     def bind(self, place, x_ref, shard, gate_at, up_at, grad_at, *refs):
-        hn, full, inner, dgate, dup, gate_w, up_w, grads, slope, silu = refs[:10]
-        loads, own_line = refs[10:12]
-        line_sems, ring_refs = refs[12:18], refs[18:]
+        hn, full, inner, dgate, dup, gate_w, up_w, grads, slope, silu, dinner = refs[:11]
+        loads, own_line = refs[11:13]
+        line_sems, ring_refs = refs[13:19], refs[19:]
         chip, chips = place.chip, place.chips
         pair, held = inner.shape[1:]
         width = gate_w.shape[1]
@@ -880,8 +893,26 @@
                 arrived(at)
                 forward(at)
 
+        chunk = held // place.dps
+        early = chunk % 128 == 0
+
+        def back(owner, part):
+            def each(at, _):
+                dinner[owner, at] = lax.dot_general(
+                    grads[at], part, contract_cols, preferred_element_type=jnp.float32
+                )
+                return 0
+
+            lax.fori_loop(0, chips, each, 0)
+
+        def back_from(owner):
+            back(owner, full[owner].reshape(chunk, width))
+
         def tick(hop, half):
             step(hop, half)
+            if early and hop == 1 and half == 1:
+                copies[2].wait()
+                back(place.d, shard[...].reshape(chunk, width))
             if hop == 1 and half == 0:
                 own.wait()
                 copies[0].wait()
@@ -897,15 +928,38 @@
             last = chips - 1
             when_there(chip - last, chip - last >= 0)
             when_there(chip + last, chip + last < chips)
-            copies[2].wait()
             copies[3].wait()
-            ring[2]()
-
-            def back(at, _):
+            if not early:
+                copies[2].wait()
+                ring[2]()
+                last_all()
+            else:
+                ring[2](True)
+                if place.hops > 2:
+                    back_between()
+                back_from(place.ring(place.hops))
+
+                def each(at, _):
+                    for q in range(place.dps):
+                        span = slice(q * chunk, (q + 1) * chunk)
+                        grad = dinner[q, at]
+                        dgate[at, :, span] = (grad * slope[at, :, span]).astype(jnp.bfloat16)
+                        dup[at, :, span] = (grad * silu[at, :, span]).astype(jnp.bfloat16)
+                    return 0
+
+                lax.fori_loop(0, chips, each, 0)
+            sent()
+
+        def back_between():
+            for hop in range(1, place.hops):
+                back_from(place.ring(hop))
+                back_from(place.ring(-hop))
+
+        def last_all():
+            def each(at, _):
                 rows = grads[at]
                 for first in range(0, held, wide):
                     span = slice(first, first + wide)
-                    chunk = full.shape[1] * full.shape[2]
                     part = full[first // chunk : (first + wide) // chunk].reshape(wide, width)
                     grad = lax.dot_general(
                         rows, part, contract_cols, preferred_element_type=jnp.float32
@@ -914,8 +968,7 @@
                     dup[at, :, span] = (grad * silu[at, :, span]).astype(jnp.bfloat16)
                 return 0
 
-            lax.fori_loop(0, chips, back, 0)
-            sent()
+            lax.fori_loop(0, chips, each, 0)
 
         ticks = {
             (hop - 1) * SUB + half: functools.partial(tick, hop, half)
@@ -927,9 +980,17 @@
             ticks[tick]()
             ring[1](hop)
 
+        def with_near(tick):
+            ticks[tick]()
+            ring[3]()
+            if place.hops == 2:
+                back_between()
+
         merged = dict(ticks)
         for hop in range(1, place.hops):
             merged[2 * hop - 1] = functools.partial(with_ring, 2 * hop - 1, hop)
+        if early:
+            merged[2 * place.hops - 1] = functools.partial(with_near, 2 * place.hops - 1)
         return start, merged, finish
 
 
@@ -1444,7 +1505,7 @@
             ColumnsBack(qkv_term, order, local_width, kv_copies, weight_rows, dps, groups),
             LineScatter(partial.astype(jnp.bfloat16), dps, groups),
             RowsBack(out_term, weight_rows, dps, groups),
-            RingScatter(up_term, dps, groups),
+            RingScatter(up_term, dps, groups, late=True),
             Spread(terms, True, dps, groups),
         ],
         dps,

time: 477 us -> 456 us (0.956)
  Pallas kernels: 355 us -> 336 us
    pallas_call x6, Pallas kernels: 355 us -> 336 us  [move(): pl.pallas_call(kernel, out_shape=[out for part in parts for out in part.o...]
  transfers between devices with their start and end apart: 2 -> 2, of which waited for: 0 -> 0; matrix products, arithmetic and copies ran while one was open for 16% -> 17% of each run, Pallas kernels for 26% -> 26%
where the time goes in v4:
time: 456 us; the launch traced here: 452 us
  Pallas kernels  336 us (74%)
  matrix products  40.6 us (9%)
  other arithmetic  40.2 us (9%)
  local copies, waits for them, and re-layouts  19.7 us (4%)
  between operations  15.2 us (3%)
    pallas_call x6, Pallas kernels, move(): pl.pallas_call(kernel, out_shape=[out for part in parts for out in part.o...  336 us
    unnamed x102, local copies, waits for them, and re-layouts  9.45 us
  transfers between devices with their start and end apart: 2, of which 0 were waited for; matrix products, arithmetic and copies ran while one was open for 17% of the time, Pallas kernels for 26%

profile of v4, /device:TPU:0, one launch (start us, length us, event | category | flops | bytes accessed | tf_op | source)
XLA Modules:
  0.0 452.3 jit_solution(7026812465367222808)
XLA Ops:
  7.2 0.9 fusion.83
  8.1 1.0 slice.255
  13.5 69.5 %move_1.1 = (bf16[4,8,64,384]{3,2,1,0:T(8,128)(2,1)}, bf16[8,2,64,2048]{3,2,1,0:T(8,128)(2,1)}, bf16[4,2,32,2048]{3,2,1,0:T(8,128)(2,1)}, bf16[4,2,128,2048]{3,2,1,0:T(8,128)(2,1)}, f32[32,8,128]{2,1,0:T(8,128)}) custom-call(bf16[8,64,384]{2,1,0:T(8,128)(2,1)} %copy-done.23, bf16[2,64,2048]{2,1,0:T(8,128)(2,1)} %bitcast.297, bf16[2,32,2048]{2,1,0:T(8,128)(2,1)} %bitcast.347, ...), custom_call_target="tpu_custom_call" | custom-call | bytes 120000000 | tf_op jit(solution)/shard_map/move_1/pallas_call | solution.py:1242
  83.2 0.9 copy.51
  84.2 3.1 multiply_reduce_fusion
  88.0 3.6 multiply_convert_fusion
  91.7 1.9 fusion.87
  93.6 1.1 slice_reduce_fusion
  96.2 1.2 fusion.63
  97.6 0.9 fusion.11
  98.5 0.9 exponential_reduce_fusion.1
  99.9 1.5 fusion.6
  101.4 2.1 exponential_reduce_fusion
  103.5 1.3 fusion.19
  104.8 2.4 fusion.14
  108.1 3.4 convolution_convert_fusion.1
  111.5 46.5 %move_2.1 = (f32[2,64,2048]{2,1,0:T(8,128)}, bf16[4,2,128,2048]{3,2,1,0:T(8,128)(2,1)}) custom-call(bf16[8,2,64,2048]{3,2,1,0:T(8,128)(2,1)} %bitcast.296, bf16[2,128,2048]{2,1,0:T(8,128)(2,1)} %bitcast.330), custom_call_target="tpu_custom_call" | custom-call | bytes 120000000 | tf_op jit(solution)/shard_map/move_2/pallas_call | solution.py:1242
  158.0 1.5 multiply_reduce_fusion.4
  160.1 2.2 multiply_convert_fusion.1.refs_0_
  162.3 5.2 %fusion.4 = bf16[1024,2048]{1,0:T(8,128)(2,1)} fusion(f32[2048]{0:T(1024)} %copy-done.24, f32[1024]{0:T(1024)} %rsqrt.42, bf16[8,2,64,2048]{3,2,1,0:T(8,128)(2,1)} %get-tuple-element.124), kind=kLoop, calls=%fused_computation.7 | loop fusion | flops 8388608 | bytes 8400896 | tf_op jit(solution)/shard_map/convert_element_type | solution.py:1366
  167.6 55.0 %move_3.1 = (bf16[8,2,64,2048]{3,2,1,0:T(8,128)(2,1)}, bf16[4,2,128,2048]{3,2,1,0:T(8,128)(2,1)}, bf16[4,256,1024]{2,1,0:T(8,128)(2,1)}, bf16[4,256,1024]{2,1,0:T(8,128)(2,1)}, bf16[4,256,1024]{2,1,0:T(8,128)(2,1)}) custom-call(bf16[2,64,2048]{2,1,0:T(8,128)(2,1)} %multiply_convert_fusion.1.refs_0_, bf16[2,128,2048]{2,1,0:T(8,128)(2,1)} %bitcast.331, ...), custom_call_target="tpu_custom_call" | custom-call | bytes 120000000 | tf_op jit(solution)/shard_map/move_3/pallas_call | solution.py:1242
  222.5 48.3 %move_4.1 = (f32[2,64,2048]{2,1,0:T(8,128)}, f32[2,128,2048]{2,1,0:T(8,128)}, bf16[4,2,2,64,2048]{4,3,2,1,0:T(8,128)(2,1)}, bf16[4,2,2,64,2048]{4,3,2,1,0:T(8,128)(2,1)}, bf16[4,2,2,64,2048]{4,3,2,1,0:T(8,128)(2,1)}) custom-call(bf16[1024,1024]{1,0:T(8,128)(2,1)} %bitcast.324, bf16[1024,1024]{1,0:T(8,128)(2,1)} %bitcast.325, bf16[1024,1024]{1,0:T(8,128)(2,1)} %bitcast.326, ...), custom_call_target="tpu_custom_call" | custom-call | bytes 120000000 | tf_op jit(solution)/shard_map/move_4/pallas_call | solution.py:1242
  270.9 2.4 multiply_reduce_fusion.2
  273.4 3.9 fusion.80
  277.3 47.0 %move_5.1 = (bf16[8,2,64,2048]{3,2,1,0:T(8,128)(2,1)}, f32[2,128,2048]{2,1,0:T(8,128)}) custom-call(bf16[2,64,2048]{2,1,0:T(8,128)(2,1)} %bitcast.318, bf16[4,2,128,2048]{3,2,1,0:T(8,128)(2,1)} %bitcast.307), custom_call_target="tpu_custom_call" | custom-call | bytes 120000000 | tf_op jit(solution)/shard_map/move_5/pallas_call | solution.py:1242
  324.3 1.2 copy-done.17
  325.5 4.3 convolution_convert_fusion.4
  329.9 1.1 fusion.82
  331.0 3.9 fusion.7
  335.0 1.3 fusion.9
  337.6 3.8 fusion
  341.4 2.8 fusion.2
  344.3 1.4 fusion.18
  346.7 0.8 fusion.13
  347.8 1.2 convolution_bitcast_fusion.2
  349.1 2.4 fusion.20
  351.8 3.7 multiply_reduce_fusion.1
  356.4 4.3 convolution_convert_fusion
  360.7 2.2 convolution_convert_fusion.3
  362.9 69.9 %move_6.1 = (f32[64,3072]{1,0:T(8,128)}, f32[2,64,2048]{2,1,0:T(8,128)}, f32[2,32,2048]{2,1,0:T(8,128)}, f32[2,128,2048]{2,1,0:T(8,128)}, f32[8,128]{1,0:T(8,128)}) custom-call(bf16[4,2,4,64,384]{4,3,2,1,0:T(8,128)(2,1)} %bitcast.327, bf16[8,2,64,2048]{3,2,1,0:T(8,128)(2,1)} %bitcast.311, bf16[4,2,32,2048]{3,2,1,0:T(8,128)(2,1)} %bitcast.338, ...), custom_call_target="tpu_custom_call" | custom-call | bytes 120000000 | tf_op jit(solution)/shard_map/move_6/pallas_call | solution.py:1242
  432.9 1.5 fusion.22
  434.5 1.3 slice_bitcast_fusion.7
  435.8 3.7 fusion.27
  439.5 0.9 copy.130
  440.4 0.8 copy.131
  441.2 1.3 copy.132
  442.5 1.3 copy.133
  443.9 1.3 copy.134
  (167 shorter events, 12.8 us)
Async XLA Ops:
  7.2 160.4 %all-gather.2.cloned.1.call-start = ((), (), s32[]{:S(2)}) async-start(), calls=%async_computation.1 | async-start | bytes 4718592 | tf_op jit(solution)/shard_map/all_gather | solution.py:1369
  83.0 352.8 %reduce-scatter.2.cloned.1.call-start = ((), (), s32[]{:S(2)}) async-start(), calls=%async_computation.2 | async-start | bytes 4718592 | tf_op jit(solution)/shard_map/reduce_scatter | solution.py:1447
  87.9 3.7 copy-start.26
  88.0 3.7 copy-start.24
  88.0 3.7 copy-start.43
  93.6 11.2 %copy-start.34 = (bf16[1024,384]{0,1:T(8,128)(2,1)}, bf16[1024,384]{0,1:T(8,128)(2,1)S(1)}, u32[]{:S(2)}) copy-start(bf16[1024,384]{0,1:T(8,128)(2,1)S(1)} %get-tuple-element.201) | copy-start | bytes 2359300
  95.5 3.0 copy-start.38
  95.5 3.0 copy-start.32
  96.2 3.7 copy-start.19
  97.6 2.3 copy-start.9
  97.6 2.3 copy-start.11
  98.5 5.0 %copy-start.1 = (f32[512,512,4]{1,0,2:T(8,128)}, f32[512,512,4]{1,0,2:T(8,128)S(1)}, u32[]{:S(2)}) copy-start(f32[512,512,4]{1,0,2:T(8,128)S(1)} %get-tuple-element.206) | copy-start | bytes 12582916
  99.4 4.1 copy-start.30
  99.8 5.0 %copy-start.4 = (pred[512,1024]{0,1:T(8,128)(4,1)}, pred[512,1024]{0,1:T(8,128)(4,1)S(1)}, u32[]{:S(2)}) copy-start(pred[512,1024]{0,1:T(8,128)(4,1)S(1)} %iota_compare_fusion) | copy-start | bytes 1572868
  101.4 3.4 copy-start
  103.5 3.7 copy-start.28
  104.8 3.3 copy-start.16
  107.3 0.8 copy-start.7
  111.5 46.5 %copy-start.3 = (bf16[1,128,2048]{2,1,0:T(8,128)(2,1)S(1)}, bf16[1,128,2048]{2,1,0:T(8,128)(2,1)}, u32[]{:S(2)}) copy-start(bf16[1,128,2048]{2,1,0:T(8,128)(2,1)} %param.25) | copy-start | bytes 1572868
  159.5 8.1 %copy-start.37 = (f32[2,64]{1,0:T(2,128)}, f32[2,64]{1,0:T(2,128)S(1)}, u32[]{:S(2)}) copy-start(f32[2,64]{1,0:T(2,128)S(1)} %add_rsqrt_fusion.1) | copy-start | bytes 1540
  159.6 8.0 %copy-start.41 = (f32[128]{0:T(128)}, f32[128]{0:T(128)S(1)}, u32[]{:S(2)}) copy-start(f32[128]{0:T(128)S(1)} %rsqrt.40) | copy-start | bytes 1540
  324.3 1.2 copy-start.17
  325.5 4.3 copy-start.35
  325.5 5.4 %copy-start.31 = (f32[4,512]{1,0:T(4,128)S(1)}, f32[4,512]{1,0:T(4,128)}, u32[]{:S(2)}) copy-start(f32[4,512]{1,0:T(4,128)} %copy-done.30) | copy-start | bytes 24580
  331.0 3.9 copy-start.2
  331.0 6.1 %slice-start = ((s8[8388608]{0:T(1024)(128)(4,1)}), s8[4194304]{0:T(1024)(128)(4,1)S(1)}, s32[]{:S(2)}) async-start(s8[8388608]{0:T(1024)(128)(4,1)} %bitcast.294), calls=%async_computation.3 | async-start | bytes 8388608
  334.9 1.4 copy-start.10
  334.9 1.4 copy-start.12
  334.9 2.6 slice-start.1
  334.9 2.6 copy-start.5
  335.0 2.6 copy-start.29
  344.2 1.4 copy-start.33
  344.2 1.4 copy-start.39
  344.2 2.0 copy-start.20
  345.7 1.9 copy-start.21
  349.0 2.4 copy-start.6
  349.0 2.7 copy-start.44
  351.8 3.8 copy-start.27
  351.8 4.6 %copy-start.45 = (bf16[4,8,64,384]{3,2,1,0:T(8,128)(2,1)S(1)}, bf16[4,8,64,384]{3,2,1,0:T(8,128)(2,1)}, u32[]{:S(2)}) copy-start(bf16[4,8,64,384]{3,2,1,0:T(8,128)(2,1)} %get-tuple-element.126) | copy-start | bytes 4718596
  356.4 4.3 copy-start.8
  356.4 4.3 copy-start.42
  362.9 69.9 %copy-start.25 = (f32[2048]{0:T(1024)S(1)}, f32[2048]{0:T(1024)}, u32[]{:S(2)}) copy-start(f32[2048]{0:T(1024)} %copy-done.24) | copy-start | bytes 24580
  362.9 71.6 %copy-start.40 = (f32[128]{0:T(128)S(1)}, f32[128]{0:T(128)}, u32[]{:S(2)}) copy-start(f32[128]{0:T(128)} %get-tuple-element.161) | copy-start | bytes 1540
  432.8 6.7 %copy-start.18 = (f32[64,3072]{1,0:T(8,128)S(1)}, f32[64,3072]{1,0:T(8,128)}, u32[]{:S(2)}) copy-start(f32[64,3072]{1,0:T(8,128)} %get-tuple-element.248) | copy-start | bytes 2359300
  432.9 7.6 %copy-start.22 = (f32[2,32,2048]{2,1,0:T(8,128)S(1)}, f32[2,32,2048]{2,1,0:T(8,128)}, u32[]{:S(2)}) copy-start(f32[2,32,2048]{2,1,0:T(8,128)} %get-tuple-element.146) | copy-start | bytes 1572868
  435.8 5.4 %copy-start.14 = (f32[2,128,2048]{2,1,0:T(8,128)S(1)}, f32[2,128,2048]{2,1,0:T(8,128)}, u32[]{:S(2)}) copy-start(f32[2,128,2048]{2,1,0:T(8,128)} %get-tuple-element.147) | copy-start | bytes 6291460
  439.5 3.0 copy-start.15
  441.2 2.6 copy-start.13
  (2 other events, 1.4 us)
Sparse Core Ops, SparseCore 0:
  83.1 45.5 all-gather.1
  324.5 48.0 reduce-scatter.1

commit v5 on v4

--- a/solution.py
+++ b/solution.py
@@ -175,16 +175,31 @@
 
 
 class LineGather:
-    def __init__(self, x, dps, groups):
+    def __init__(self, x, dps, groups, normed=False):
         rows, width = x.shape
         shape = (SUB, rows // SUB, width)
+        self.normed = normed
         self.inputs, self.in_specs = [x.reshape(shape)], [VM]
         self.outs, self.out_specs = [jax.ShapeDtypeStruct((groups,) + shape, x.dtype)], [ANY]
         self.scratch = [DMA] + [DMA((groups // 2, SUB))] * 6
+        if normed:
+            self.scratch = [pltpu.VMEM(shape, x.dtype)] + self.scratch
         self.result = lambda out: out.reshape(groups * rows, width)
 
-    def bind(self, place, *refs):
-        own, start, step, arrived, sent = line_gather(place, *refs)
+    def bind(self, place, x_ref, out_ref, *refs):
+        if self.normed:
+            source, x_ref, refs = x_ref, refs[0], refs[1:]
+            many = 16 if x_ref.shape[1] % 16 == 0 else x_ref.shape[1]
+
+            def norm(i, _):
+                span = pl.ds(pl.multiple_of(i * many, many), many)
+                for half in range(SUB):
+                    values = source[half, span, :].astype(jnp.float32)
+                    x_ref[half, span, :] = (values * norm_factor(values)).astype(x_ref.dtype)
+                return 0
+
+            lax.fori_loop(0, x_ref.shape[1] // many, norm, 0)
+        own, start, step, arrived, sent = line_gather(place, x_ref, out_ref, *refs)
 
         def finish():
             own.wait()
@@ -357,10 +372,13 @@
             src, out(chunk, half), ls.at[hop - 1, half], lr.at[hop - 1, half], dp=place.ring(-1)
         )
 
+    def begin(half):
+        right(own(half), place.d, 1, half).start()
+        left(own(1 - half), place.d, 1, 1 - half).start()
+
     def start():
-        for half in range(2):
-            right(own(half), place.d, 1, half).start()
-            left(own(1 - half), place.d, 1, 1 - half).start()
+        begin(0)
+        begin(1)
 
     def forward(hop):
         before, after = place.ring(-hop), place.ring(hop)
@@ -392,7 +410,7 @@
                 if hop < hops or half == 1:
                     left(out(place.d, half), place.d, hop, half).wait_send()
 
-    return start, forward, finish, near
+    return start, forward, finish, near, begin
 
 
 def ring_scatter(place, part, put, rbuf, lbuf, rout, lout, rs, rr, ls, lr):
@@ -463,7 +481,8 @@
 
 
 class RingGather:
-    def __init__(self, x, dps, groups):
+    def __init__(self, x, dps, groups, late=False):
+        self.late = late
         rows, width = x.shape
         shape = (2, rows // 2, width)
         self.inputs, self.in_specs = [x.reshape(shape)], [VM]
@@ -478,14 +497,21 @@
         )
 
         def start():
-            ring[0]()
+            if not self.late:
+                ring[0]()
             own.start()
 
         def finish():
             own.wait()
             ring[2]()
 
-        ticks = {2 * hop - 1: functools.partial(ring[1], hop) for hop in range(1, place.hops)}
+        first = 3 if self.late else -1
+        ticks = {
+            2 * hop + first: functools.partial(ring[1], hop) for hop in range(1, place.hops)
+        }
+        if self.late:
+            ticks[1] = functools.partial(ring[4], 0)
+            ticks[3] = functools.partial(ring[4], 1)
         return start, ticks, finish
 
 
@@ -698,7 +724,7 @@
                 swap(i).wait_send()
 
         ticks = {2 * hop - 1: functools.partial(ring[1], hop) for hop in range(1, place.hops)}
-        ticks[2 * place.hops] = last
+        ticks[2 * place.hops - 1] = last
         return start, ticks, finish
 
 
@@ -1344,12 +1370,12 @@
     tile = jnp.zeros((8, 128), jnp.float32)
     tile = tile.at[0, :gain_width].set(attn_gain.astype(jnp.float32))
     tile = tile.at[1, :gain_width].set(mlp_gain.astype(jnp.float32))
-    qkv_local, tokens_all, out_rows, gate_part, gains = move(
+    qkv_local, out_rows, normed_all, gate_part, gains = move(
         [
             Columns(columns, dps, groups),
-            LineGather(tokens[0], dps, groups),
             Rows(out_weight, dps, groups),
-            RingGather(gate_weight, dps, groups),
+            LineGather(tokens[0], dps, groups, normed=True),
+            RingGather(gate_weight, dps, groups, late=True),
             Spread(tile, False, dps, groups),
         ],
         dps,
@@ -1362,13 +1388,12 @@
 
     x_rows = tokens[0].astype(jnp.float32)
     factor_one = norm_factor(x_rows)
-    all_rows = tokens_all.astype(jnp.float32)
-    normed_all = (all_rows * norm_factor(all_rows) * gain_one).astype(jnp.bfloat16)
+    qkv_gained = (qkv_local.astype(jnp.float32) * gain_one[:, None]).astype(jnp.bfloat16)
     grad_low = cotangent[0]
     grad_low, _ = lax.optimization_barrier((grad_low, gains))
     grad_all = lax.all_gather(grad_low, "seq", axis=0, tiled=True)
 
-    mixed = jnp.dot(normed_all, qkv_local, preferred_element_type=jnp.float32)
+    mixed = jnp.dot(normed_all, qkv_gained, preferred_element_type=jnp.float32)
     cosine_table, sine_table = rope_tables(jnp.arange(seq_len, dtype=jnp.int32), HEAD_DIM)
     query_heads = rotate(
         mixed[:, :local_width].reshape(seq_len, local_heads, HEAD_DIM), cosine_table, sine_table
@@ -1494,10 +1519,8 @@
     partial = lax.dot_general(
         grad_mixed, qkv_local, contract_cols, preferred_element_type=jnp.float32
     )
-    qkv_term = qkv_term.astype(jnp.bfloat16)
-    gain_one_term = (
-        jnp.sum(qkv_term.astype(jnp.float32) * qkv_local.astype(jnp.float32), axis=1) / gain_one
-    )
+    gain_one_term = jnp.sum(qkv_term * qkv_local.astype(jnp.float32), axis=1)
+    qkv_term = (qkv_term * gain_one[:, None]).astype(jnp.bfloat16)
     terms = jnp.stack([gain_one_term, gain_two_term]).reshape(2, dps * groups, gain_width)
     terms = jnp.pad(terms.transpose(1, 0, 2), ((0, 0), (0, 6), (0, 128 - gain_width)))
     qkv_owned, grad_normed_one, out_owned, up_owned, gain_grads = move(

time: 456 us -> 466 us (1.022); the launches traced: 452 us -> 458 us
  Pallas kernels: 336 us -> 350 us
  other arithmetic: 40.2 us -> 30 us
    pallas_call x6, Pallas kernels: 336 us -> 350 us  [move(): pl.pallas_call(kernel, out_shape=[out for part in parts for out in part.o...]
    convert_element_type x2 -> x1, other arithmetic: 8.89 us -> 1.78 us  [per_device(): (qkv_local.astype(jnp.float32) * gain_one[:, None]).astype(jnp.bfloat16)]
    unnamed x102 -> x98, local copies, waits for them, and re-layouts: 9.45 us -> 9.43 us
  transfers between devices with their start and end apart: 2 -> 2, of which waited for: 0 -> 0; matrix products, arithmetic and copies ran while one was open for 17% -> 15% of each run, Pallas kernels for 26% -> 26%
where the time goes in v5:
time: 466 us; the launch traced here: 458 us
  Pallas kernels  350 us (75%)
  matrix products  44.2 us (9%)
  other arithmetic  30 us (6%)
  local copies, waits for them, and re-layouts  18.2 us (4%)
  between operations  15.4 us (3%)
    pallas_call x6, Pallas kernels, move(): pl.pallas_call(kernel, out_shape=[out for part in parts for out in part.o...  350 us
    unnamed x98, local copies, waits for them, and re-layouts  9.43 us
  transfers between devices with their start and end apart: 2, of which 0 were waited for; matrix products, arithmetic and copies ran while one was open for 15% of the time, Pallas kernels for 26%

profile of v5, /device:TPU:0, one launch (start us, length us, event | category | flops | bytes accessed | tf_op | source)
XLA Modules:
  0.0 457.6 jit_solution(2751038978251926851)
XLA Ops:
  7.2 0.9 fusion.82
  8.1 1.0 slice.255
  12.8 0.7 copy-done.24
  13.5 80.1 %move_1.1 = (bf16[4,8,64,384]{3,2,1,0:T(8,128)(2,1)}, bf16[4,2,32,2048]{3,2,1,0:T(8,128)(2,1)}, bf16[8,2,64,2048]{3,2,1,0:T(8,128)(2,1)}, bf16[4,2,128,2048]{3,2,1,0:T(8,128)(2,1)}, f32[32,8,128]{2,1,0:T(8,128)}) custom-call(bf16[8,64,384]{2,1,0:T(8,128)(2,1)} %copy-done.24, bf16[2,32,2048]{2,1,0:T(8,128)(2,1)} %bitcast.341, bf16[2,64,2048]{2,1,0:T(8,128)(2,1)} %bitcast.290, ...), custom_call_target="tpu_custom_call" | custom-call | bytes 120000000 | tf_op jit(solution)/shard_map/move_1/pallas_call | solution.py:1268
  93.7 1.1 slice_reduce_fusion.1
  96.1 1.8 multiply_convert_fusion.1
  97.9 4.5 fusion.86
  103.2 1.2 fusion.62
  104.6 0.9 fusion.9
  105.5 0.9 exponential_reduce_fusion.1
  106.9 1.5 fusion.4
  108.5 2.1 exponential_reduce_fusion
  110.6 1.3 fusion.17
  111.9 2.4 fusion.12
  114.3 0.8 copy-done.6
  115.1 3.4 convolution_convert_fusion.1
  118.5 50.1 %move_2.1 = (f32[2,64,2048]{2,1,0:T(8,128)}, bf16[4,2,128,2048]{3,2,1,0:T(8,128)(2,1)}) custom-call(bf16[8,2,64,2048]{3,2,1,0:T(8,128)(2,1)} %bitcast.289, bf16[2,128,2048]{2,1,0:T(8,128)(2,1)} %bitcast.324), custom_call_target="tpu_custom_call" | custom-call | bytes 120000000 | tf_op jit(solution)/shard_map/move_2/pallas_call | solution.py:1268
  168.6 1.5 multiply_reduce_fusion.3
  170.7 2.2 multiply_convert_fusion.2.refs_0_
  172.9 54.5 %move_3.1 = (bf16[8,2,64,2048]{3,2,1,0:T(8,128)(2,1)}, bf16[4,2,128,2048]{3,2,1,0:T(8,128)(2,1)}, bf16[4,256,1024]{2,1,0:T(8,128)(2,1)}, bf16[4,256,1024]{2,1,0:T(8,128)(2,1)}, bf16[4,256,1024]{2,1,0:T(8,128)(2,1)}) custom-call(bf16[2,64,2048]{2,1,0:T(8,128)(2,1)} %multiply_convert_fusion.2.refs_0_, bf16[2,128,2048]{2,1,0:T(8,128)(2,1)} %bitcast.325, ...), custom_call_target="tpu_custom_call" | custom-call | bytes 120000000 | tf_op jit(solution)/shard_map/move_3/pallas_call | solution.py:1268
  227.3 48.4 %move_4.1 = (f32[2,64,2048]{2,1,0:T(8,128)}, f32[2,128,2048]{2,1,0:T(8,128)}, bf16[4,2,2,64,2048]{4,3,2,1,0:T(8,128)(2,1)}, bf16[4,2,2,64,2048]{4,3,2,1,0:T(8,128)(2,1)}, bf16[4,2,2,64,2048]{4,3,2,1,0:T(8,128)(2,1)}) custom-call(bf16[1024,1024]{1,0:T(8,128)(2,1)} %bitcast.316, bf16[1024,1024]{1,0:T(8,128)(2,1)} %bitcast.317, bf16[1024,1024]{1,0:T(8,128)(2,1)} %bitcast.318, ...), custom_call_target="tpu_custom_call" | custom-call | bytes 120000000 | tf_op jit(solution)/shard_map/move_4/pallas_call | solution.py:1268
  275.7 2.4 multiply_reduce_fusion.1
  278.3 4.0 fusion.79
  282.2 46.5 %move_5.1 = (bf16[8,2,64,2048]{3,2,1,0:T(8,128)(2,1)}, f32[2,128,2048]{2,1,0:T(8,128)}) custom-call(bf16[2,64,2048]{2,1,0:T(8,128)(2,1)} %bitcast.310, bf16[4,2,128,2048]{3,2,1,0:T(8,128)(2,1)} %bitcast.300), custom_call_target="tpu_custom_call" | custom-call | bytes 120000000 | tf_op jit(solution)/shard_map/move_5/pallas_call | solution.py:1268
  328.8 1.2 copy-done.17
  330.0 3.5 convolution_convert_fusion.3
  333.5 0.7 stack.46
  334.3 3.9 fusion.5
  338.2 1.3 fusion.7
  339.5 0.8 fusion.19
  340.8 3.8 fusion
  344.6 2.8 fusion.2
  347.4 1.4 fusion.16
  349.9 0.8 fusion.11
  351.0 1.2 convolution_bitcast_fusion.2
  352.3 2.4 fusion.18
  355.0 4.2 multiply_reduce_fusion
  360.0 5.7 %convolution_convert_fusion = bf16[1024,2048]{1,0:T(8,128)(2,1)} fusion(bf16[2048,384]{1,0:T(8,128)(2,1)S(1)} %bitcast.319, bf16[1024,64]{0,1:T(8,128)(2,1)S(1)} %fusion.18, bf16[1024,64]{0,1:T(8,128)(2,1)} %copy-done.25, bf16[1024,256]{0,1:T(8,128)(2,1)} %bitcast.340), kind=kOutput, calls=%fused_computation.18 | convolution fusion | flops 1615069184 | bytes 6553600 | tf_op jit(solution)/shard_map/dot_general | solution.py:1519
  365.7 2.2 convolution_convert_fusion.2
  367.9 70.0 %move_6.1 = (f32[64,3072]{1,0:T(8,128)}, f32[2,64,2048]{2,1,0:T(8,128)}, f32[2,32,2048]{2,1,0:T(8,128)}, f32[2,128,2048]{2,1,0:T(8,128)}, f32[8,128]{1,0:T(8,128)}) custom-call(bf16[4,2,4,64,384]{4,3,2,1,0:T(8,128)(2,1)} %bitcast.321, bf16[8,2,64,2048]{3,2,1,0:T(8,128)(2,1)} %bitcast.304, bf16[4,2,32,2048]{3,2,1,0:T(8,128)(2,1)} %bitcast.332, ...), custom_call_target="tpu_custom_call" | custom-call | bytes 120000000 | tf_op jit(solution)/shard_map/move_6/pallas_call | solution.py:1268
  437.9 1.6 fusion.20
  439.6 1.3 slice_bitcast_fusion.7
  440.9 3.7 fusion.25
  444.6 0.9 copy.128
  445.5 0.8 copy.129
  446.3 1.3 copy.130
  447.6 1.3 copy.131
  449.0 1.3 copy.132
  (156 shorter events, 10.2 us)
Async XLA Ops:
  7.2 165.7 %all-gather.2.cloned.1.call-start = ((), (), s32[]{:S(2)}) async-start(), calls=%async_computation.1 | async-start | bytes 4718592 | tf_op jit(solution)/shard_map/all_gather | solution.py:1394
  12.1 0.7 copy-start.36
  12.8 0.7 copy-start.24
  93.7 347.2 %reduce-scatter.2.cloned.1.call-start = ((), (), s32[]{:S(2)}) async-start(), calls=%async_computation.2 | async-start | bytes 4718592 | tf_op jit(solution)/shard_map/reduce_scatter | solution.py:1472
  102.4 9.4 %copy-start.34 = (bf16[1024,384]{0,1:T(8,128)(2,1)}, bf16[1024,384]{0,1:T(8,128)(2,1)S(1)}, u32[]{:S(2)}) copy-start(bf16[1024,384]{0,1:T(8,128)(2,1)S(1)} %get-tuple-element.206) | copy-start | bytes 2359300
  102.5 3.0 copy-start.38
  102.5 1.9 copy-start.31
  103.2 3.6 copy-start.19
  104.6 2.3 copy-start.8
  104.6 2.3 copy-start.10
  105.5 5.0 %copy-start.1 = (f32[512,512,4]{1,0,2:T(8,128)}, f32[512,512,4]{1,0,2:T(8,128)S(1)}, u32[]{:S(2)}) copy-start(f32[512,512,4]{1,0,2:T(8,128)S(1)} %get-tuple-element.211) | copy-start | bytes 12582916
  106.5 4.1 copy-start.29
  106.9 5.0 %copy-start.4 = (pred[512,1024]{0,1:T(8,128)(4,1)}, pred[512,1024]{0,1:T(8,128)(4,1)S(1)}, u32[]{:S(2)}) copy-start(pred[512,1024]{0,1:T(8,128)(4,1)S(1)} %iota_compare_fusion) | copy-start | bytes 1572868
  108.4 3.4 copy-start
  110.5 3.7 copy-start.26
  111.9 3.3 copy-start.16
  114.3 0.8 copy-start.6
  118.5 50.1 %copy-start.3 = (bf16[1,128,2048]{2,1,0:T(8,128)(2,1)S(1)}, bf16[1,128,2048]{2,1,0:T(8,128)(2,1)}, u32[]{:S(2)}) copy-start(bf16[1,128,2048]{2,1,0:T(8,128)(2,1)} %param.25) | copy-start | bytes 1572868
  170.0 0.6 copy-start.37
  170.1 2.7 copy-start.41
  328.8 1.2 copy-start.17
  330.0 3.5 copy-start.35
  330.0 4.2 copy-start.30
  334.2 3.9 copy-start.2
  334.2 6.0 %slice-start = ((s8[8388608]{0:T(1024)(128)(4,1)}), s8[4194304]{0:T(1024)(128)(4,1)S(1)}, s32[]{:S(2)}) async-start(s8[8388608]{0:T(1024)(128)(4,1)} %bitcast.287), calls=%async_computation.3 | async-start | bytes 8388608
  338.1 1.4 copy-start.9
  338.1 1.4 copy-start.11
  338.1 2.6 slice-start.1
  338.2 2.6 copy-start.5
  338.2 2.6 copy-start.27
  347.4 1.4 copy-start.32
  347.4 1.4 copy-start.39
  347.4 2.0 copy-start.20
  348.8 2.0 copy-start.21
  349.4 5.2 %copy-start.25 = (bf16[1024,64]{0,1:T(8,128)(2,1)}, bf16[1024,64]{0,1:T(8,128)(2,1)S(1)}, u32[]{:S(2)}) copy-start(bf16[1024,64]{0,1:T(8,128)(2,1)S(1)} %maximum_bitcast_fusion.1) | copy-start | bytes 393220
  351.0 3.7 copy-start.23
  352.2 2.4 copy-start.15
  352.2 2.4 copy-start.28
  352.3 2.7 copy-start.42
  355.0 4.3 copy-start.33
  360.0 5.7 %copy-start.7 = (bf16[1024,4,64]{0,2,1:T(8,128)(2,1)S(1)}, bf16[1024,4,64]{0,2,1:T(8,128)(2,1)}, u32[]{:S(2)}) copy-start(bf16[1024,4,64]{0,2,1:T(8,128)(2,1)} %copy-done.6) | copy-start | bytes 1572868
  360.0 5.7 %copy-start.43 = (bf16[8,2,64,2048]{3,2,1,0:T(8,128)(2,1)S(1)}, bf16[8,2,64,2048]{3,2,1,0:T(8,128)(2,1)}, u32[]{:S(2)}) copy-start(bf16[8,2,64,2048]{3,2,1,0:T(8,128)(2,1)} %get-tuple-element.140) | copy-start | bytes 12582916
  367.9 71.6 %copy-start.40 = (f32[128]{0:T(128)S(1)}, f32[128]{0:T(128)}, u32[]{:S(2)}) copy-start(f32[128]{0:T(128)} %get-tuple-element.165) | copy-start | bytes 1540
  437.9 6.7 %copy-start.18 = (f32[64,3072]{1,0:T(8,128)S(1)}, f32[64,3072]{1,0:T(8,128)}, u32[]{:S(2)}) copy-start(f32[64,3072]{1,0:T(8,128)} %get-tuple-element.251) | copy-start | bytes 2359300
  437.9 7.6 %copy-start.22 = (f32[2,32,2048]{2,1,0:T(8,128)S(1)}, f32[2,32,2048]{2,1,0:T(8,128)}, u32[]{:S(2)}) copy-start(f32[2,32,2048]{2,1,0:T(8,128)} %get-tuple-element.146) | copy-start | bytes 1572868
  440.9 5.4 %copy-start.13 = (f32[2,128,2048]{2,1,0:T(8,128)S(1)}, f32[2,128,2048]{2,1,0:T(8,128)}, u32[]{:S(2)}) copy-start(f32[2,128,2048]{2,1,0:T(8,128)} %get-tuple-element.147) | copy-start | bytes 6291460
  444.6 3.0 copy-start.14
  446.3 2.6 copy-start.12
Sparse Core Ops, SparseCore 0:
  93.8 49.1 all-gather.1
  328.9 48.0 reduce-scatter.1

commit v6 on v5

--- a/solution.py
+++ b/solution.py
@@ -318,41 +318,59 @@
     return [pltpu.VMEM((chips,) + shape, jnp.bfloat16)] * 3 + [DMA((chips, SUB))] * 6
 
 
-class LineScatter:
-    def __init__(self, partial, dps, groups):
-        total, width = partial.shape
-        rows = total // groups
+class LineProduct:
+    def __init__(self, left, right, dims, dps, groups):
+        total, inner = left.shape
+        width = right.shape[1 - dims[0][1][0]]
+        rows, chips = total // groups, groups // 2
         shape = (SUB, rows // SUB, width)
-        self.inputs, self.in_specs = [partial.reshape((groups,) + shape)], [VM]
+        self.dims = dims
+        self.inputs, self.in_specs = [left.reshape(chips, 2 * rows, inner), right], [VM, VM]
         self.outs, self.out_specs = [jax.ShapeDtypeStruct(shape, jnp.float32)], [VM]
-        self.scratch = line_scatter_scratch(groups // 2, shape)
+        self.scratch = [pltpu.VMEM((groups,) + shape, jnp.bfloat16)]
+        self.scratch += line_scatter_scratch(chips, shape)
         self.result = lambda out: out.reshape(rows, width)
 
-    def bind(self, place, *refs):
-        send, step, finish = line_scatter(place, *refs)
+    def bind(self, place, left, right, out_ref, p_ref, *refs):
+        send, step, finish = line_scatter(place, p_ref, out_ref, *refs)
         chip, chips = place.chip, place.chips
-
-        def start():
-            def issue(low, _):
-                high = chips - 1 - low
-
-                @pl.when(high > chip)
-                def _():
-                    send(high)
-
-                @pl.when(low < chip)
-                def _():
-                    send(low)
-
-                return 0
-
-            lax.fori_loop(0, chips - 1, issue, 0)
-            send(chip)
+        width = p_ref.shape[3]
+        wide = 512 if width % 512 == 0 else width
+
+        def partial(at):
+            for first in range(0, width, wide):
+                span = slice(first, first + wide)
+                part = right[:, span] if self.dims[0][1][0] == 0 else right[span, :]
+                value = lax.dot_general(
+                    left[at], part, self.dims, preferred_element_type=jnp.float32
+                )
+                p_ref[pl.ds(2 * at, 2), :, :, span] = value.astype(jnp.bfloat16).reshape(
+                    (2,) + p_ref.shape[1:3] + (wide,)
+                )
+            send(at)
+
+        def partials(wave):
+            if wave == chips - 1:
+                partial(chip)
+                return
+
+            @pl.when(chips - 1 - wave > chip)
+            def _():
+                partial(chips - 1 - wave)
+
+            @pl.when(wave < chip)
+            def _():
+                partial(wave)
+
+        def tick(wave, half):
+            step(wave, half)
+            if half == SUB - 1:
+                partials(wave + 1)
 
         ticks = {
-            i: functools.partial(step, i // SUB, i % SUB) for i in range((chips - 1) * SUB)
+            i: functools.partial(tick, i // SUB, i % SUB) for i in range((chips - 1) * SUB)
         }
-        return start, ticks, finish
+        return lambda: partials(0), ticks, finish
 
 
 def ring_sems(hops):
@@ -497,21 +515,22 @@
         )
 
         def start():
+            ring[4](0)
             if not self.late:
-                ring[0]()
+                ring[4](1)
             own.start()
+
+        def second():
+            ring[4](1)
+            ring[1](1)
 
         def finish():
             own.wait()
             ring[2]()
 
-        first = 3 if self.late else -1
-        ticks = {
-            2 * hop + first: functools.partial(ring[1], hop) for hop in range(1, place.hops)
-        }
+        ticks = {2 * hop - 1: functools.partial(ring[1], hop) for hop in range(1, place.hops)}
         if self.late:
-            ticks[1] = functools.partial(ring[4], 0)
-            ticks[3] = functools.partial(ring[4], 1)
+            ticks[1] = second
         return start, ticks, finish
 
 
@@ -723,8 +742,8 @@
                 swap(i).wait_recv()
                 swap(i).wait_send()
 
-        ticks = {2 * hop - 1: functools.partial(ring[1], hop) for hop in range(1, place.hops)}
-        ticks[2 * place.hops - 1] = last
+        ticks = {2 * hop - 2: functools.partial(ring[1], hop) for hop in range(1, place.hops)}
+        ticks[2 * place.hops - 2] = last
         return start, ticks, finish
 
 
@@ -1417,11 +1436,10 @@
         outputs.append(attended.astype(jnp.bfloat16))
         log_sums.append(log_sum)
     attended = jnp.concatenate(outputs, axis=0).reshape(seq_len, local_width)
-    partial = jnp.dot(attended, out_rows, preferred_element_type=jnp.float32)
-    summed, up_part = move(
+    up_part, summed = move(
         [
-            LineScatter(partial.astype(jnp.bfloat16), dps, groups),
             RingGather(up_weight, dps, groups),
+            LineProduct(attended, out_rows, (((1,), (0,)), ((), ())), dps, groups),
         ],
         dps,
         groups,
@@ -1516,18 +1534,15 @@
     qkv_term = lax.dot_general(
         normed_all, grad_mixed, contract_rows, preferred_element_type=jnp.float32
     )
-    partial = lax.dot_general(
-        grad_mixed, qkv_local, contract_cols, preferred_element_type=jnp.float32
-    )
     gain_one_term = jnp.sum(qkv_term * qkv_local.astype(jnp.float32), axis=1)
     qkv_term = (qkv_term * gain_one[:, None]).astype(jnp.bfloat16)
     terms = jnp.stack([gain_one_term, gain_two_term]).reshape(2, dps * groups, gain_width)
     terms = jnp.pad(terms.transpose(1, 0, 2), ((0, 0), (0, 6), (0, 128 - gain_width)))
-    qkv_owned, grad_normed_one, out_owned, up_owned, gain_grads = move(
+    qkv_owned, out_owned, grad_normed_one, up_owned, gain_grads = move(
         [
             ColumnsBack(qkv_term, order, local_width, kv_copies, weight_rows, dps, groups),
-            LineScatter(partial.astype(jnp.bfloat16), dps, groups),
             RowsBack(out_term, weight_rows, dps, groups),
+            LineProduct(grad_mixed, qkv_local, contract_cols, dps, groups),
             RingScatter(up_term, dps, groups, late=True),
             Spread(terms, True, dps, groups),
         ],

time: 466 us -> 466 us (level)
  Pallas kernels: 350 us -> 342 us
  local copies, waits for them, and re-layouts: 18.2 us -> 25.3 us
    dot_general x2 -> x0, matrix products: 9.05 us -> none  [the longest x1 5.67 us: per_device(): lax.dot_general(grad_mixed, qkv_local, contract_cols, preferred_element_t...]
    pallas_call x6, Pallas kernels: 350 us -> 342 us  [move(): pl.pallas_call(kernel, out_shape=[out for part in parts for out in part.o...]
    unnamed x98 -> x104, local copies, waits for them, and re-layouts: 9.43 us -> 11.4 us
  transfers between devices with their start and end apart: 2 -> 2, of which waited for: 0 -> 0; matrix products, arithmetic and copies ran while one was open for 15% -> 16% of each run, Pallas kernels for 26% -> 27%
where the time goes in v6:
time: 466 us; the launch traced here: 457 us
  Pallas kernels  342 us (73%)
  matrix products  43.4 us (9%)
  other arithmetic  31.2 us (7%)
  local copies, waits for them, and re-layouts  25.3 us (5%)
  between operations  15.4 us (3%)
    pallas_call x6, Pallas kernels, move(): pl.pallas_call(kernel, out_shape=[out for part in parts for out in part.o...  342 us
    unnamed x104, local copies, waits for them, and re-layouts  11.4 us
  transfers between devices with their start and end apart: 2, of which 0 were waited for; matrix products, arithmetic and copies ran while one was open for 16% of the time, Pallas kernels for 27%

profile of v6, /device:TPU:0, one launch (start us, length us, event | category | flops | bytes accessed | tf_op | source)
XLA Modules:
  0.0 457.2 jit_solution(18367779940218358187)
XLA Ops:
  7.2 0.9 fusion.84
  8.1 1.0 slice.255
  13.5 70.3 %move_1.1 = (bf16[4,8,64,384]{3,2,1,0:T(8,128)(2,1)}, bf16[4,2,32,2048]{3,2,1,0:T(8,128)(2,1)}, bf16[8,2,64,2048]{3,2,1,0:T(8,128)(2,1)}, bf16[4,2,128,2048]{3,2,1,0:T(8,128)(2,1)}, f32[32,8,128]{2,1,0:T(8,128)}) custom-call(bf16[8,64,384]{2,1,0:T(8,128)(2,1)} %copy-done.28, bf16[2,32,2048]{2,1,0:T(8,128)(2,1)} %bitcast.340, bf16[2,64,2048]{2,1,0:T(8,128)(2,1)} %bitcast.290, ...), custom_call_target="tpu_custom_call" | custom-call | bytes 120000000 | tf_op jit(solution)/shard_map/move_1/pallas_call | solution.py:1287
  83.9 1.1 slice_reduce_fusion.1
  86.3 1.8 multiply_convert_fusion.1
  88.1 4.5 fusion.88
  93.4 1.2 fusion.65
  94.8 0.9 fusion.9
  95.7 0.9 exponential_reduce_fusion.1
  97.1 1.5 fusion.4
  98.6 2.1 exponential_reduce_fusion
  100.7 1.3 fusion.17
  102.0 2.4 fusion.12
  105.7 1.1 copy.56.refs_1_
  106.8 52.0 %move_2.1 = (bf16[4,2,128,2048]{3,2,1,0:T(8,128)(2,1)}, f32[2,64,2048]{2,1,0:T(8,128)}) custom-call(bf16[2,128,2048]{2,1,0:T(8,128)(2,1)} %bitcast.328, bf16[4,256,256]{2,1,0:T(8,128)(2,1)} %copy.56.refs_1_, bf16[256,2048]{1,0:T(8,128)(2,1)} %bitcast.329), custom_call_target="tpu_custom_call" | custom-call | bytes 120000000 | tf_op jit(solution)/shard_map/move_2/pallas_call | solution.py:1287
  158.8 1.5 multiply_reduce_fusion.3
  160.9 2.2 multiply_convert_fusion.2.refs_0_
  163.1 54.6 %move_3.1 = (bf16[8,2,64,2048]{3,2,1,0:T(8,128)(2,1)}, bf16[4,2,128,2048]{3,2,1,0:T(8,128)(2,1)}, bf16[4,256,1024]{2,1,0:T(8,128)(2,1)}, bf16[4,256,1024]{2,1,0:T(8,128)(2,1)}, bf16[4,256,1024]{2,1,0:T(8,128)(2,1)}) custom-call(bf16[2,64,2048]{2,1,0:T(8,128)(2,1)} %multiply_convert_fusion.2.refs_0_, bf16[2,128,2048]{2,1,0:T(8,128)(2,1)} %bitcast.323, ...), custom_call_target="tpu_custom_call" | custom-call | bytes 120000000 | tf_op jit(solution)/shard_map/move_3/pallas_call | solution.py:1287
  217.7 48.4 %move_4.1 = (f32[2,64,2048]{2,1,0:T(8,128)}, f32[2,128,2048]{2,1,0:T(8,128)}, bf16[4,2,2,64,2048]{4,3,2,1,0:T(8,128)(2,1)}, bf16[4,2,2,64,2048]{4,3,2,1,0:T(8,128)(2,1)}, bf16[4,2,2,64,2048]{4,3,2,1,0:T(8,128)(2,1)}) custom-call(bf16[1024,1024]{1,0:T(8,128)(2,1)} %bitcast.316, bf16[1024,1024]{1,0:T(8,128)(2,1)} %bitcast.317, bf16[1024,1024]{1,0:T(8,128)(2,1)} %bitcast.318, ...), custom_call_target="tpu_custom_call" | custom-call | bytes 120000000 | tf_op jit(solution)/shard_map/move_4/pallas_call | solution.py:1287
  266.1 1.9 multiply_reduce_fusion.1
  268.7 3.9 fusion.81
  272.6 46.9 %move_5.1 = (bf16[8,2,64,2048]{3,2,1,0:T(8,128)(2,1)}, f32[2,128,2048]{2,1,0:T(8,128)}) custom-call(bf16[2,64,2048]{2,1,0:T(8,128)(2,1)} %bitcast.308, bf16[4,2,128,2048]{3,2,1,0:T(8,128)(2,1)} %bitcast.301), custom_call_target="tpu_custom_call" | custom-call | bytes 120000000 | tf_op jit(solution)/shard_map/move_5/pallas_call | solution.py:1287
  319.6 1.2 copy-done.22
  320.8 3.6 convolution_convert_fusion.1
  324.6 1.2 convolution_bitcast_fusion.2
  325.8 5.6 %fusion.18 = bf16[1024,64]{0,1:T(8,128)(2,1)S(1)} fusion(bf16[512,4,64]{0,2,1:T(8,128)(2,1)S(1)} %bitcast.321, f32[512,64]{0,1:T(8,128)S(1)} %convolution_bitcast_fusion.2, f32[1024,512,4]{1,0,2:T(8,128)} %copy-done, f32[4,512]{1,0:T(4,128)S(1)} %copy-done.32, pred[512,1024]{0,1:T(8,128)(4,1)S(1)} %copy-done.7), kind=kOutput, calls=%fused_computation.45 | convolution fusion | flops 276955136 | bytes 9445376 | tf_op jit(solution)/shard_map/hqk,qhd->kd/dot_general | solution.py:1527
  331.4 0.8 copy.64
  332.3 3.9 fusion.5
  336.2 1.3 fusion.7
  338.7 3.8 fusion
  342.5 2.8 fusion.2
  345.3 2.0 copy-done.1
  347.4 0.8 fusion.11
  348.4 0.8 maximum_convert_fusion
  349.2 2.2 concatenate.107
  352.3 4.1 fusion.16
  357.1 4.1 multiply_reduce_fusion
  362.5 1.0 pad_maximum_fusion.refs_2_
  363.6 4.4 convolution_convert_fusion
  368.0 69.5 %move_6.1 = (f32[64,3072]{1,0:T(8,128)}, f32[2,32,2048]{2,1,0:T(8,128)}, f32[2,64,2048]{2,1,0:T(8,128)}, f32[2,128,2048]{2,1,0:T(8,128)}, f32[8,128]{1,0:T(8,128)}) custom-call(bf16[4,2,4,64,384]{4,3,2,1,0:T(8,128)(2,1)} %bitcast.319, bf16[4,2,32,2048]{3,2,1,0:T(8,128)(2,1)} %bitcast.324, bf16[4,256,384]{2,1,0:T(8,128)(2,1)} %pad_maximum_fusion.refs_2_, ...), custom_call_target="tpu_custom_call" | custom-call | bytes 120000000 | tf_op jit(solution)/shard_map/move_6/pallas_call | solution.py:1287
  437.6 1.6 fusion.20
  439.2 1.3 slice_bitcast_fusion.7
  440.5 3.7 fusion.25
  444.3 0.9 copy.136
  445.2 0.8 copy.137
  446.0 1.3 copy.138
  447.3 1.3 copy.139
  448.6 1.3 copy.140
  (168 shorter events, 14.0 us)
Async XLA Ops:
  7.2 156.0 %all-gather.2.cloned.1.call-start = ((), (), s32[]{:S(2)}) async-start(), calls=%async_computation.1 | async-start | bytes 4718592 | tf_op jit(solution)/shard_map/all_gather | solution.py:1413
  83.8 356.7 %reduce-scatter.2.cloned.1.call-start = ((), (), s32[]{:S(2)}) async-start(), calls=%async_computation.2 | async-start | bytes 4718592 | tf_op jit(solution)/shard_map/reduce_scatter | solution.py:1490
  92.6 9.4 %copy-start.39 = (bf16[1024,384]{0,1:T(8,128)(2,1)}, bf16[1024,384]{0,1:T(8,128)(2,1)S(1)}, u32[]{:S(2)}) copy-start(bf16[1024,384]{0,1:T(8,128)(2,1)S(1)} %get-tuple-element.206) | copy-start | bytes 2359300
  92.7 3.0 copy-start.42
  92.7 1.9 copy-start.36
  93.4 3.6 copy-start.24
  94.8 2.3 copy-start.10
  94.8 2.3 copy-start.12
  95.7 5.0 %copy-start.2 = (f32[512,512,4]{1,0,2:T(8,128)}, f32[512,512,4]{1,0,2:T(8,128)S(1)}, u32[]{:S(2)}) copy-start(f32[512,512,4]{1,0,2:T(8,128)S(1)} %get-tuple-element.211) | copy-start | bytes 12582916
  96.6 4.1 copy-start.34
  97.0 5.0 %copy-start.6 = (pred[512,1024]{0,1:T(8,128)(4,1)}, pred[512,1024]{0,1:T(8,128)(4,1)S(1)}, u32[]{:S(2)}) copy-start(pred[512,1024]{0,1:T(8,128)(4,1)S(1)} %iota_compare_fusion) | copy-start | bytes 1572868
  98.6 3.4 copy-start
  100.7 3.7 copy-start.31
  104.4 54.4 %copy-start.5 = (bf16[1,128,2048]{2,1,0:T(8,128)(2,1)S(1)}, bf16[1,128,2048]{2,1,0:T(8,128)(2,1)}, u32[]{:S(2)}) copy-start(bf16[1,128,2048]{2,1,0:T(8,128)(2,1)} %param.25) | copy-start | bytes 1572868
  104.5 0.8 copy-start.17
  160.4 2.7 copy-start.45
  319.6 1.2 copy-start.22
  320.8 3.7 copy-start.3
  320.8 3.7 copy-start.35
  324.4 1.3 copy-start.7
  324.5 1.3 copy-start.32
  331.4 4.8 %copy-start.29 = (bf16[1024,64]{0,1:T(8,128)(2,1)}, bf16[1024,64]{0,1:T(8,128)(2,1)S(1)}, u32[]{:S(2)}) copy-start(bf16[1024,64]{0,1:T(8,128)(2,1)S(1)} %fusion.18) | copy-start | bytes 393220
  332.3 3.9 copy-start.4
  332.3 5.8 %slice-start = ((s8[8388608]{0:T(1024)(128)(4,1)}), s8[4194304]{0:T(1024)(128)(4,1)S(1)}, s32[]{:S(2)}) async-start(s8[8388608]{0:T(1024)(128)(4,1)} %bitcast.288), calls=%async_computation.3 | async-start | bytes 8388608
  336.2 1.3 copy-start.25
  336.2 2.5 slice-start.1
  336.2 2.5 copy-start.8
  345.3 2.0 copy-start.1
  347.4 0.9 copy-start.26
  347.4 4.1 copy-start.11
  347.4 4.1 copy-start.13
  351.5 4.9 %copy-start.37 = (f32[1024]{0:T(1024)S(1)}, f32[1024]{0:T(1024)}, u32[]{:S(2)}) copy-start(f32[1024]{0:T(1024)} %copy-done.36) | copy-start | bytes 12292
  351.5 4.9 %copy-start.43 = (f32[32]{0:T(128)S(1)}, f32[32]{0:T(128)}, u32[]{:S(2)}) copy-start(f32[32]{0:T(128)} %copy-done.42) | copy-start | bytes 388
  351.5 5.5 %copy-start.9 = (bf16[4,8,64,384]{3,2,1,0:T(8,128)(2,1)S(1)}, bf16[4,8,64,384]{3,2,1,0:T(8,128)(2,1)}, u32[]{:S(2)}) copy-start(bf16[4,8,64,384]{3,2,1,0:T(8,128)(2,1)} %get-tuple-element.125) | copy-start | bytes 4718596
  351.5 5.5 %copy-start.20 = (bf16[1024,4,64]{0,2,1:T(8,128)(2,1)S(1)}, bf16[1024,4,64]{0,2,1:T(8,128)(2,1)}, u32[]{:S(2)}) copy-start(bf16[1024,4,64]{0,2,1:T(8,128)(2,1)} %maximum_convert_fusion) | copy-start | bytes 1572868
  351.5 5.5 %copy-start.30 = (bf16[1024,64]{0,1:T(8,128)(2,1)S(1)}, bf16[1024,64]{0,1:T(8,128)(2,1)}, u32[]{:S(2)}) copy-start(bf16[1024,64]{0,1:T(8,128)(2,1)} %copy-done.29) | copy-start | bytes 393220
  351.5 5.5 %copy-start.33 = (f32[2048]{0:T(1024)S(1)}, f32[2048]{0:T(1024)}, u32[]{:S(2)}) copy-start(f32[2048]{0:T(1024)} %mul.500) | copy-start | bytes 24580
  351.5 5.5 %copy-start.46 = (bf16[8,2,64,2048]{3,2,1,0:T(8,128)(2,1)S(1)}, bf16[8,2,64,2048]{3,2,1,0:T(8,128)(2,1)}, u32[]{:S(2)}) copy-start(bf16[8,2,64,2048]{3,2,1,0:T(8,128)(2,1)} %get-tuple-element.124) | copy-start | bytes 12582916
  357.0 4.4 copy-start.19
  357.0 4.8 %copy-start.38 = (f32[1,32,64]{2,0,1:T(1,128)S(1)}, f32[1,32,64]{2,0,1:T(1,128)}, u32[]{:S(2)}) copy-start(f32[1,32,64]{2,0,1:T(1,128)} %stack.46) | copy-start | bytes 24580
  357.0 5.5 %copy-start.21 = (bf16[1024,64]{1,0:T(8,128)(2,1)S(1)}, bf16[1024,64]{1,0:T(8,128)(2,1)}, u32[]{:S(2)}) copy-start(bf16[1024,64]{1,0:T(8,128)(2,1)} %copy.64) | copy-start | bytes 393220
  357.0 6.5 %copy-start.18 = (bf16[1024,4,64]{0,2,1:T(8,128)(2,1)S(1)}, bf16[1024,4,64]{0,2,1:T(8,128)(2,1)}, u32[]{:S(2)}) copy-start(bf16[1024,4,64]{0,2,1:T(8,128)(2,1)} %copy-done.17) | copy-start | bytes 1572868
  368.0 71.2 %copy-start.44 = (f32[128]{0:T(128)S(1)}, f32[128]{0:T(128)}, u32[]{:S(2)}) copy-start(f32[128]{0:T(128)} %get-tuple-element.165) | copy-start | bytes 1540
  437.6 6.7 %copy-start.23 = (f32[64,3072]{1,0:T(8,128)S(1)}, f32[64,3072]{1,0:T(8,128)}, u32[]{:S(2)}) copy-start(f32[64,3072]{1,0:T(8,128)} %get-tuple-element.251) | copy-start | bytes 2359300
  437.6 7.6 %copy-start.27 = (f32[2,32,2048]{2,1,0:T(8,128)S(1)}, f32[2,32,2048]{2,1,0:T(8,128)}, u32[]{:S(2)}) copy-start(f32[2,32,2048]{2,1,0:T(8,128)} %get-tuple-element.146) | copy-start | bytes 1572868
  440.5 5.4 %copy-start.15 = (f32[2,128,2048]{2,1,0:T(8,128)S(1)}, f32[2,128,2048]{2,1,0:T(8,128)}, u32[]{:S(2)}) copy-start(f32[2,128,2048]{2,1,0:T(8,128)} %get-tuple-element.147) | copy-start | bytes 6291460
  444.3 3.0 copy-start.16
  446.0 2.6 copy-start.14
  (3 other events, 2.0 us)
Sparse Core Ops, SparseCore 0:
  84.0 51.1 all-gather.1
  319.7 48.0 reduce-scatter.1

commit v7 on v6

--- a/solution.py
+++ b/solution.py
@@ -316,6 +316,43 @@
 
 def line_scatter_scratch(chips, shape):
     return [pltpu.VMEM((chips,) + shape, jnp.bfloat16)] * 3 + [DMA((chips, SUB))] * 6
+
+
+class LineScatter:
+    def __init__(self, partial, dps, groups):
+        total, width = partial.shape
+        rows = total // groups
+        shape = (SUB, rows // SUB, width)
+        self.inputs, self.in_specs = [partial.reshape((groups,) + shape)], [VM]
+        self.outs, self.out_specs = [jax.ShapeDtypeStruct(shape, jnp.float32)], [VM]
+        self.scratch = line_scatter_scratch(groups // 2, shape)
+        self.result = lambda out: out.reshape(rows, width)
+
+    def bind(self, place, *refs):
+        send, step, finish = line_scatter(place, *refs)
+        chip, chips = place.chip, place.chips
+
+        def start():
+            def issue(low, _):
+                high = chips - 1 - low
+
+                @pl.when(high > chip)
+                def _():
+                    send(high)
+
+                @pl.when(low < chip)
+                def _():
+                    send(low)
+
+                return 0
+
+            lax.fori_loop(0, chips - 1, issue, 0)
+            send(chip)
+
+        ticks = {
+            i: functools.partial(step, i // SUB, i % SUB) for i in range((chips - 1) * SUB)
+        }
+        return start, ticks, finish
 
 
 class LineProduct:
@@ -560,8 +597,8 @@
             for hop in range(1, place.hops)
         }
         if self.late:
-            ticks[1] = ring[0]
-            return lambda: None, ticks, ring[2]
+            ticks[1] = ring[4]
+            return ring[3], ticks, ring[2]
         return ring[0], ticks, ring[2]
 
 
@@ -1039,6 +1076,10 @@
         return start, merged, finish
 
 
+class Loaded:
+    start = wait = staticmethod(lambda: None)
+
+
 class FeedBack:
     def __init__(self, inner, dgate, dup, gate, up, down, normed, grads, dps, groups):
         length, held = inner.shape
@@ -1091,7 +1132,12 @@
         line_refs, ring_refs = refs[18:27], refs[27:]
         chip, chips, hops = place.chip, place.chips, place.hops
         held, width = gate.shape
-        pair = inner.shape[0] // chips
+        pair = (inner.shape[0] if len(inner.shape) == 2 else inner.shape[0] * inner.shape[1]) // chips
+
+        def flat(ref, lanes):
+            value = ref[(slice(None),) * (len(ref.shape) - 1) + (lanes,)]
+            return value.reshape(-1, value.shape[-1])
+
         chunk = held // place.dps
         wide = 1024 if width % 1024 == 0 else width
         send, step, finish_line = line_scatter(place, p_ref, total_ref, *line_refs)
@@ -1104,13 +1150,16 @@
         copies = [
             pltpu.make_async_copy(source, target, loads.at[i])
             for i, (source, target) in enumerate(zip(sources, targets))
-        ]
+            if source is not None
+        ] or [Loaded] * len(targets)
 
         def start():
             for i in (0, 7, 1, 3, 2, 4, 6, 5):
                 copies[i].start()
 
         def rows_of(ref, at):
+            if len(ref.shape) == 3:
+                return ref[at]
             return ref[pl.ds(pl.multiple_of(at * pair, pair), pair), :]
 
         def partial(at):
@@ -1126,8 +1175,8 @@
 
         def term_rows(ref, other, start, count, span):
             return lax.dot_general(
-                ref[:, pl.ds(start, count)],
-                other[:, span],
+                flat(ref, pl.ds(start, count)),
+                flat(other, span),
                 contract_rows,
                 preferred_element_type=jnp.float32,
             ).astype(jnp.bfloat16)
@@ -1196,7 +1245,7 @@
                 left = rows_of(inner, at)
                 for first in range(0, width, wide):
                     span = slice(first, first + wide)
-                    value = jnp.dot(left, down[:, span], preferred_element_type=jnp.float32)
+                    value = jnp.dot(left, flat(down, span), preferred_element_type=jnp.float32)
                     slot[:, :, :, span] = value.astype(jnp.bfloat16).reshape(
                         slot.shape[:3] + (wide,)
                     )
@@ -1257,6 +1306,45 @@
                 copy.wait()
 
         return start, {0: sequence}, finish
+
+
+class Feed:
+    def __init__(self, normed, down, gate, up, grad_all, dps, groups):
+        forth = FeedForward(normed, down, gate, up, grad_all, dps, groups)
+        act = jax.ShapeDtypeStruct((grad_all.shape[0], gate.shape[0]), jnp.bfloat16)
+        back = FeedBack(act, act, act, gate, up, gate, grad_all, grad_all, dps, groups)
+        self.forth, self.back = forth, back
+        self.inputs, self.in_specs = forth.inputs, forth.in_specs
+        self.outs, self.out_specs, self.result = back.outs, back.out_specs, back.result
+        self.scratch = [pltpu.VMEM(out.shape, out.dtype) for out in forth.outs]
+        self.scratch += forth.scratch[:3] + forth.scratch[6:] + back.scratch[12:]
+
+    def bind(self, place, *refs):
+        inputs, outs, held, refs = refs[:5], refs[5:10], refs[10:18], refs[18:]
+        hn, full, inner, dgate, dup, gate, up, grads = held
+        split = len(self.forth.scratch) - 6
+        forth_sems, back_refs = refs[:split], refs[split:]
+
+        def run_forth(*local):
+            start, ticks, finish = self.forth.bind(place, *inputs, *held, *local, *forth_sems)
+            start()
+            for tick in sorted(ticks):
+                ticks[tick]()
+            finish()
+
+        def run_back(*local):
+            shared = (inner, dgate, dup, gate, up, full, hn, grads)
+            _, ticks, finish = self.back.bind(
+                place, *[None] * 8, *outs, *shared, *local, None, *back_refs
+            )
+            ticks[0]()
+            finish()
+
+        def run():
+            pl.run_scoped(run_forth, *self.forth.scratch[3:6])
+            pl.run_scoped(run_back, *self.back.scratch[8:11])
+
+        return lambda: None, {0: run}, lambda: None
 
 
 def move(parts, dps, groups, number, greet=greet_near):
@@ -1448,30 +1536,11 @@
     hidden = x_rows + summed
     factor_two = norm_factor(hidden)
     normed_two = (hidden * factor_two * gain_two).astype(jnp.bfloat16)
-    ((hn_all, down_part, inner, grad_gate, grad_upward),) = move(
-        [FeedForward(normed_two, down_weight, gate_part, up_part, grad_all, dps, groups)],
+    ((grad_normed, down_owned, gate_term, up_term, result),) = move(
+        [Feed(normed_two, down_weight, gate_part, up_part, grad_all, dps, groups)],
         dps,
         groups,
         3,
-    )
-    ((grad_normed, down_owned, gate_term, up_term, result),) = move(
-        [
-            FeedBack(
-                inner,
-                grad_gate,
-                grad_upward,
-                gate_part,
-                up_part,
-                down_part,
-                hn_all,
-                grad_all,
-                dps,
-                groups,
-            )
-        ],
-        dps,
-        groups,
-        4,
     )
     gain_two_term = jnp.sum(grad_normed * hidden * factor_two, axis=0)
     grad_hidden = grad_low.astype(jnp.float32) + norm_grad(
@@ -1534,6 +1603,9 @@
     qkv_term = lax.dot_general(
         normed_all, grad_mixed, contract_rows, preferred_element_type=jnp.float32
     )
+    partial = lax.dot_general(
+        grad_mixed, qkv_local, contract_cols, preferred_element_type=jnp.float32
+    )
     gain_one_term = jnp.sum(qkv_term * qkv_local.astype(jnp.float32), axis=1)
     qkv_term = (qkv_term * gain_one[:, None]).astype(jnp.bfloat16)
     terms = jnp.stack([gain_one_term, gain_two_term]).reshape(2, dps * groups, gain_width)
@@ -1542,7 +1614,7 @@
         [
             ColumnsBack(qkv_term, order, local_width, kv_copies, weight_rows, dps, groups),
             RowsBack(out_term, weight_rows, dps, groups),
-            LineProduct(grad_mixed, qkv_local, contract_cols, dps, groups),
+            LineScatter(partial.astype(jnp.bfloat16), dps, groups),
             RingScatter(up_term, dps, groups, late=True),
             Spread(terms, True, dps, groups),
         ],

time: 466 us -> 445 us (0.955)
  Pallas kernels: 342 us -> 331 us
  local copies, waits for them, and re-layouts: 25.3 us -> 19.7 us
    pallas_call x6 -> x5, Pallas kernels: 342 us -> 331 us  [move(): pl.pallas_call(kernel, out_shape=[out for part in parts for out in part.o...]
    dot_general x0 -> x1, matrix products: none -> 5.68 us  [per_device(): lax.dot_general(grad_mixed, qkv_local, contract_cols, preferred_element_t...]
    unnamed x104 -> x96, local copies, waits for them, and re-layouts: 11.4 us -> 9.4 us
  transfers between devices with their start and end apart: 2 -> 2, of which waited for: 0 -> 0; matrix products, arithmetic and copies ran while one was open for 16% -> 15% of each run, Pallas kernels for 27% -> 28%
where the time goes in v7:
time: 445 us; the launch traced here: 437 us
  Pallas kernels  331 us (74%)
  matrix products  40.9 us (9%)
  other arithmetic  29.9 us (7%)
  local copies, waits for them, and re-layouts  19.7 us (4%)
  between operations  15.4 us (3%)
    pallas_call x5, Pallas kernels, move(): pl.pallas_call(kernel, out_shape=[out for part in parts for out in part.o...  331 us
    unnamed x96, local copies, waits for them, and re-layouts  9.4 us
  transfers between devices with their start and end apart: 2, of which 0 were waited for; matrix products, arithmetic and copies ran while one was open for 15% of the time, Pallas kernels for 28%

profile of v7, /device:TPU:0, one launch (start us, length us, event | category | flops | bytes accessed | tf_op | source)
XLA Modules:
  0.0 437.0 jit_solution(243453294530305596)
XLA Ops:
  7.2 0.9 fusion.82
  8.1 1.0 slice.255
  12.8 0.7 copy-done.23
  13.5 70.3 %move_1.1 = (bf16[4,8,64,384]{3,2,1,0:T(8,128)(2,1)}, bf16[4,2,32,2048]{3,2,1,0:T(8,128)(2,1)}, bf16[8,2,64,2048]{3,2,1,0:T(8,128)(2,1)}, bf16[4,2,128,2048]{3,2,1,0:T(8,128)(2,1)}, f32[32,8,128]{2,1,0:T(8,128)}) custom-call(bf16[8,64,384]{2,1,0:T(8,128)(2,1)} %copy-done.23, bf16[2,32,2048]{2,1,0:T(8,128)(2,1)} %bitcast.326, bf16[2,64,2048]{2,1,0:T(8,128)(2,1)} %bitcast.283, ...), custom_call_target="tpu_custom_call" | custom-call | bytes 120000000 | tf_op jit(solution)/shard_map/move_1/pallas_call | solution.py:1375
  83.9 1.1 slice_reduce_fusion.1
  86.3 1.8 multiply_convert_fusion.1
  88.1 4.5 %fusion.86 = (bf16[1024,384]{0,1:T(8,128)(2,1)S(1)}, f32[1024,384]{0,1:T(8,128)S(1)}) fusion(bf16[1024,2048]{1,0:T(8,128)(2,1)} %bitcast.329, bf16[2048,384]{1,0:T(8,128)(2,1)S(1)} %bitcast.305), kind=kOutput, calls=%fused_computation.188 | convolution fusion | flops 1611005952 | bytes 8126464 | tf_op jit(solution)/shard_map/dot_general | solution.py:1503
  93.4 1.2 fusion.62
  94.8 0.9 fusion.9
  95.7 0.9 exponential_reduce_fusion.1
  97.0 1.5 fusion.4
  98.6 2.1 exponential_reduce_fusion
  100.7 1.3 fusion.17
  102.0 2.4 fusion.12
  104.5 0.8 copy-done.13
  105.7 1.1 copy.53.refs_1_
  106.8 52.1 %move_2.1 = (bf16[4,2,128,2048]{3,2,1,0:T(8,128)(2,1)}, f32[2,64,2048]{2,1,0:T(8,128)}) custom-call(bf16[2,128,2048]{2,1,0:T(8,128)(2,1)} %bitcast.311, bf16[4,256,256]{2,1,0:T(8,128)(2,1)} %copy.53.refs_1_, bf16[256,2048]{1,0:T(8,128)(2,1)} %bitcast.312), custom_call_target="tpu_custom_call" | custom-call | bytes 120000000 | tf_op jit(solution)/shard_map/move_2/pallas_call | solution.py:1375
  158.9 1.5 multiply_reduce_fusion.3
  161.0 2.2 multiply_convert_fusion.2.refs_0_
  163.2 91.0 %move_3.1 = (f32[2,64,2048]{2,1,0:T(8,128)}, f32[2,128,2048]{2,1,0:T(8,128)}, bf16[4,2,2,64,2048]{4,3,2,1,0:T(8,128)(2,1)}, bf16[4,2,2,64,2048]{4,3,2,1,0:T(8,128)(2,1)}, bf16[4,2,2,64,2048]{4,3,2,1,0:T(8,128)(2,1)}) custom-call(bf16[2,64,2048]{2,1,0:T(8,128)(2,1)} %multiply_convert_fusion.2.refs_0_, bf16[2,128,2048]{2,1,0:T(8,128)(2,1)} %bitcast.309, ...), custom_call_target="tpu_custom_call" | custom-call | bytes 120000000 | tf_op jit(solution)/shard_map/move_3/pallas_call | solution.py:1375
  254.2 2.4 multiply_reduce_fusion.1
  256.8 3.9 fusion.79
  260.7 46.9 %move_5.1 = (bf16[8,2,64,2048]{3,2,1,0:T(8,128)(2,1)}, f32[2,128,2048]{2,1,0:T(8,128)}) custom-call(bf16[2,64,2048]{2,1,0:T(8,128)(2,1)} %bitcast.297, bf16[4,2,128,2048]{3,2,1,0:T(8,128)(2,1)} %bitcast.291), custom_call_target="tpu_custom_call" | custom-call | bytes 120000000 | tf_op jit(solution)/shard_map/move_5/pallas_call | solution.py:1375
  307.6 1.2 copy-done.16
  308.8 3.5 convolution_convert_fusion.2
  312.3 0.7 stack.46
  313.1 3.9 fusion.5
  317.0 1.3 fusion.7
  318.3 0.7 fusion.19
  319.6 3.8 fusion
  323.4 2.8 fusion.2
  326.2 1.4 fusion.16
  328.7 0.8 fusion.11
  329.8 1.2 convolution_bitcast_fusion.2
  331.1 2.4 fusion.18
  333.8 4.2 multiply_reduce_fusion
  338.2 0.7 pad.25.refs_4_
  338.8 5.7 %convolution_convert_fusion = bf16[1024,2048]{1,0:T(8,128)(2,1)} fusion(bf16[2048,384]{1,0:T(8,128)(2,1)S(1)} %bitcast.304, bf16[1024,64]{0,1:T(8,128)(2,1)S(1)} %fusion.18, bf16[1024,64]{0,1:T(8,128)(2,1)} %copy-done.24, bf16[1024,256]{0,1:T(8,128)(2,1)} %bitcast.325), kind=kOutput, calls=%fused_computation.18 | convolution fusion | flops 1615069184 | bytes 6553600 | tf_op jit(solution)/shard_map/dot_general | solution.py:1606
  344.5 2.2 convolution_convert_fusion.1
  346.8 70.6 %move_6.1 = (f32[64,3072]{1,0:T(8,128)}, f32[2,32,2048]{2,1,0:T(8,128)}, f32[2,64,2048]{2,1,0:T(8,128)}, f32[2,128,2048]{2,1,0:T(8,128)}, f32[8,128]{1,0:T(8,128)}) custom-call(bf16[4,2,4,64,384]{4,3,2,1,0:T(8,128)(2,1)} %bitcast.306, bf16[4,2,32,2048]{3,2,1,0:T(8,128)(2,1)} %bitcast.317, bf16[8,2,64,2048]{3,2,1,0:T(8,128)(2,1)} %bitcast.295, ...), custom_call_target="tpu_custom_call" | custom-call | bytes 120000000 | tf_op jit(solution)/shard_map/move_6/pallas_call | solution.py:1375
  417.4 1.6 fusion.20
  419.0 1.3 slice_bitcast_fusion.7
  420.3 3.7 fusion.25
  424.1 0.9 copy.130
  425.0 0.8 copy.131
  425.8 1.3 copy.132
  427.1 1.3 copy.133
  428.4 1.3 copy.134
  (154 shorter events, 9.9 us)
Async XLA Ops:
  7.2 156.0 %all-gather.2.cloned.1.call-start = ((), (), s32[]{:S(2)}) async-start(), calls=%async_computation.1 | async-start | bytes 4718592 | tf_op jit(solution)/shard_map/all_gather | solution.py:1501
  12.1 0.7 copy-start.35
  12.8 0.7 copy-start.23
  83.8 336.5 %reduce-scatter.2.cloned.1.call-start = ((), (), s32[]{:S(2)}) async-start(), calls=%async_computation.2 | async-start | bytes 4718592 | tf_op jit(solution)/shard_map/reduce_scatter | solution.py:1559
  92.6 9.4 %copy-start.33 = (bf16[1024,384]{0,1:T(8,128)(2,1)}, bf16[1024,384]{0,1:T(8,128)(2,1)S(1)}, u32[]{:S(2)}) copy-start(bf16[1024,384]{0,1:T(8,128)(2,1)S(1)} %get-tuple-element.196) | copy-start | bytes 2359300
  92.7 2.1 copy-start.37
  92.7 3.0 copy-start.30
  93.4 3.6 copy-start.18
  94.7 2.3 copy-start.6
  94.8 2.3 copy-start.8
  95.7 5.0 %copy-start.1 = (f32[512,512,4]{1,0,2:T(8,128)}, f32[512,512,4]{1,0,2:T(8,128)S(1)}, u32[]{:S(2)}) copy-start(f32[512,512,4]{1,0,2:T(8,128)S(1)} %get-tuple-element.201) | copy-start | bytes 12582916
  96.6 4.1 copy-start.28
  97.0 5.0 %copy-start.4 = (pred[512,1024]{0,1:T(8,128)(4,1)}, pred[512,1024]{0,1:T(8,128)(4,1)S(1)}, u32[]{:S(2)}) copy-start(pred[512,1024]{0,1:T(8,128)(4,1)S(1)} %iota_compare_fusion) | copy-start | bytes 1572868
  98.6 3.4 copy-start
  100.7 3.7 copy-start.25
  104.4 54.5 %copy-start.3 = (bf16[1,128,2048]{2,1,0:T(8,128)(2,1)S(1)}, bf16[1,128,2048]{2,1,0:T(8,128)(2,1)}, u32[]{:S(2)}) copy-start(bf16[1,128,2048]{2,1,0:T(8,128)(2,1)} %param.25) | copy-start | bytes 1572868
  104.5 0.8 copy-start.13
  160.4 0.6 copy-start.36
  160.4 2.7 copy-start.40
  307.6 1.2 copy-start.16
  308.8 3.5 copy-start.34
  308.8 4.2 copy-start.29
  313.0 3.9 copy-start.2
  313.1 6.0 %slice-start = ((s8[8388608]{0:T(1024)(128)(4,1)}), s8[4194304]{0:T(1024)(128)(4,1)S(1)}, s32[]{:S(2)}) async-start(s8[8388608]{0:T(1024)(128)(4,1)} %bitcast.281), calls=%async_computation.3 | async-start | bytes 8388608
  316.9 1.4 copy-start.7
  317.0 1.4 copy-start.9
  317.0 2.5 slice-start.1
  317.0 2.6 copy-start.5
  317.0 2.6 copy-start.26
  326.2 1.4 copy-start.31
  326.2 1.4 copy-start.38
  326.2 2.0 copy-start.19
  327.6 2.0 copy-start.20
  328.2 5.2 %copy-start.24 = (bf16[1024,64]{0,1:T(8,128)(2,1)}, bf16[1024,64]{0,1:T(8,128)(2,1)S(1)}, u32[]{:S(2)}) copy-start(bf16[1024,64]{0,1:T(8,128)(2,1)S(1)} %maximum_bitcast_fusion.1) | copy-start | bytes 393220
  329.8 3.7 copy-start.22
  331.0 2.4 copy-start.15
  331.0 2.4 copy-start.27
  331.1 2.7 copy-start.41
  333.8 4.3 copy-start.32
  338.8 5.7 %copy-start.14 = (bf16[1024,4,64]{0,2,1:T(8,128)(2,1)S(1)}, bf16[1024,4,64]{0,2,1:T(8,128)(2,1)}, u32[]{:S(2)}) copy-start(bf16[1024,4,64]{0,2,1:T(8,128)(2,1)} %copy-done.13) | copy-start | bytes 1572868
  338.8 5.7 %copy-start.42 = (bf16[8,2,64,2048]{3,2,1,0:T(8,128)(2,1)S(1)}, bf16[8,2,64,2048]{3,2,1,0:T(8,128)(2,1)}, u32[]{:S(2)}) copy-start(bf16[8,2,64,2048]{3,2,1,0:T(8,128)(2,1)} %get-tuple-element.130) | copy-start | bytes 12582916
  346.8 72.3 %copy-start.39 = (f32[128]{0:T(128)S(1)}, f32[128]{0:T(128)}, u32[]{:S(2)}) copy-start(f32[128]{0:T(128)} %get-tuple-element.155) | copy-start | bytes 1540
  417.4 6.7 %copy-start.17 = (f32[64,3072]{1,0:T(8,128)S(1)}, f32[64,3072]{1,0:T(8,128)}, u32[]{:S(2)}) copy-start(f32[64,3072]{1,0:T(8,128)} %get-tuple-element.241) | copy-start | bytes 2359300
  417.4 7.6 %copy-start.21 = (f32[2,32,2048]{2,1,0:T(8,128)S(1)}, f32[2,32,2048]{2,1,0:T(8,128)}, u32[]{:S(2)}) copy-start(f32[2,32,2048]{2,1,0:T(8,128)} %get-tuple-element.136) | copy-start | bytes 1572868
  420.3 5.4 %copy-start.11 = (f32[2,128,2048]{2,1,0:T(8,128)S(1)}, f32[2,128,2048]{2,1,0:T(8,128)}, u32[]{:S(2)}) copy-start(f32[2,128,2048]{2,1,0:T(8,128)} %get-tuple-element.137) | copy-start | bytes 6291460
  424.1 3.0 copy-start.12
  425.8 2.6 copy-start.10
Sparse Core Ops, SparseCore 0:
  83.9 51.1 all-gather.1
  307.7 48.9 reduce-scatter.1

commit v8 on v7

--- a/solution.py
+++ b/solution.py
@@ -603,22 +603,39 @@
 
 
 class Columns:
-    def __init__(self, blocks, dps, groups):
-        _, rows, width = blocks.shape
-        self.inputs, self.in_specs = [blocks], [VM]
-        self.outs = [jax.ShapeDtypeStruct((dps, groups, rows, width), blocks.dtype)]
+    def __init__(self, joint, order, heads_width, copies, dps, groups):
+        rows, width = joint.shape[0], heads_width + 2 * HEAD_DIM
+        self.order, self.heads_width, self.copies = order, heads_width, copies
+        self.inputs, self.in_specs = [joint], [VM]
+        self.outs = [jax.ShapeDtypeStruct((dps, groups, rows, width), joint.dtype)]
         self.out_specs = [ANY]
         self.scratch = [
-            pltpu.VMEM((groups, rows, width), blocks.dtype),
+            pltpu.VMEM((groups, rows, width), joint.dtype),
+            pltpu.VMEM((groups, rows, width), joint.dtype),
             DMA((2,)),
             DMA((groups,)),
             DMA((groups,)),
         ] + ring_sems(dps // 2)
         self.result = lambda out: out.reshape(dps * groups * rows, width)
 
-    def bind(self, place, x_ref, out_ref, landing, own_sem, sends, recvs, *sems):
+    def bind(self, place, joint_ref, out_ref, x_ref, landing, own_sem, sends, recvs, *sems):
         s, groups = place.s, place.groups
         half_of = groups // 2
+        heads, pair = self.heads_width, 2 * HEAD_DIM
+
+        def pair_of(head, first):
+            at = groups * heads + first + head // 2 * pair
+            value = joint_ref[:, at : at + pair].astype(jnp.float32)
+            return value, pltpu.roll(value, HEAD_DIM, 1)
+
+        for at, g in enumerate(self.order):
+            x_ref[at, :, :heads] = joint_ref[:, g * heads : (g + 1) * heads]
+            head = g // self.copies
+            keys, values = pair_of(head, 0), pair_of(head, KV_HEADS * HEAD_DIM)
+            lanes = lax.broadcasted_iota(jnp.int32, keys[0].shape, 1)
+            both = jnp.where(lanes < HEAD_DIM, keys[head % 2], values[1 - head % 2])
+            x_ref[at, :, heads:] = both.astype(x_ref.dtype)
+
         here = pltpu.make_async_copy(x_ref.at[s], landing.at[s], own_sem.at[0])
         own = pltpu.make_async_copy(landing, out_ref.at[place.d], own_sem.at[1])
 
@@ -1460,26 +1477,13 @@
     fold = groups // dps
     order = [(at % dps) * fold + at // dps for at in range(groups)]
 
-    q_part = qkv_weight[:, :model_width].reshape(weight_rows, groups, local_width)
-    k_part = qkv_weight[:, model_width : model_width + KV_HEADS * HEAD_DIM]
-    v_part = qkv_weight[:, model_width + KV_HEADS * HEAD_DIM :]
-    k_part = k_part.reshape(weight_rows, KV_HEADS, HEAD_DIM)
-    v_part = v_part.reshape(weight_rows, KV_HEADS, HEAD_DIM)
-    columns = jnp.stack(
-        [
-            jnp.concatenate(
-                [q_part[:, g], k_part[:, g // kv_copies], v_part[:, g // kv_copies]], axis=1
-            )
-            for g in order
-        ]
-    )
     gain_width = attn_gain.shape[0]
     tile = jnp.zeros((8, 128), jnp.float32)
     tile = tile.at[0, :gain_width].set(attn_gain.astype(jnp.float32))
     tile = tile.at[1, :gain_width].set(mlp_gain.astype(jnp.float32))
     qkv_local, out_rows, normed_all, gate_part, gains = move(
         [
-            Columns(columns, dps, groups),
+            Columns(qkv_weight, order, local_width, kv_copies, dps, groups),
             Rows(out_weight, dps, groups),
             LineGather(tokens[0], dps, groups, normed=True),
             RingGather(gate_weight, dps, groups, late=True),

time: 445 us -> 440 us (0.989)
    unnamed x96 -> x93, local copies, waits for them, and re-layouts: 9.4 us -> 9.2 us
where the time goes in v8:
time: 440 us; the launch traced here: 432 us
  Pallas kernels  331 us (75%)
  matrix products  40.9 us (9%)
  other arithmetic  29.2 us (7%)
  local copies, waits for them, and re-layouts  16.3 us (4%)
  between operations  15 us (3%)
    pallas_call x5, Pallas kernels, move(): pl.pallas_call(kernel, out_shape=[out for part in parts for out in part.o...  331 us
    unnamed x93, local copies, waits for them, and re-layouts  9.2 us
  transfers between devices with their start and end apart: 2, of which 0 were waited for; matrix products, arithmetic and copies ran while one was open for 15% of the time, Pallas kernels for 28%

profile of v8, /device:TPU:0, one launch (start us, length us, event | category | flops | bytes accessed | tf_op | source)
XLA Modules:
  0.0 432.5 jit_solution(8632830500376901908)
XLA Ops:
  7.9 0.7 pad_convert_fusion
  9.2 70.4 %move_1.1 = (bf16[4,8,64,384]{3,2,1,0:T(8,128)(2,1)}, bf16[4,2,32,2048]{3,2,1,0:T(8,128)(2,1)}, bf16[8,2,64,2048]{3,2,1,0:T(8,128)(2,1)}, bf16[4,2,128,2048]{3,2,1,0:T(8,128)(2,1)}, f32[32,8,128]{2,1,0:T(8,128)}) custom-call(bf16[64,3072]{1,0:T(8,128)(2,1)} %refs_0_.1, bf16[2,32,2048]{2,1,0:T(8,128)(2,1)} %bitcast.242, bf16[2,64,2048]{2,1,0:T(8,128)(2,1)} %bitcast.201, ...), custom_call_target="tpu_custom_call" | custom-call | bytes 120000000 | tf_op jit(solution)/shard_map/move_1/pallas_call | solution.py:1392
  79.7 1.1 slice_reduce_fusion.1
  80.8 0.7 mul.500
  81.5 0.7 mul.462
  82.1 1.8 multiply_convert_fusion.1
  83.9 4.5 %fusion.74 = (bf16[1024,384]{0,1:T(8,128)(2,1)S(1)}, f32[1024,384]{0,1:T(8,128)S(1)}) fusion(bf16[1024,2048]{1,0:T(8,128)(2,1)} %bitcast.245, bf16[2048,384]{1,0:T(8,128)(2,1)S(1)} %bitcast.222), kind=kOutput, calls=%fused_computation.144 | convolution fusion | flops 1611005952 | bytes 8126464 | tf_op jit(solution)/shard_map/dot_general | solution.py:1507
  89.2 1.2 fusion.54
  90.6 0.9 fusion.9
  91.5 0.9 exponential_reduce_fusion.1
  92.9 1.5 fusion.4
  94.4 2.0 exponential_reduce_fusion
  96.5 1.3 fusion.17
  97.8 2.4 fusion.12
  100.3 0.8 copy-done.13
  101.4 1.1 copy.29.refs_1_
  102.6 52.1 %move_2.1 = (bf16[4,2,128,2048]{3,2,1,0:T(8,128)(2,1)}, f32[2,64,2048]{2,1,0:T(8,128)}) custom-call(bf16[2,128,2048]{2,1,0:T(8,128)(2,1)} %bitcast.228, bf16[4,256,256]{2,1,0:T(8,128)(2,1)} %copy.29.refs_1_, bf16[256,2048]{1,0:T(8,128)(2,1)} %bitcast.229), custom_call_target="tpu_custom_call" | custom-call | bytes 120000000 | tf_op jit(solution)/shard_map/move_2/pallas_call | solution.py:1392
  154.7 1.5 multiply_reduce_fusion.3
  156.8 2.2 multiply_convert_fusion.2.refs_0_
  159.0 91.0 %move_3.1 = (f32[2,64,2048]{2,1,0:T(8,128)}, f32[2,128,2048]{2,1,0:T(8,128)}, bf16[4,2,2,64,2048]{4,3,2,1,0:T(8,128)(2,1)}, bf16[4,2,2,64,2048]{4,3,2,1,0:T(8,128)(2,1)}, bf16[4,2,2,64,2048]{4,3,2,1,0:T(8,128)(2,1)}) custom-call(bf16[2,64,2048]{2,1,0:T(8,128)(2,1)} %multiply_convert_fusion.2.refs_0_, bf16[2,128,2048]{2,1,0:T(8,128)(2,1)} %bitcast.226, ...), custom_call_target="tpu_custom_call" | custom-call | bytes 120000000 | tf_op jit(solution)/shard_map/move_3/pallas_call | solution.py:1392
  250.0 2.4 multiply_reduce_fusion.1
  252.5 3.9 fusion.71
  256.5 46.8 %move_5.1 = (bf16[8,2,64,2048]{3,2,1,0:T(8,128)(2,1)}, f32[2,128,2048]{2,1,0:T(8,128)}) custom-call(bf16[2,64,2048]{2,1,0:T(8,128)(2,1)} %bitcast.214, bf16[4,2,128,2048]{3,2,1,0:T(8,128)(2,1)} %bitcast.209), custom_call_target="tpu_custom_call" | custom-call | bytes 120000000 | tf_op jit(solution)/shard_map/move_5/pallas_call | solution.py:1392
  303.3 1.2 copy-done.16
  304.5 3.5 convolution_convert_fusion.2
  308.0 0.7 stack.10
  308.8 3.9 fusion.5
  312.7 1.3 fusion.7
  314.0 0.7 fusion.19
  315.3 3.8 fusion
  319.1 2.8 fusion.2
  321.9 1.4 fusion.16
  324.4 0.8 fusion.11
  325.5 1.2 convolution_bitcast_fusion.2
  326.7 2.4 fusion.18
  329.5 4.2 multiply_reduce_fusion
  333.8 0.7 pad.25.refs_4_
  334.5 5.7 %convolution_convert_fusion = bf16[1024,2048]{1,0:T(8,128)(2,1)} fusion(bf16[2048,384]{1,0:T(8,128)(2,1)S(1)} %bitcast.221, bf16[1024,64]{0,1:T(8,128)(2,1)S(1)} %fusion.18, bf16[1024,64]{0,1:T(8,128)(2,1)} %copy-done.23, bf16[1024,256]{0,1:T(8,128)(2,1)} %bitcast.241), kind=kOutput, calls=%fused_computation.18 | convolution fusion | flops 1615069184 | bytes 6553600 | tf_op jit(solution)/shard_map/dot_general | solution.py:1610
  340.2 2.2 convolution_convert_fusion.1
  342.4 70.6 %move_6.1 = (f32[64,3072]{1,0:T(8,128)}, f32[2,32,2048]{2,1,0:T(8,128)}, f32[2,64,2048]{2,1,0:T(8,128)}, f32[2,128,2048]{2,1,0:T(8,128)}, f32[8,128]{1,0:T(8,128)}) custom-call(bf16[4,2,4,64,384]{4,3,2,1,0:T(8,128)(2,1)} %bitcast.223, bf16[4,2,32,2048]{3,2,1,0:T(8,128)(2,1)} %bitcast.233, bf16[8,2,64,2048]{3,2,1,0:T(8,128)(2,1)} %bitcast.213, ...), custom_call_target="tpu_custom_call" | custom-call | bytes 120000000 | tf_op jit(solution)/shard_map/move_6/pallas_call | solution.py:1392
  413.1 1.6 fusion.20
  414.7 1.3 slice_bitcast_fusion.7
  416.0 3.7 fusion.25
  419.8 0.9 copy.50
  420.7 0.8 copy.51
  421.4 1.3 copy.52
  422.8 1.3 copy.53
  424.1 1.3 copy.54
  (124 shorter events, 6.4 us)
Async XLA Ops:
  7.2 151.8 %all-gather.2.cloned.1.call-start = ((), (), s32[]{:S(2)}) async-start(), calls=%async_computation.1 | async-start | bytes 4718592 | tf_op jit(solution)/shard_map/all_gather | solution.py:1505
  8.6 0.6 copy-start.34
  79.7 336.4 %reduce-scatter.2.cloned.1.call-start = ((), (), s32[]{:S(2)}) async-start(), calls=%async_computation.2 | async-start | bytes 4718592 | tf_op jit(solution)/shard_map/reduce_scatter | solution.py:1563
  88.4 9.4 %copy-start.32 = (bf16[1024,384]{0,1:T(8,128)(2,1)}, bf16[1024,384]{0,1:T(8,128)(2,1)S(1)}, u32[]{:S(2)}) copy-start(bf16[1024,384]{0,1:T(8,128)(2,1)S(1)} %get-tuple-element.170) | copy-start | bytes 2359300
  88.5 3.0 copy-start.36
  88.5 1.9 copy-start.29
  89.2 3.6 copy-start.18
  90.6 2.3 copy-start.6
  90.6 2.3 copy-start.8
  91.5 5.0 %copy-start.1 = (f32[512,512,4]{1,0,2:T(8,128)}, f32[512,512,4]{1,0,2:T(8,128)S(1)}, u32[]{:S(2)}) copy-start(f32[512,512,4]{1,0,2:T(8,128)S(1)} %get-tuple-element.175) | copy-start | bytes 12582916
  92.4 4.1 copy-start.27
  92.8 4.9 %copy-start.4 = (pred[512,1024]{0,1:T(8,128)(4,1)}, pred[512,1024]{0,1:T(8,128)(4,1)S(1)}, u32[]{:S(2)}) copy-start(pred[512,1024]{0,1:T(8,128)(4,1)S(1)} %iota_compare_fusion) | copy-start | bytes 1572868
  94.4 3.4 copy-start
  96.5 3.7 copy-start.24
  100.2 54.5 %copy-start.3 = (bf16[1,128,2048]{2,1,0:T(8,128)(2,1)S(1)}, bf16[1,128,2048]{2,1,0:T(8,128)(2,1)}, u32[]{:S(2)}) copy-start(bf16[1,128,2048]{2,1,0:T(8,128)(2,1)} %param.25) | copy-start | bytes 1572868
  100.3 0.8 copy-start.13
  156.2 0.6 copy-start.35
  156.3 2.7 copy-start.39
  303.3 1.2 copy-start.16
  304.5 3.5 copy-start.33
  304.5 4.2 copy-start.28
  308.7 3.9 copy-start.2
  308.8 6.0 %slice-start = ((s8[8388608]{0:T(1024)(128)(4,1)}), s8[4194304]{0:T(1024)(128)(4,1)S(1)}, s32[]{:S(2)}) async-start(s8[8388608]{0:T(1024)(128)(4,1)} %bitcast.199), calls=%async_computation.3 | async-start | bytes 8388608
  312.7 1.4 copy-start.7
  312.7 1.4 copy-start.9
  312.7 2.5 slice-start.1
  312.7 2.6 copy-start.5
  312.7 2.6 copy-start.25
  321.9 1.4 copy-start.30
  321.9 1.4 copy-start.37
  321.9 2.0 copy-start.19
  323.3 2.0 copy-start.20
  323.9 5.2 %copy-start.23 = (bf16[1024,64]{0,1:T(8,128)(2,1)}, bf16[1024,64]{0,1:T(8,128)(2,1)S(1)}, u32[]{:S(2)}) copy-start(bf16[1024,64]{0,1:T(8,128)(2,1)S(1)} %maximum_bitcast_fusion.1) | copy-start | bytes 393220
  325.4 3.7 copy-start.22
  326.7 2.4 copy-start.15
  326.7 2.4 copy-start.26
  326.7 2.7 copy-start.40
  329.5 4.3 copy-start.31
  334.5 5.7 %copy-start.14 = (bf16[1024,4,64]{0,2,1:T(8,128)(2,1)S(1)}, bf16[1024,4,64]{0,2,1:T(8,128)(2,1)}, u32[]{:S(2)}) copy-start(bf16[1024,4,64]{0,2,1:T(8,128)(2,1)} %copy-done.13) | copy-start | bytes 1572868
  334.5 5.7 %copy-start.41 = (bf16[8,2,64,2048]{3,2,1,0:T(8,128)(2,1)S(1)}, bf16[8,2,64,2048]{3,2,1,0:T(8,128)(2,1)}, u32[]{:S(2)}) copy-start(bf16[8,2,64,2048]{3,2,1,0:T(8,128)(2,1)} %get-tuple-element.130) | copy-start | bytes 12582916
  342.4 72.3 %copy-start.38 = (f32[128]{0:T(128)S(1)}, f32[128]{0:T(128)}, u32[]{:S(2)}) copy-start(f32[128]{0:T(128)} %get-tuple-element.155) | copy-start | bytes 1540
  413.1 6.7 %copy-start.17 = (f32[64,3072]{1,0:T(8,128)S(1)}, f32[64,3072]{1,0:T(8,128)}, u32[]{:S(2)}) copy-start(f32[64,3072]{1,0:T(8,128)} %get-tuple-element.191) | copy-start | bytes 2359300
  413.1 7.6 %copy-start.21 = (f32[2,32,2048]{2,1,0:T(8,128)S(1)}, f32[2,32,2048]{2,1,0:T(8,128)}, u32[]{:S(2)}) copy-start(f32[2,32,2048]{2,1,0:T(8,128)} %get-tuple-element.136) | copy-start | bytes 1572868
  416.0 5.4 %copy-start.11 = (f32[2,128,2048]{2,1,0:T(8,128)S(1)}, f32[2,128,2048]{2,1,0:T(8,128)}, u32[]{:S(2)}) copy-start(f32[2,128,2048]{2,1,0:T(8,128)} %get-tuple-element.137) | copy-start | bytes 6291460
  419.8 3.0 copy-start.12
  421.4 2.6 copy-start.10
Sparse Core Ops, SparseCore 0:
  79.8 51.2 all-gather.1
  303.4 48.9 reduce-scatter.1
